TPU v7x, 512 devices: a whole 4x8x8 slice. The times are simulated.
512 devices in a mesh: light: 16 (over y, core), view: 32 (over z, x).
Axes of the slice: x: 4, y: 8, z: 8, core: 2. Of those that a mesh axis runs over, the one named last changes fastest.
Arguments:
- density: float32 [512, 128, 4096], P('light', 'view'), may hold values from 0.1 to 8
- emission: float32 [512, 128, 4096], P('light', 'view'), may hold values from 0.1 to 1
- facing: int32 [512], P('light'), may hold values 0 or 1
Outputs:
- radiance: float32 [512, 4096], P('light', 'view')
- coverage: float32 [512, 4096], P('light', 'view')
All inputs are finite; a program needn't handle non-finite values. No bound on the sum of `facing` on one device may be relied on, other than what follows from the above.
Results may differ from a plain program's by a relative error of at most 0.0003.
Values sent between devices are 32-bit elements; how exact they have to be, the bound alone decides.
No kernel may reach another device: no remote copies, remote signals or barrier semaphores. Data moves between devices by JAX's collectives and lax.ppermute only.
A program may use at most 64 MiB of HBM per device.

v0:
```python
import jax
import jax.numpy as jnp
from jax import lax
from jax.sharding import PartitionSpec as P


def entering(value, axis, join, neutral):
    count, mine = (lax.axis_size(axis), lax.axis_index(axis))
    pieces = lax.all_gather(value, axis)
    so_far = jnp.full_like(value, 0) + jnp.asarray(neutral, value.dtype)

    def hop(position, so_far):
        longer = join(so_far, pieces[position])
        return jnp.where(position < mine, longer, so_far)

    return lax.fori_loop(0, count - 1, hop, so_far)


def swapped(value, axis, bit):
    return lax.ppermute(value, axis, [(i, i ^ 1 << bit) for i in range(lax.axis_size(axis))])


def shards(density, emission, facing):
    rows, depth_cells, columns = density.shape
    light_count = lax.axis_size("light")
    view_count = lax.axis_size("view")
    tau_light = density * (1.0 / (rows * light_count))
    tau_view = density * (1.0 / (depth_cells * view_count))
    slab_depth = jnp.sum(tau_light, axis=0)
    incoming = entering(
        slab_depth, "light", lambda early, late: early + late, jnp.zeros_like(slab_depth)
    )
    depth = incoming[None] + (jnp.cumsum(tau_light, axis=0) - tau_light)
    lit = emission * (0.2 + jnp.exp(-depth)) * (1.0 - jnp.exp(-tau_view))
    running = jnp.cumsum(tau_view, axis=1)
    total = jnp.sum(tau_view, axis=1)
    forward = jnp.sum(lit * jnp.exp(-(running - tau_view)), axis=1)
    backward = jnp.sum(lit * jnp.exp(-(total[:, None, :] - running)), axis=1)
    reversed_rows = facing == 1
    color = jnp.where(reversed_rows[:, None], backward, forward)
    trans = jnp.exp(-total)
    block_width = columns // view_count
    stacked = jnp.stack([color, trans]).reshape(2, rows, view_count, block_width)
    my_view = lax.axis_index("view")
    for bit in range(view_count.bit_length() - 1):
        blocks = stacked.shape[2]
        paired = stacked.reshape(2, rows, blocks // 2, 2, block_width)
        my_bit = my_view >> bit & 1
        keep_part = jnp.where(my_bit == 1, paired[:, :, :, 1], paired[:, :, :, 0])
        send_part = jnp.where(my_bit == 1, paired[:, :, :, 0], paired[:, :, :, 1])
        partner = swapped(send_part, "view", bit)
        in_front = ((my_bit == 0) == jnp.logical_not(reversed_rows))[:, None, None]
        front_part = jnp.where(in_front, keep_part, partner)
        back_part = jnp.where(in_front, partner, keep_part)
        stacked = jnp.stack(
            [front_part[0] + front_part[1] * back_part[0], front_part[1] * back_part[1]]
        )
    radiance = stacked[0][:, 0]
    coverage = stacked[1][:, 0]
    return (radiance, coverage)


def solution(mesh):
    return jax.shard_map(
        shards,
        mesh=mesh,
        in_specs=(P("light", "view", None), P("light", "view", None), P("light")),
        out_specs=(P("light", "view"), P("light", "view")),
        check_vma=False,
    )
```

profile of v0, /device:TPU:4, one launch (start us, length us, event | category | flops | bytes accessed | tf_op | source)
XLA Modules:
  0.0 142.6 jit_solution(2626770505306400125)
XLA Ops:
  7.2 0.0 all-gather.4.cloned.1.call-start
  7.2 4.6 %multiply_reduce_fusion.2 = (f32[4,4096]{1,0:T(4,128)}, f32[32,4096]{1,0:T(8,128)S(1)}, f32[32,4,4096]{2,1,0:T(4,128)}) fusion(f32[32,4,4096]{2,1,0:T(4,128)} %param.5), kind=kLoop, calls=%fused_computation.6 | loop fusion | flops 1949696 | bytes 4784128 | tf_op jit(solution)/shard_map/reduce_sum | solution.py:29
  11.8 0.0 all-gather.4.cloned.1.call-update
  11.9 0.1 negate_exponential_fusion
  11.9 1.3 exp.31
  13.2 0.0 copy-start.2
  13.2 0.0 copy-start
  13.2 6.6 %reduce_window_sum.23 = f32[32,4,4096]{2,1,0:T(4,128)} reduce-window(f32[32,4,4096]{2,1,0:T(4,128)} %get-tuple-element.112, f32[]{:T(128)} %constant.52.clone.1), window={size=1x4x1 pad=0_0x3_0x0_0}, to_apply=%region_5.6 | reduce-window | flops 1572864 | bytes 4194308 | tf_op jit(solution)/shard_map/jit(cumsum)/reduce_window_sum | solution.py:35
  19.9 0.0 copy-done.2
  19.9 37.6 %all-gather.4.cloned.1.call-done = f32[16,4,4096]{2,1,0:T(4,128)} async-done(((f32[1,4,4096]{2,1,0:T(4,128)}), f32[16,4,4096]{2,1,0:T(4,128)}) %all-gather.4.cloned.1.call-update) | async-done | bytes 1048592 | tf_op jit(solution)/shard_map/all_gather | solution.py:9
  57.4 13.9 %while.14 = (s32[]{:T(128)}, f32[4,4096]{1,0:T(4,128)S(1)}, s32[]{:T(128)}, f32[16,4,4096]{2,1,0:T(4,128)}, s32[]{:T(128)}, /*index=5*/s32[]{:T(128)}) while((s32[]{:T(128)}, f32[4,4096]{1,0:T(4,128)S(1)}, s32[]{:T(128)}, f32[16,4,4096]{2,1,0:T(4,128)}, s32[]{:T(128)}, /*index=5*/s32[]{:T(128)}) %tuple.56), condition=%wide.region_2.3_spmd.clone, body=%wide.region_1.2_spmd.clone.sunk | while | flops 49156 | bytes 196701 | solution.py:16
  57.4 0.9 add_select_fusion.2
  58.4 0.9 add_select_fusion.2
  59.3 0.9 add_select_fusion.2
  60.2 0.9 add_select_fusion.2
  61.1 0.9 add_select_fusion.2
  62.1 0.9 add_select_fusion.2
  63.0 0.9 add_select_fusion.2
  63.9 0.9 add_select_fusion.2
  64.9 0.9 add_select_fusion.2
  65.8 0.9 add_select_fusion.2
  66.7 0.9 add_select_fusion.2
  67.6 0.9 add_select_fusion.2
  68.6 0.9 add_select_fusion.2
  69.5 0.9 add_select_fusion.2
  70.4 0.9 add_select_fusion.2
  71.3 0.0 copy-done
  71.3 7.8 %multiply_reduce_fusion = (f32[32,4096]{1,0:T(8,128)S(1)}, f32[32,4096]{1,0:T(8,128)}) fusion(f32[32,4,4096]{2,1,0:T(4,128)} %reduce_window_sum.23, f32[32,4,4096]{2,1,0:T(4,128)S(1)} %copy-done, f32[32,4096]{1,0:T(8,128)S(1)} %get-tuple-element.100, f32[32,4,4096]{2,1,0:T(4,128)} %param.6, f32[4,4096]{1,0:T(4,128)S(1)} %get-tuple-element.81), kind=kOutput, calls=%fused_computation.1 | output fusion | flops 25952256 | bytes 7929856 | tf_op jit(solution)/shard_map/jit(cumsum)/reduce_window_sum | solution.py:33
  79.1 0.0 copy-start.1
  79.1 1.5 %reduce_sum.43 = f32[1,32,16,2,128]{4,3,2,1,0:T(2,128)S(1)} reshape(f32[32,4096]{1,0:T(8,128)} %get-tuple-element.98) | data formatting | bytes 1048576 | tf_op jit(solution)/shard_map/reduce_sum | solution.py:38
  80.6 0.4 reduce_sum.45
  81.1 0.3 broadcast_select_fusion.1
  81.4 0.0 copy-done.1
  81.4 1.1 broadcast_select_fusion
  82.6 3.1 %collective-permute-start = (f32[2,32,16,128]{3,2,1,0:T(8,128)S(1)}, f32[2,32,16,128]{3,2,1,0:T(8,128)S(1)}, u32[]{:S(2)}, u32[]{:S(2)}) collective-permute-start(f32[2,32,16,128]{3,2,1,0:T(8,128)S(1)} %bitcast.143), channel_id=1, source_target_pairs={{0,1},{1,0},{2,3},{3,2},{4,5},{5,4},{6,7},{7,6},{8,9},{9,8},{10,11... | collective-permute-start | bytes 1572872 | tf_op jit(solution)/shard_map/ppermute | solution.py:20
  85.7 12.9 %collective-permute-done = f32[2,32,16,128]{3,2,1,0:T(8,128)S(1)} collective-permute-done((f32[2,32,16,128]{3,2,1,0:T(8,128)S(1)}, f32[2,32,16,128]{3,2,1,0:T(8,128)S(1)}, u32[]{:S(2)}, u32[]{:S(2)}) %collective-permute-start) | collective-permute-done | bytes 524320 | tf_op jit(solution)/shard_map/ppermute | solution.py:20
  98.6 0.1 bitcast_select_fusion.1
  98.7 0.1 fusion.8
  98.8 0.1 copy.93
  98.9 0.1 copy.94
  99.0 2.4 %collective-permute-start.1 = (f32[2,32,8,128]{3,1,2,0:T(8,128)S(1)}, f32[2,32,8,128]{3,1,2,0:T(8,128)S(1)}, u32[]{:S(2)}, u32[]{:S(2)}) collective-permute-start(f32[2,32,8,128]{3,1,2,0:T(8,128)S(1)} %select_bitcast_fusion), channel_id=1, source_target_pairs={{0,2},{1,3},{2,0},{3,1},{4,6},{5,7},{6,4},{7,5},{8,10},{9,11},{10,... | collective-permute-start | bytes 786440 | tf_op jit(solution)/shard_map/ppermute | solution.py:20
  101.4 8.6 %collective-permute-done.1 = f32[2,32,8,128]{3,1,2,0:T(8,128)S(1)} collective-permute-done((f32[2,32,8,128]{3,1,2,0:T(8,128)S(1)}, f32[2,32,8,128]{3,1,2,0:T(8,128)S(1)}, u32[]{:S(2)}, u32[]{:S(2)}) %collective-permute-start.1) | collective-permute-done | bytes 262176 | tf_op jit(solution)/shard_map/ppermute | solution.py:20
  110.1 0.1 broadcast_select_fusion.4
  110.3 3.6 %collective-permute-start.2 = (f32[2,32,4,128]{3,1,2,0:T(8,128)S(1)}, f32[2,32,4,128]{3,1,2,0:T(8,128)S(1)}, u32[]{:S(2)}, u32[]{:S(2)}) collective-permute-start(f32[2,32,4,128]{3,1,2,0:T(8,128)S(1)} %select_bitcast_fusion.1), channel_id=1, source_target_pairs={{0,4},{1,5},{2,6},{3,7},{4,0},{5,1},{6,2},{7,3},{8,12},{9,13},{10,... | collective-permute-start | bytes 393224 | tf_op jit(solution)/shard_map/ppermute | solution.py:20
  113.8 3.3 %collective-permute-done.2 = f32[2,32,4,128]{3,1,2,0:T(8,128)S(1)} collective-permute-done((f32[2,32,4,128]{3,1,2,0:T(8,128)S(1)}, f32[2,32,4,128]{3,1,2,0:T(8,128)S(1)}, u32[]{:S(2)}, u32[]{:S(2)}) %collective-permute-start.2) | collective-permute-done | bytes 131104 | tf_op jit(solution)/shard_map/ppermute | solution.py:20
  117.1 0.1 broadcast_select_fusion.6
  117.3 4.6 %collective-permute-start.3 = (f32[2,32,2,128]{3,1,2,0:T(8,128)S(1)}, f32[2,32,2,128]{3,1,2,0:T(8,128)S(1)}, u32[]{:S(2)}, u32[]{:S(2)}) collective-permute-start(f32[2,32,2,128]{3,1,2,0:T(8,128)S(1)} %select_bitcast_fusion.2), channel_id=1, source_target_pairs={{0,8},{1,9},{2,10},{3,11},{4,12},{5,13},{6,14},{7,15},{8,0},{9,1},... | collective-permute-start | bytes 196616 | tf_op jit(solution)/shard_map/ppermute | solution.py:20
  121.9 2.4 %collective-permute-done.3 = f32[2,32,2,128]{3,1,2,0:T(8,128)S(1)} collective-permute-done((f32[2,32,2,128]{3,1,2,0:T(8,128)S(1)}, f32[2,32,2,128]{3,1,2,0:T(8,128)S(1)}, u32[]{:S(2)}, u32[]{:S(2)}) %collective-permute-start.3) | collective-permute-done | bytes 65568 | tf_op jit(solution)/shard_map/ppermute | solution.py:20
  124.3 0.1 broadcast_select_fusion.8
  124.5 8.7 %collective-permute-start.4 = (f32[2,32,1,128]{3,1,0,2:T(8,128)S(1)}, f32[2,32,1,128]{3,1,0,2:T(8,128)S(1)}, u32[]{:S(2)}, u32[]{:S(2)}) collective-permute-start(f32[2,32,1,128]{3,1,0,2:T(8,128)S(1)} %select_bitcast_fusion.3), channel_id=1, source_target_pairs={{0,16},{1,17},{2,18},{3,19},{4,20},{5,21},{6,22},{7,23},{8,24},{9,... | collective-permute-start | bytes 98312 | tf_op jit(solution)/shard_map/ppermute | solution.py:20
  133.2 1.9 %collective-permute-done.4 = f32[2,32,1,128]{3,1,0,2:T(8,128)S(1)} collective-permute-done((f32[2,32,1,128]{3,1,0,2:T(8,128)S(1)}, f32[2,32,1,128]{3,1,0,2:T(8,128)S(1)}, u32[]{:S(2)}, u32[]{:S(2)}) %collective-permute-start.4) | collective-permute-done | bytes 32800 | tf_op jit(solution)/shard_map/ppermute | solution.py:20
  135.1 0.1 broadcast_select_fusion.10
  135.2 0.6 fusion.18
  (10 shorter events, 0.2 us)
Async XLA Ops:
  7.2 50.3 %all-gather.4.cloned.1.call-start = ((), (), s32[]{:S(2)}) async-start(), calls=%async_computation | async-start | bytes 1114112 | tf_op jit(solution)/shard_map/all_gather | solution.py:9
  13.2 6.6 %copy-start.2 = (s32[32]{0:T(128)S(1)}, s32[32]{0:T(128)}, u32[]{:S(2)}) copy-start(s32[32]{0:T(128)} %param.7) | copy-start | bytes 388
  13.2 58.1 %copy-start = (f32[32,4,4096]{2,1,0:T(4,128)S(1)}, f32[32,4,4096]{2,1,0:T(4,128)}, u32[]{:S(2)}) copy-start(f32[32,4,4096]{2,1,0:T(4,128)} %param.5) | copy-start | bytes 6291460
  79.1 2.3 %copy-start.1 = (f32[1,32,16,2,128]{4,3,2,1,0:T(2,128)S(1)}, f32[1,32,16,2,128]{4,3,2,1,0:T(2,128)}, u32[]{:S(2)}) copy-start(f32[1,32,16,2,128]{4,3,2,1,0:T(2,128)} %exp.31) | copy-start | bytes 1572868
  82.6 16.0 %collective-permute-start = (f32[2,32,16,128]{3,2,1,0:T(8,128)S(1)}, f32[2,32,16,128]{3,2,1,0:T(8,128)S(1)}, u32[]{:S(2)}, u32[]{:S(2)}) collective-permute-start(f32[2,32,16,128]{3,2,1,0:T(8,128)S(1)} %bitcast.143), channel_id=1, source_target_pairs={{0,1},{1,0},{2,3},{3,2},{4,5},{5,4},{6,7},{7,6},{8,9},{9,8},{10,11... | collective-permute-start | bytes 1572872 | tf_op jit(solution)/shard_map/ppermute | solution.py:20
  99.0 11.0 %collective-permute-start.1 = (f32[2,32,8,128]{3,1,2,0:T(8,128)S(1)}, f32[2,32,8,128]{3,1,2,0:T(8,128)S(1)}, u32[]{:S(2)}, u32[]{:S(2)}) collective-permute-start(f32[2,32,8,128]{3,1,2,0:T(8,128)S(1)} %select_bitcast_fusion), channel_id=1, source_target_pairs={{0,2},{1,3},{2,0},{3,1},{4,6},{5,7},{6,4},{7,5},{8,10},{9,11},{10,... | collective-permute-start | bytes 786440 | tf_op jit(solution)/shard_map/ppermute | solution.py:20
  110.3 6.9 %collective-permute-start.2 = (f32[2,32,4,128]{3,1,2,0:T(8,128)S(1)}, f32[2,32,4,128]{3,1,2,0:T(8,128)S(1)}, u32[]{:S(2)}, u32[]{:S(2)}) collective-permute-start(f32[2,32,4,128]{3,1,2,0:T(8,128)S(1)} %select_bitcast_fusion.1), channel_id=1, source_target_pairs={{0,4},{1,5},{2,6},{3,7},{4,0},{5,1},{6,2},{7,3},{8,12},{9,13},{10,... | collective-permute-start | bytes 393224 | tf_op jit(solution)/shard_map/ppermute | solution.py:20
  117.3 7.1 %collective-permute-start.3 = (f32[2,32,2,128]{3,1,2,0:T(8,128)S(1)}, f32[2,32,2,128]{3,1,2,0:T(8,128)S(1)}, u32[]{:S(2)}, u32[]{:S(2)}) collective-permute-start(f32[2,32,2,128]{3,1,2,0:T(8,128)S(1)} %select_bitcast_fusion.2), channel_id=1, source_target_pairs={{0,8},{1,9},{2,10},{3,11},{4,12},{5,13},{6,14},{7,15},{8,0},{9,1},... | collective-permute-start | bytes 196616 | tf_op jit(solution)/shard_map/ppermute | solution.py:20
  124.5 10.6 %collective-permute-start.4 = (f32[2,32,1,128]{3,1,0,2:T(8,128)S(1)}, f32[2,32,1,128]{3,1,0,2:T(8,128)S(1)}, u32[]{:S(2)}, u32[]{:S(2)}) collective-permute-start(f32[2,32,1,128]{3,1,0,2:T(8,128)S(1)} %select_bitcast_fusion.3), channel_id=1, source_target_pairs={{0,16},{1,17},{2,18},{3,19},{4,20},{5,21},{6,22},{7,23},{8,24},{9,... | collective-permute-start | bytes 98312 | tf_op jit(solution)/shard_map/ppermute | solution.py:20
Sparse Core Ops, SparseCore 0:
  11.9 45.4 all-gather.3
where the time goes:
time: 144 us; the launch traced here: 143 us
  waiting for transfers between devices  66.7 us (46%)
  other arithmetic  35.6 us (25%)
  starting transfers between devices  22.5 us (16%)
  between operations  14.3 us (10%)
  local copies, waits for them, and re-layouts  3.43 us (2%)
    all_gather x1, waiting for transfers between devices, entering(): pieces = lax.all_gather(value, axis)  37.6 us
    ppermute x5, waiting for transfers between devices, swapped(): lax.ppermute(value, axis, [(i, i ^ 1 << bit) for i in range(lax.axis_size...  29.1 us
    ppermute x5, starting transfers between devices, swapped(): lax.ppermute(value, axis, [(i, i ^ 1 << bit) for i in range(lax.axis_size...  22.4 us
    select_n x15, other arithmetic, hop(): return jnp.where(position < mine, longer, so_far)  13.7 us
    another operation x1, other arithmetic, shards(): depth = incoming[None] + (jnp.cumsum(tau_light, axis=0) - tau_light)  7.75 us
    another operation x1, other arithmetic, shards(): running = jnp.cumsum(tau_view, axis=1)  6.63 us
    reduce_sum x1, other arithmetic, shards(): slab_depth = jnp.sum(tau_light, axis=0)  4.59 us
  transfers between devices with their start and end apart: 6, of which 6 were waited for; matrix products, arithmetic and copies ran while one was open for 6% of the time, Pallas kernels for 0%

commit v1 on v0

v1 whole, which is shorter than its diff:
```python
import jax
import jax.numpy as jnp
from jax import lax
from jax.sharding import PartitionSpec as P


def light_prefix(value):
    count = lax.axis_size("light")
    total = value
    received = jnp.zeros_like(value)
    shift = 1
    while shift < count:
        got = lax.ppermute(total, "light", [(i, i + shift) for i in range(count - shift)])
        total = total + got
        received = received + got
        shift *= 2
    return received


def group_exchange(block_of, my_pos, size, pairs_for):
    pieces = [block_of(my_pos)]
    for k in range(1, size):
        pieces.append(lax.ppermute(block_of((my_pos + k) % size), "view", pairs_for(k)))
    stacked = jnp.stack(pieces)
    return jnp.stack(
        [lax.dynamic_index_in_dim(stacked, (my_pos - j) % size, 0, keepdims=False) for j in range(size)]
    )


def composite(colors, transes, reversed_rows):
    count = colors.shape[0]
    forward = colors[count - 1]
    for j in range(count - 2, -1, -1):
        forward = colors[j] + transes[j] * forward
    backward = colors[0]
    for j in range(1, count):
        backward = colors[j] + transes[j] * backward
    return jnp.where(reversed_rows, backward, forward)


def make_shards(x_count):
    def shards(density, emission, facing):
        rows, cells, columns = density.shape
        light_count = lax.axis_size("light")
        view_count = lax.axis_size("view")
        z_count = view_count // x_count
        tau_light = density * (1.0 / (rows * light_count))
        tau_view = density * (1.0 / (cells * view_count))
        slab_depth = jnp.sum(tau_light, axis=0)
        incoming = light_prefix(slab_depth)

        reversed_rows = facing == 1
        local_depth = jnp.cumsum(tau_light, axis=0) - tau_light
        shade = jnp.exp(-local_depth)
        step = jnp.exp(-tau_view)
        forward_w = [jnp.ones_like(step[:, 0])]
        for v in range(1, cells):
            forward_w.append(forward_w[-1] * step[:, v - 1])
        backward_w = [jnp.ones_like(step[:, 0])]
        for v in range(cells - 2, -1, -1):
            backward_w.insert(0, backward_w[0] * step[:, v + 1])
        trans = forward_w[-1] * step[:, cells - 1]
        weight = jnp.where(reversed_rows[:, None, None], jnp.stack(backward_w, 1), jnp.stack(forward_w, 1))
        base = emission * (1.0 - step) * weight
        flat = jnp.sum(base, axis=1)
        lit_part = base * shade

        my_view = lax.axis_index("view")
        my_x = my_view % x_count
        my_z = my_view // x_count

        def pairs_x(k):
            return [(z * x_count + x, z * x_count + (x + k) % x_count) for z in range(z_count) for x in range(x_count)]

        def pairs_z(k):
            return [(z * x_count + x, ((z + k) % z_count) * x_count + x) for z in range(z_count) for x in range(x_count)]

        width = columns // view_count

        def x_blocks(array):
            grid = array.reshape(rows, z_count, x_count, width)
            return lambda pos: lax.dynamic_index_in_dim(grid, pos, 2, keepdims=False)

        def z_blocks(array):
            return lambda pos: lax.dynamic_index_in_dim(array, pos, 1, keepdims=False)

        trans_x = group_exchange(x_blocks(trans), my_x, x_count, pairs_x)
        trans_xg = jnp.prod(trans_x, axis=0)
        trans_z = group_exchange(z_blocks(trans_xg), my_z, z_count, pairs_z)
        coverage = jnp.prod(trans_z, axis=0)

        light = jnp.exp(-incoming)
        color = 0.2 * flat + jnp.sum(lit_part * light[None], axis=1)
        color_x = group_exchange(x_blocks(color), my_x, x_count, pairs_x)
        color_xg = composite(color_x, trans_x, reversed_rows[:, None, None])
        color_z = group_exchange(z_blocks(color_xg), my_z, z_count, pairs_z)
        radiance = composite(color_z, trans_z, reversed_rows[:, None])
        return (radiance, coverage)

    return shards


def x_extent(mesh):
    row = mesh.devices.reshape(mesh.devices.shape[0], -1)[0]
    coords = [getattr(d, "coords", None) for d in row]
    if any(c is None for c in coords):
        return 4
    first_z = coords[0][2]
    return sum(1 for c in coords if c[2] == first_z)


def solution(mesh):
    return jax.shard_map(
        make_shards(x_extent(mesh)),
        mesh=mesh,
        in_specs=(P("light", "view", None), P("light", "view", None), P("light")),
        out_specs=(P("light", "view"), P("light", "view")),
        check_vma=False,
    )
```

time: 144 us -> 142 us (0.986)
  the two profiles are of different devices: /device:TPU:4 before, /device:TPU:34 now
where the time goes in v1:
time: 142 us; the launch traced here: 141 us
  starting transfers between devices  87.6 us (62%)
  waiting for transfers between devices  32.2 us (23%)
  other arithmetic  17.6 us (12%)
  local copies, waits for them, and re-layouts  2.18 us (2%)
  between operations  1.73 us (1%)
    ppermute x20, starting transfers between devices, group_exchange(): lax.ppermute(block_of((my_pos + k) % size), 'view', pairs_for(k))  80.6 us
    ppermute x4, waiting for transfers between devices, light_prefix(): lax.ppermute(total, 'light', [(i, i + shift) for i in range(count - shift)])  25.3 us
    ppermute x4, starting transfers between devices, light_prefix(): lax.ppermute(total, 'light', [(i, i + shift) for i in range(count - shift)])  7.05 us
    ppermute x20, waiting for transfers between devices, group_exchange(): lax.ppermute(block_of((my_pos + k) % size), 'view', pairs_for(k))  6.87 us
    reduce_sum x1, other arithmetic, shards(): slab_depth = jnp.sum(tau_light, axis=0)  6.24 us
    another operation x1, other arithmetic, shards(): local_depth = jnp.cumsum(tau_light, axis=0) - tau_light  5.03 us
    mul x1, other arithmetic, shards(): trans = forward_w[-1] * step[:, cells - 1]  3.01 us
  transfers between devices with their start and end apart: 24, of which 7 were waited for; matrix products, arithmetic and copies ran while one was open for 0% of the time, Pallas kernels for 0%

profile of v1, /device:TPU:34, one launch (start us, length us, event | category | flops | bytes accessed | tf_op | source)
XLA Modules:
  0.0 141.4 jit_solution(679142526012948634)
XLA Ops:
  0.6 2.3 %negate_exponential_fusion = f32[32,4,4096]{2,1,0:T(4,128)S(1)} fusion(f32[32,4,4096]{2,1,0:T(4,128)} %param.3), kind=kLoop, calls=%fused_computation.3 | loop fusion | flops 1048576 | bytes 4194304 | tf_op jit(solution)/shard_map/exp | solution.py:55
  2.9 0.0 copy-start.2
  3.0 0.0 copy-start
  3.0 0.0 copy-start.1
  3.0 3.0 %slice_multiply_fusion.4 = (f32[32,1,4096]{2,1,0:T(1,128)S(1)}, f32[32,1,4096]{2,1,0:T(1,128)S(1)}, f32[32,1,4096]{2,1,0:T(1,128)S(1)}, f32[32,1,4096]{2,1,0:T(1...) fusion(f32[32,4,4096]{2,1,0:T(4,128)S(1)} %negate_exponential_fusion), kind=kLoop, calls=%fused_computation.110 | loop fusion | flops 655360 | bytes 5767168 | tf_op jit(solution)/shard_map/mul | solution.py:62
  6.0 0.0 copy-done.2
  6.0 0.5 broadcast.33
  6.5 6.2 %multiply_reduce_fusion.1 = (f32[4,4096]{1,0:T(4,128)S(1)}, f32[32,4,4096]{2,1,0:T(4,128)}) fusion(f32[32,4,4096]{2,1,0:T(4,128)S(1)} %copy-done, f32[32,1,4096]{2,1,0:T(1,128)S(1)} %get-tuple-element.5, f32[32,1,4096]{2,1,0:T(1,128)S(1)} %get-tuple-element.6, f32[32,1,4096]{2,1,0:T(1,128)S(1)} %get-tuple-element.12, f32[32,1,4096]{2,1,0:T(1,128)S(1)} %broadcast.33, ...), kind=kLoop, calls=%fused_computation.4 | loop fusion | flops 7323648 | bytes 10027040 | tf_op jit(solution)/shard_map/reduce_sum | solution.py:49
  12.8 1.9 %collective-permute-start = (f32[4,4096]{1,0:T(4,128)S(1)}, f32[4,4096]{1,0:T(4,128)S(1)}, u32[]{:S(2)}, u32[]{:S(2)}) collective-permute-start(f32[4,4096]{1,0:T(4,128)S(1)} %get-tuple-element.9), channel_id=1, source_target_pairs={{0,32},{32,64},{64,96},{96,128},{128,160},{160,192},{192,224},{224... | collective-permute-start | bytes 196616 | tf_op jit(solution)/shard_map/ppermute | solution.py:13
  14.7 4.9 %collective-permute-done = f32[4,4096]{1,0:T(4,128)S(1)} collective-permute-done((f32[4,4096]{1,0:T(4,128)S(1)}, f32[4,4096]{1,0:T(4,128)S(1)}, u32[]{:S(2)}, u32[]{:S(2)}) %collective-permute-start) | collective-permute-done | bytes 65568 | tf_op jit(solution)/shard_map/ppermute | solution.py:13
  19.6 1.9 %collective-permute-start.1 = (f32[4,4096]{1,0:T(4,128)S(1)}, f32[4,4096]{1,0:T(4,128)S(1)}, u32[]{:S(2)}, u32[]{:S(2)}) collective-permute-start(f32[4,4096]{1,0:T(4,128)S(1)} %add.328), channel_id=1, source_target_pairs={{0,64},{32,96},{64,128},{96,160},{128,192},{160,224},{192,256},{22... | collective-permute-start | bytes 196616 | tf_op jit(solution)/shard_map/ppermute | solution.py:13
  21.5 5.4 %collective-permute-done.1 = f32[4,4096]{1,0:T(4,128)S(1)} collective-permute-done((f32[4,4096]{1,0:T(4,128)S(1)}, f32[4,4096]{1,0:T(4,128)S(1)}, u32[]{:S(2)}, u32[]{:S(2)}) %collective-permute-start.1) | collective-permute-done | bytes 65568 | tf_op jit(solution)/shard_map/ppermute | solution.py:13
  27.0 1.9 %collective-permute-start.2 = (f32[4,4096]{1,0:T(4,128)S(1)}, f32[4,4096]{1,0:T(4,128)S(1)}, u32[]{:S(2)}, u32[]{:S(2)}) collective-permute-start(f32[4,4096]{1,0:T(4,128)S(1)} %add.330), channel_id=1, source_target_pairs={{0,128},{32,160},{64,192},{96,224},{128,256},{160,288},{192,320},{... | collective-permute-start | bytes 196616 | tf_op jit(solution)/shard_map/ppermute | solution.py:13
  28.9 6.3 %collective-permute-done.2 = f32[4,4096]{1,0:T(4,128)S(1)} collective-permute-done((f32[4,4096]{1,0:T(4,128)S(1)}, f32[4,4096]{1,0:T(4,128)S(1)}, u32[]{:S(2)}, u32[]{:S(2)}) %collective-permute-start.2) | collective-permute-done | bytes 65568 | tf_op jit(solution)/shard_map/ppermute | solution.py:13
  35.3 1.3 collective-permute-start.3
  36.6 8.7 %collective-permute-done.3 = f32[4,4096]{1,0:T(4,128)S(1)} collective-permute-done((f32[4,4096]{1,0:T(4,128)S(1)}, f32[4,4096]{1,0:T(4,128)S(1)}, u32[]{:S(2)}, u32[]{:S(2)}) %collective-permute-start.3) | collective-permute-done | bytes 65568 | tf_op jit(solution)/shard_map/ppermute | solution.py:13
  45.4 5.0 %fusion.43 = (f32[32,4096]{1,0:T(8,128)S(1)}, f32[32,4096]{1,0:T(8,128)S(1)}) fusion(f32[32,4,4096]{2,1,0:T(4,128)} %get-tuple-element.10, f32[4,4096]{1,0:T(4,128)S(1)} %negate_exponential_fusion.1, f32[32,4,4096]{2,1,0:T(4,128)S(1)} %copy-done), kind=kOutput, calls=%fused_computation.111 | output fusion | flops 20185088 | bytes 5308416 | tf_op jit(solution)/shard_map/jit(cumsum)/reduce_window_sum | solution.py:53
  50.4 0.1 multiply_add_fusion
  50.5 0.4 add.335
  50.8 1.1 constant_dynamic-slice_fusion.19
  51.9 3.4 %collective-permute-start.4 = (f32[32,8,128]{2,1,0:T(8,128)S(1)}, f32[32,8,128]{2,1,0:T(8,128)S(1)}, u32[]{:S(2)}, u32[]{:S(2)}) collective-permute-start(f32[32,8,128]{2,1,0:T(8,128)S(1)} %bitcast.237), channel_id=1, source_target_pairs={{0,1},{1,2},{2,3},{3,0},{4,5},{5,6},{6,7},{7,4},{8,9},{9,10},{10,1... | collective-permute-start | bytes 393224 | tf_op jit(solution)/shard_map/ppermute | solution.py:23
  55.3 3.0 %collective-permute-start.5 = (f32[32,8,128]{2,1,0:T(8,128)S(1)}, f32[32,8,128]{2,1,0:T(8,128)S(1)}, u32[]{:S(2)}, u32[]{:S(2)}) collective-permute-start(f32[32,8,128]{2,1,0:T(8,128)S(1)} %bitcast.236), channel_id=1, source_target_pairs={{0,2},{1,3},{2,0},{3,1},{4,6},{5,7},{6,4},{7,5},{8,10},{9,11},{10,... | collective-permute-start | bytes 393224 | tf_op jit(solution)/shard_map/ppermute | solution.py:23
  58.4 4.1 %collective-permute-start.6 = (f32[32,8,128]{2,1,0:T(8,128)S(1)}, f32[32,8,128]{2,1,0:T(8,128)S(1)}, u32[]{:S(2)}, u32[]{:S(2)}) collective-permute-start(f32[32,8,128]{2,1,0:T(8,128)S(1)} %bitcast.235), channel_id=1, source_target_pairs={{0,3},{1,0},{2,1},{3,2},{4,7},{5,4},{6,5},{7,6},{8,11},{9,8},{10,9... | collective-permute-start | bytes 393224 | tf_op jit(solution)/shard_map/ppermute | solution.py:23
  62.7 1.9 %collective-permute-start.7 = (f32[32,8,128]{2,1,0:T(8,128)S(1)}, f32[32,8,128]{2,1,0:T(8,128)S(1)}, u32[]{:S(2)}, u32[]{:S(2)}) collective-permute-start(f32[32,8,128]{2,1,0:T(8,128)S(1)} %bitcast.234), channel_id=1, source_target_pairs={{0,1},{1,2},{2,3},{3,0},{4,5},{5,6},{6,7},{7,4},{8,9},{9,10},{10,1... | collective-permute-start | bytes 393224 | tf_op jit(solution)/shard_map/ppermute | solution.py:23
  64.6 5.4 %collective-permute-start.8 = (f32[32,8,128]{2,1,0:T(8,128)S(1)}, f32[32,8,128]{2,1,0:T(8,128)S(1)}, u32[]{:S(2)}, u32[]{:S(2)}) collective-permute-start(f32[32,8,128]{2,1,0:T(8,128)S(1)} %bitcast.233), channel_id=1, source_target_pairs={{0,2},{1,3},{2,0},{3,1},{4,6},{5,7},{6,4},{7,5},{8,10},{9,11},{10,... | collective-permute-start | bytes 393224 | tf_op jit(solution)/shard_map/ppermute | solution.py:23
  70.0 0.0 collective-permute-done.4
  70.0 1.9 %collective-permute-start.9 = (f32[32,8,128]{2,1,0:T(8,128)S(1)}, f32[32,8,128]{2,1,0:T(8,128)S(1)}, u32[]{:S(2)}, u32[]{:S(2)}) collective-permute-start(f32[32,8,128]{2,1,0:T(8,128)S(1)} %bitcast.232), channel_id=1, source_target_pairs={{0,3},{1,0},{2,1},{3,2},{4,7},{5,4},{6,5},{7,6},{8,11},{9,8},{10,9... | collective-permute-start | bytes 393224 | tf_op jit(solution)/shard_map/ppermute | solution.py:23
  72.1 0.0 collective-permute-done.5
  72.2 0.0 collective-permute-done.6
  72.2 0.0 collective-permute-done.7
  72.2 0.8 collective-permute-done.8
  73.0 3.9 %collective-permute-done.9 = f32[32,8,128]{2,1,0:T(8,128)S(1)} collective-permute-done((f32[32,8,128]{2,1,0:T(8,128)S(1)}, f32[32,8,128]{2,1,0:T(8,128)S(1)}, u32[]{:S(2)}, u32[]{:S(2)}) %collective-permute-start.9) | collective-permute-done | bytes 131104 | tf_op jit(solution)/shard_map/ppermute | solution.py:23
  76.9 0.1 fusion.7
  77.0 0.1 constant_dynamic-slice_fusion.8
  77.2 4.3 %collective-permute-start.10 = (f32[32,128]{1,0:T(8,128)S(1)}, f32[32,128]{1,0:T(8,128)S(1)}, u32[]{:S(2)}, u32[]{:S(2)}) collective-permute-start(f32[32,128]{1,0:T(8,128)S(1)} %bitcast.259), channel_id=1, source_target_pairs={{0,4},{1,5},{2,6},{3,7},{4,8},{5,9},{6,10},{7,11},{8,12},{9,13},{1... | collective-permute-start | bytes 49160 | tf_op jit(solution)/shard_map/ppermute | solution.py:23
  81.5 6.1 %collective-permute-start.11 = (f32[32,128]{1,0:T(8,128)S(1)}, f32[32,128]{1,0:T(8,128)S(1)}, u32[]{:S(2)}, u32[]{:S(2)}) collective-permute-start(f32[32,128]{1,0:T(8,128)S(1)} %bitcast.258), channel_id=1, source_target_pairs={{0,8},{1,9},{2,10},{3,11},{4,12},{5,13},{6,14},{7,15},{8,16},{9,17... | collective-permute-start | bytes 49160 | tf_op jit(solution)/shard_map/ppermute | solution.py:23
  87.5 7.3 %collective-permute-start.12 = (f32[32,128]{1,0:T(8,128)S(1)}, f32[32,128]{1,0:T(8,128)S(1)}, u32[]{:S(2)}, u32[]{:S(2)}) collective-permute-start(f32[32,128]{1,0:T(8,128)S(1)} %bitcast.257), channel_id=1, source_target_pairs={{0,12},{1,13},{2,14},{3,15},{4,16},{5,17},{6,18},{7,19},{8,20},{9,... | collective-permute-start | bytes 49160 | tf_op jit(solution)/shard_map/ppermute | solution.py:23
  94.9 2.8 %collective-permute-start.13 = (f32[32,128]{1,0:T(8,128)S(1)}, f32[32,128]{1,0:T(8,128)S(1)}, u32[]{:S(2)}, u32[]{:S(2)}) collective-permute-start(f32[32,128]{1,0:T(8,128)S(1)} %bitcast.256), channel_id=1, source_target_pairs={{0,16},{1,17},{2,18},{3,19},{4,20},{5,21},{6,22},{7,23},{8,24},{9,... | collective-permute-start | bytes 49160 | tf_op jit(solution)/shard_map/ppermute | solution.py:23
  97.7 6.9 %collective-permute-start.14 = (f32[32,128]{1,0:T(8,128)S(1)}, f32[32,128]{1,0:T(8,128)S(1)}, u32[]{:S(2)}, u32[]{:S(2)}) collective-permute-start(f32[32,128]{1,0:T(8,128)S(1)} %bitcast.255), channel_id=1, source_target_pairs={{0,20},{1,21},{2,22},{3,23},{4,24},{5,25},{6,26},{7,27},{8,28},{9,... | collective-permute-start | bytes 49160 | tf_op jit(solution)/shard_map/ppermute | solution.py:23
  104.6 0.1 constant_dynamic-slice_fusion
  104.8 0.0 collective-permute-done.10
  104.8 3.7 %collective-permute-start.15 = (f32[32,128]{1,0:T(8,128)S(1)}, f32[32,128]{1,0:T(8,128)S(1)}, u32[]{:S(2)}, u32[]{:S(2)}) collective-permute-start(f32[32,128]{1,0:T(8,128)S(1)} %bitcast.253), channel_id=1, source_target_pairs={{0,24},{1,25},{2,26},{3,27},{4,28},{5,29},{6,30},{7,31},{8,0},{9,1... | collective-permute-start | bytes 49160 | tf_op jit(solution)/shard_map/ppermute | solution.py:23
  108.5 0.0 collective-permute-done.11
  108.5 2.5 %collective-permute-start.16 = (f32[32,128]{1,0:T(8,128)S(1)}, f32[32,128]{1,0:T(8,128)S(1)}, u32[]{:S(2)}, u32[]{:S(2)}) collective-permute-start(f32[32,128]{1,0:T(8,128)S(1)} %bitcast.251), channel_id=1, source_target_pairs={{0,28},{1,29},{2,30},{3,31},{4,0},{5,1},{6,2},{7,3},{8,4},{9,5},{1... | collective-permute-start | bytes 49160 | tf_op jit(solution)/shard_map/ppermute | solution.py:23
  110.9 0.0 collective-permute-done.12
  111.0 3.4 %collective-permute-start.17 = (f32[32,128]{1,0:T(8,128)S(1)}, f32[32,128]{1,0:T(8,128)S(1)}, u32[]{:S(2)}, u32[]{:S(2)}) collective-permute-start(f32[32,128]{1,0:T(8,128)S(1)} %bitcast.254), channel_id=1, source_target_pairs={{0,4},{1,5},{2,6},{3,7},{4,8},{5,9},{6,10},{7,11},{8,12},{9,13},{1... | collective-permute-start | bytes 49160 | tf_op jit(solution)/shard_map/ppermute | solution.py:23
  114.4 0.0 collective-permute-done.13
  114.4 3.1 %collective-permute-start.18 = (f32[32,128]{1,0:T(8,128)S(1)}, f32[32,128]{1,0:T(8,128)S(1)}, u32[]{:S(2)}, u32[]{:S(2)}) collective-permute-start(f32[32,128]{1,0:T(8,128)S(1)} %bitcast.252), channel_id=1, source_target_pairs={{0,8},{1,9},{2,10},{3,11},{4,12},{5,13},{6,14},{7,15},{8,16},{9,17... | collective-permute-start | bytes 49160 | tf_op jit(solution)/shard_map/ppermute | solution.py:23
  117.5 0.0 collective-permute-done.14
  117.5 2.6 %collective-permute-start.19 = (f32[32,128]{1,0:T(8,128)S(1)}, f32[32,128]{1,0:T(8,128)S(1)}, u32[]{:S(2)}, u32[]{:S(2)}) collective-permute-start(f32[32,128]{1,0:T(8,128)S(1)} %bitcast.250), channel_id=1, source_target_pairs={{0,12},{1,13},{2,14},{3,15},{4,16},{5,17},{6,18},{7,19},{8,20},{9,... | collective-permute-start | bytes 49160 | tf_op jit(solution)/shard_map/ppermute | solution.py:23
  120.1 0.0 collective-permute-done.15
  120.1 6.3 %collective-permute-start.20 = (f32[32,128]{1,0:T(8,128)S(1)}, f32[32,128]{1,0:T(8,128)S(1)}, u32[]{:S(2)}, u32[]{:S(2)}) collective-permute-start(f32[32,128]{1,0:T(8,128)S(1)} %bitcast.249), channel_id=1, source_target_pairs={{0,16},{1,17},{2,18},{3,19},{4,20},{5,21},{6,22},{7,23},{8,24},{9,... | collective-permute-start | bytes 49160 | tf_op jit(solution)/shard_map/ppermute | solution.py:23
  126.4 0.0 collective-permute-done.16
  126.4 3.1 %collective-permute-start.21 = (f32[32,128]{1,0:T(8,128)S(1)}, f32[32,128]{1,0:T(8,128)S(1)}, u32[]{:S(2)}, u32[]{:S(2)}) collective-permute-start(f32[32,128]{1,0:T(8,128)S(1)} %bitcast.248), channel_id=1, source_target_pairs={{0,20},{1,21},{2,22},{3,23},{4,24},{5,25},{6,26},{7,27},{8,28},{9,... | collective-permute-start | bytes 49160 | tf_op jit(solution)/shard_map/ppermute | solution.py:23
  129.5 0.0 collective-permute-done.17
  129.5 5.5 %collective-permute-start.22 = (f32[32,128]{1,0:T(8,128)S(1)}, f32[32,128]{1,0:T(8,128)S(1)}, u32[]{:S(2)}, u32[]{:S(2)}) collective-permute-start(f32[32,128]{1,0:T(8,128)S(1)} %bitcast.247), channel_id=1, source_target_pairs={{0,24},{1,25},{2,26},{3,27},{4,28},{5,29},{6,30},{7,31},{8,0},{9,1... | collective-permute-start | bytes 49160 | tf_op jit(solution)/shard_map/ppermute | solution.py:23
  135.1 0.0 collective-permute-done.18
  135.1 3.4 %collective-permute-start.23 = (f32[32,128]{1,0:T(8,128)S(1)}, f32[32,128]{1,0:T(8,128)S(1)}, u32[]{:S(2)}, u32[]{:S(2)}) collective-permute-start(f32[32,128]{1,0:T(8,128)S(1)} %bitcast.246), channel_id=1, source_target_pairs={{0,28},{1,29},{2,30},{3,31},{4,0},{5,1},{6,2},{7,3},{8,4},{9,5},{1... | collective-permute-start | bytes 49160 | tf_op jit(solution)/shard_map/ppermute | solution.py:23
  138.5 0.0 collective-permute-done.19
  138.5 0.0 collective-permute-done.20
  138.5 0.0 collective-permute-done.21
  138.5 0.0 collective-permute-done.22
  138.5 2.2 %collective-permute-done.23 = f32[32,128]{1,0:T(8,128)S(1)} collective-permute-done((f32[32,128]{1,0:T(8,128)S(1)}, f32[32,128]{1,0:T(8,128)S(1)}, u32[]{:S(2)}, u32[]{:S(2)}) %collective-permute-start.23) | collective-permute-done | bytes 16416 | tf_op jit(solution)/shard_map/ppermute | solution.py:23
  140.7 0.7 fusion.22
  (25 shorter events, 0.2 us)
Async XLA Ops:
  2.9 3.1 %copy-start.2 = (s32[32]{0:T(128)S(1)}, s32[32]{0:T(128)}, u32[]{:S(2)}) copy-start(s32[32]{0:T(128)} %param.5) | copy-start | bytes 388
  3.0 3.5 %copy-start = (f32[32,4,4096]{2,1,0:T(4,128)S(1)}, f32[32,4,4096]{2,1,0:T(4,128)}, u32[]{:S(2)}) copy-start(f32[32,4,4096]{2,1,0:T(4,128)} %param.3) | copy-start | bytes 6291460
  3.0 3.5 %copy-start.1 = (f32[32,4,4096]{2,1,0:T(4,128)S(1)}, f32[32,4,4096]{2,1,0:T(4,128)}, u32[]{:S(2)}) copy-start(f32[32,4,4096]{2,1,0:T(4,128)} %param.4) | copy-start | bytes 6291460
  12.8 6.8 %collective-permute-start = (f32[4,4096]{1,0:T(4,128)S(1)}, f32[4,4096]{1,0:T(4,128)S(1)}, u32[]{:S(2)}, u32[]{:S(2)}) collective-permute-start(f32[4,4096]{1,0:T(4,128)S(1)} %get-tuple-element.9), channel_id=1, source_target_pairs={{0,32},{32,64},{64,96},{96,128},{128,160},{160,192},{192,224},{224... | collective-permute-start | bytes 196616 | tf_op jit(solution)/shard_map/ppermute | solution.py:13
  19.6 7.4 %collective-permute-start.1 = (f32[4,4096]{1,0:T(4,128)S(1)}, f32[4,4096]{1,0:T(4,128)S(1)}, u32[]{:S(2)}, u32[]{:S(2)}) collective-permute-start(f32[4,4096]{1,0:T(4,128)S(1)} %add.328), channel_id=1, source_target_pairs={{0,64},{32,96},{64,128},{96,160},{128,192},{160,224},{192,256},{22... | collective-permute-start | bytes 196616 | tf_op jit(solution)/shard_map/ppermute | solution.py:13
  27.0 8.3 %collective-permute-start.2 = (f32[4,4096]{1,0:T(4,128)S(1)}, f32[4,4096]{1,0:T(4,128)S(1)}, u32[]{:S(2)}, u32[]{:S(2)}) collective-permute-start(f32[4,4096]{1,0:T(4,128)S(1)} %add.330), channel_id=1, source_target_pairs={{0,128},{32,160},{64,192},{96,224},{128,256},{160,288},{192,320},{... | collective-permute-start | bytes 196616 | tf_op jit(solution)/shard_map/ppermute | solution.py:13
  35.3 10.1 %collective-permute-start.3 = (f32[4,4096]{1,0:T(4,128)S(1)}, f32[4,4096]{1,0:T(4,128)S(1)}, u32[]{:S(2)}, u32[]{:S(2)}) collective-permute-start(f32[4,4096]{1,0:T(4,128)S(1)} %add.332), channel_id=1, source_target_pairs={{0,256},{32,288},{64,320},{96,352},{128,384},{160,416},{192,448},{... | collective-permute-start | bytes 196616 | tf_op jit(solution)/shard_map/ppermute | solution.py:13
  51.9 18.1 %collective-permute-start.4 = (f32[32,8,128]{2,1,0:T(8,128)S(1)}, f32[32,8,128]{2,1,0:T(8,128)S(1)}, u32[]{:S(2)}, u32[]{:S(2)}) collective-permute-start(f32[32,8,128]{2,1,0:T(8,128)S(1)} %bitcast.237), channel_id=1, source_target_pairs={{0,1},{1,2},{2,3},{3,0},{4,5},{5,6},{6,7},{7,4},{8,9},{9,10},{10,1... | collective-permute-start | bytes 393224 | tf_op jit(solution)/shard_map/ppermute | solution.py:23
  55.3 16.8 %collective-permute-start.5 = (f32[32,8,128]{2,1,0:T(8,128)S(1)}, f32[32,8,128]{2,1,0:T(8,128)S(1)}, u32[]{:S(2)}, u32[]{:S(2)}) collective-permute-start(f32[32,8,128]{2,1,0:T(8,128)S(1)} %bitcast.236), channel_id=1, source_target_pairs={{0,2},{1,3},{2,0},{3,1},{4,6},{5,7},{6,4},{7,5},{8,10},{9,11},{10,... | collective-permute-start | bytes 393224 | tf_op jit(solution)/shard_map/ppermute | solution.py:23
  58.4 13.8 %collective-permute-start.6 = (f32[32,8,128]{2,1,0:T(8,128)S(1)}, f32[32,8,128]{2,1,0:T(8,128)S(1)}, u32[]{:S(2)}, u32[]{:S(2)}) collective-permute-start(f32[32,8,128]{2,1,0:T(8,128)S(1)} %bitcast.235), channel_id=1, source_target_pairs={{0,3},{1,0},{2,1},{3,2},{4,7},{5,4},{6,5},{7,6},{8,11},{9,8},{10,9... | collective-permute-start | bytes 393224 | tf_op jit(solution)/shard_map/ppermute | solution.py:23
  62.7 9.5 %collective-permute-start.7 = (f32[32,8,128]{2,1,0:T(8,128)S(1)}, f32[32,8,128]{2,1,0:T(8,128)S(1)}, u32[]{:S(2)}, u32[]{:S(2)}) collective-permute-start(f32[32,8,128]{2,1,0:T(8,128)S(1)} %bitcast.234), channel_id=1, source_target_pairs={{0,1},{1,2},{2,3},{3,0},{4,5},{5,6},{6,7},{7,4},{8,9},{9,10},{10,1... | collective-permute-start | bytes 393224 | tf_op jit(solution)/shard_map/ppermute | solution.py:23
  64.6 8.4 %collective-permute-start.8 = (f32[32,8,128]{2,1,0:T(8,128)S(1)}, f32[32,8,128]{2,1,0:T(8,128)S(1)}, u32[]{:S(2)}, u32[]{:S(2)}) collective-permute-start(f32[32,8,128]{2,1,0:T(8,128)S(1)} %bitcast.233), channel_id=1, source_target_pairs={{0,2},{1,3},{2,0},{3,1},{4,6},{5,7},{6,4},{7,5},{8,10},{9,11},{10,... | collective-permute-start | bytes 393224 | tf_op jit(solution)/shard_map/ppermute | solution.py:23
  70.0 6.9 %collective-permute-start.9 = (f32[32,8,128]{2,1,0:T(8,128)S(1)}, f32[32,8,128]{2,1,0:T(8,128)S(1)}, u32[]{:S(2)}, u32[]{:S(2)}) collective-permute-start(f32[32,8,128]{2,1,0:T(8,128)S(1)} %bitcast.232), channel_id=1, source_target_pairs={{0,3},{1,0},{2,1},{3,2},{4,7},{5,4},{6,5},{7,6},{8,11},{9,8},{10,9... | collective-permute-start | bytes 393224 | tf_op jit(solution)/shard_map/ppermute | solution.py:23
  77.2 27.6 %collective-permute-start.10 = (f32[32,128]{1,0:T(8,128)S(1)}, f32[32,128]{1,0:T(8,128)S(1)}, u32[]{:S(2)}, u32[]{:S(2)}) collective-permute-start(f32[32,128]{1,0:T(8,128)S(1)} %bitcast.259), channel_id=1, source_target_pairs={{0,4},{1,5},{2,6},{3,7},{4,8},{5,9},{6,10},{7,11},{8,12},{9,13},{1... | collective-permute-start | bytes 49160 | tf_op jit(solution)/shard_map/ppermute | solution.py:23
  81.5 27.0 %collective-permute-start.11 = (f32[32,128]{1,0:T(8,128)S(1)}, f32[32,128]{1,0:T(8,128)S(1)}, u32[]{:S(2)}, u32[]{:S(2)}) collective-permute-start(f32[32,128]{1,0:T(8,128)S(1)} %bitcast.258), channel_id=1, source_target_pairs={{0,8},{1,9},{2,10},{3,11},{4,12},{5,13},{6,14},{7,15},{8,16},{9,17... | collective-permute-start | bytes 49160 | tf_op jit(solution)/shard_map/ppermute | solution.py:23
  87.5 23.4 %collective-permute-start.12 = (f32[32,128]{1,0:T(8,128)S(1)}, f32[32,128]{1,0:T(8,128)S(1)}, u32[]{:S(2)}, u32[]{:S(2)}) collective-permute-start(f32[32,128]{1,0:T(8,128)S(1)} %bitcast.257), channel_id=1, source_target_pairs={{0,12},{1,13},{2,14},{3,15},{4,16},{5,17},{6,18},{7,19},{8,20},{9,... | collective-permute-start | bytes 49160 | tf_op jit(solution)/shard_map/ppermute | solution.py:23
  94.9 19.5 %collective-permute-start.13 = (f32[32,128]{1,0:T(8,128)S(1)}, f32[32,128]{1,0:T(8,128)S(1)}, u32[]{:S(2)}, u32[]{:S(2)}) collective-permute-start(f32[32,128]{1,0:T(8,128)S(1)} %bitcast.256), channel_id=1, source_target_pairs={{0,16},{1,17},{2,18},{3,19},{4,20},{5,21},{6,22},{7,23},{8,24},{9,... | collective-permute-start | bytes 49160 | tf_op jit(solution)/shard_map/ppermute | solution.py:23
  97.7 19.8 %collective-permute-start.14 = (f32[32,128]{1,0:T(8,128)S(1)}, f32[32,128]{1,0:T(8,128)S(1)}, u32[]{:S(2)}, u32[]{:S(2)}) collective-permute-start(f32[32,128]{1,0:T(8,128)S(1)} %bitcast.255), channel_id=1, source_target_pairs={{0,20},{1,21},{2,22},{3,23},{4,24},{5,25},{6,26},{7,27},{8,28},{9,... | collective-permute-start | bytes 49160 | tf_op jit(solution)/shard_map/ppermute | solution.py:23
  104.8 15.3 %collective-permute-start.15 = (f32[32,128]{1,0:T(8,128)S(1)}, f32[32,128]{1,0:T(8,128)S(1)}, u32[]{:S(2)}, u32[]{:S(2)}) collective-permute-start(f32[32,128]{1,0:T(8,128)S(1)} %bitcast.253), channel_id=1, source_target_pairs={{0,24},{1,25},{2,26},{3,27},{4,28},{5,29},{6,30},{7,31},{8,0},{9,1... | collective-permute-start | bytes 49160 | tf_op jit(solution)/shard_map/ppermute | solution.py:23
  108.5 17.9 %collective-permute-start.16 = (f32[32,128]{1,0:T(8,128)S(1)}, f32[32,128]{1,0:T(8,128)S(1)}, u32[]{:S(2)}, u32[]{:S(2)}) collective-permute-start(f32[32,128]{1,0:T(8,128)S(1)} %bitcast.251), channel_id=1, source_target_pairs={{0,28},{1,29},{2,30},{3,31},{4,0},{5,1},{6,2},{7,3},{8,4},{9,5},{1... | collective-permute-start | bytes 49160 | tf_op jit(solution)/shard_map/ppermute | solution.py:23
  111.0 18.6 %collective-permute-start.17 = (f32[32,128]{1,0:T(8,128)S(1)}, f32[32,128]{1,0:T(8,128)S(1)}, u32[]{:S(2)}, u32[]{:S(2)}) collective-permute-start(f32[32,128]{1,0:T(8,128)S(1)} %bitcast.254), channel_id=1, source_target_pairs={{0,4},{1,5},{2,6},{3,7},{4,8},{5,9},{6,10},{7,11},{8,12},{9,13},{1... | collective-permute-start | bytes 49160 | tf_op jit(solution)/shard_map/ppermute | solution.py:23
  114.4 20.7 %collective-permute-start.18 = (f32[32,128]{1,0:T(8,128)S(1)}, f32[32,128]{1,0:T(8,128)S(1)}, u32[]{:S(2)}, u32[]{:S(2)}) collective-permute-start(f32[32,128]{1,0:T(8,128)S(1)} %bitcast.252), channel_id=1, source_target_pairs={{0,8},{1,9},{2,10},{3,11},{4,12},{5,13},{6,14},{7,15},{8,16},{9,17... | collective-permute-start | bytes 49160 | tf_op jit(solution)/shard_map/ppermute | solution.py:23
  117.5 21.0 %collective-permute-start.19 = (f32[32,128]{1,0:T(8,128)S(1)}, f32[32,128]{1,0:T(8,128)S(1)}, u32[]{:S(2)}, u32[]{:S(2)}) collective-permute-start(f32[32,128]{1,0:T(8,128)S(1)} %bitcast.250), channel_id=1, source_target_pairs={{0,12},{1,13},{2,14},{3,15},{4,16},{5,17},{6,18},{7,19},{8,20},{9,... | collective-permute-start | bytes 49160 | tf_op jit(solution)/shard_map/ppermute | solution.py:23
  120.1 18.4 %collective-permute-start.20 = (f32[32,128]{1,0:T(8,128)S(1)}, f32[32,128]{1,0:T(8,128)S(1)}, u32[]{:S(2)}, u32[]{:S(2)}) collective-permute-start(f32[32,128]{1,0:T(8,128)S(1)} %bitcast.249), channel_id=1, source_target_pairs={{0,16},{1,17},{2,18},{3,19},{4,20},{5,21},{6,22},{7,23},{8,24},{9,... | collective-permute-start | bytes 49160 | tf_op jit(solution)/shard_map/ppermute | solution.py:23
  126.4 12.1 %collective-permute-start.21 = (f32[32,128]{1,0:T(8,128)S(1)}, f32[32,128]{1,0:T(8,128)S(1)}, u32[]{:S(2)}, u32[]{:S(2)}) collective-permute-start(f32[32,128]{1,0:T(8,128)S(1)} %bitcast.248), channel_id=1, source_target_pairs={{0,20},{1,21},{2,22},{3,23},{4,24},{5,25},{6,26},{7,27},{8,28},{9,... | collective-permute-start | bytes 49160 | tf_op jit(solution)/shard_map/ppermute | solution.py:23
  129.5 9.0 %collective-permute-start.22 = (f32[32,128]{1,0:T(8,128)S(1)}, f32[32,128]{1,0:T(8,128)S(1)}, u32[]{:S(2)}, u32[]{:S(2)}) collective-permute-start(f32[32,128]{1,0:T(8,128)S(1)} %bitcast.247), channel_id=1, source_target_pairs={{0,24},{1,25},{2,26},{3,27},{4,28},{5,29},{6,30},{7,31},{8,0},{9,1... | collective-permute-start | bytes 49160 | tf_op jit(solution)/shard_map/ppermute | solution.py:23
  135.1 5.6 %collective-permute-start.23 = (f32[32,128]{1,0:T(8,128)S(1)}, f32[32,128]{1,0:T(8,128)S(1)}, u32[]{:S(2)}, u32[]{:S(2)}) collective-permute-start(f32[32,128]{1,0:T(8,128)S(1)} %bitcast.246), channel_id=1, source_target_pairs={{0,28},{1,29},{2,30},{3,31},{4,0},{5,1},{6,2},{7,3},{8,4},{9,5},{1... | collective-permute-start | bytes 49160 | tf_op jit(solution)/shard_map/ppermute | solution.py:23

commit v2 on v1

--- a/solution.py
+++ b/solution.py
@@ -6,15 +6,13 @@
 
 def light_prefix(value):
     count = lax.axis_size("light")
-    total = value
-    received = jnp.zeros_like(value)
-    shift = 1
-    while shift < count:
-        got = lax.ppermute(total, "light", [(i, i + shift) for i in range(count - shift)])
-        total = total + got
-        received = received + got
-        shift *= 2
-    return received
+    cells, columns = value.shape
+    chunks = value.reshape(cells, count, columns // count).transpose(1, 0, 2)
+    mine = lax.all_to_all(chunks, "light", 0, 0)
+    running = jnp.cumsum(mine, axis=0)
+    before = jnp.concatenate([jnp.zeros_like(running[:1]), running[:-1]], axis=0)
+    back = lax.all_to_all(before, "light", 0, 0)
+    return back.transpose(1, 0, 2).reshape(cells, columns)
 
 
 def group_exchange(block_of, my_pos, size, pairs_for):
@@ -65,36 +63,13 @@
         flat = jnp.sum(base, axis=1)
         lit_part = base * shade
 
-        my_view = lax.axis_index("view")
-        my_x = my_view % x_count
-        my_z = my_view // x_count
-
-        def pairs_x(k):
-            return [(z * x_count + x, z * x_count + (x + k) % x_count) for z in range(z_count) for x in range(x_count)]
-
-        def pairs_z(k):
-            return [(z * x_count + x, ((z + k) % z_count) * x_count + x) for z in range(z_count) for x in range(x_count)]
-
         width = columns // view_count
-
-        def x_blocks(array):
-            grid = array.reshape(rows, z_count, x_count, width)
-            return lambda pos: lax.dynamic_index_in_dim(grid, pos, 2, keepdims=False)
-
-        def z_blocks(array):
-            return lambda pos: lax.dynamic_index_in_dim(array, pos, 1, keepdims=False)
-
-        trans_x = group_exchange(x_blocks(trans), my_x, x_count, pairs_x)
-        trans_xg = jnp.prod(trans_x, axis=0)
-        trans_z = group_exchange(z_blocks(trans_xg), my_z, z_count, pairs_z)
-        coverage = jnp.prod(trans_z, axis=0)
-
         light = jnp.exp(-incoming)
         color = 0.2 * flat + jnp.sum(lit_part * light[None], axis=1)
-        color_x = group_exchange(x_blocks(color), my_x, x_count, pairs_x)
-        color_xg = composite(color_x, trans_x, reversed_rows[:, None, None])
-        color_z = group_exchange(z_blocks(color_xg), my_z, z_count, pairs_z)
-        radiance = composite(color_z, trans_z, reversed_rows[:, None])
+        stacked = jnp.stack([color, trans]).reshape(2, rows, view_count, width).transpose(2, 0, 1, 3)
+        pieces = lax.all_to_all(stacked, "view", 0, 0)
+        radiance = composite(pieces[:, 0], pieces[:, 1], reversed_rows[:, None])
+        coverage = jnp.prod(pieces[:, 1], axis=0)
         return (radiance, coverage)
 
     return shards

time: 142 us -> 85.4 us (0.60)
  the two profiles are of different devices: /device:TPU:34 before, /device:TPU:2 now
where the time goes in v2:
time: 85.4 us; the launch traced here: 85.2 us
  blocking collectives  67.1 us (79%)
  other arithmetic  16.1 us (19%)
  local copies, waits for them, and re-layouts  1.2 us (1%)
    all_to_all x1, blocking collectives, shards(): pieces = lax.all_to_all(stacked, 'view', 0, 0)  41.9 us
    all_to_all x1, blocking collectives, light_prefix(): mine = lax.all_to_all(chunks, 'light', 0, 0)  14.9 us
    all_to_all x1, blocking collectives, light_prefix(): back = lax.all_to_all(before, 'light', 0, 0)  10.4 us
    reduce_sum x1, other arithmetic, shards(): slab_depth = jnp.sum(tau_light, axis=0)  5.08 us
    another operation x1, other arithmetic, shards(): local_depth = jnp.cumsum(tau_light, axis=0) - tau_light  3.57 us
    mul x1, other arithmetic, shards(): backward_w.insert(0, backward_w[0] * step[:, v + 1])  2.93 us
    exp x1, other arithmetic, shards(): step = jnp.exp(-tau_view)  2.31 us

profile of v2, /device:TPU:2, one launch (start us, length us, event | category | flops | bytes accessed | tf_op | source)
XLA Modules:
  0.0 85.2 jit_solution(12176201331125538238)
XLA Ops:
  0.6 0.7 broadcast_compare_fusion
  1.3 2.3 %negate_exponential_fusion = f32[32,4,4096]{2,1,0:T(4,128)S(1)} fusion(f32[32,4,4096]{2,1,0:T(4,128)} %param.3), kind=kLoop, calls=%fused_computation.3 | loop fusion | flops 1048576 | bytes 4194304 | tf_op jit(solution)/shard_map/exp | solution.py:53
  3.6 0.0 copy-start
  3.6 0.0 copy-start.1
  3.6 2.9 %slice_multiply_fusion.1 = (f32[32,1,4096]{2,1,0:T(1,128)S(1)}, f32[32,1,4096]{2,1,0:T(1,128)S(1)}, f32[32,1,4096]{2,1,0:T(1,128)S(1)}, f32[32,1,4096]{2,1,0:T(1...) fusion(f32[32,4,4096]{2,1,0:T(4,128)S(1)} %negate_exponential_fusion), kind=kLoop, calls=%fused_computation.12 | loop fusion | flops 655360 | bytes 5767168 | tf_op jit(solution)/shard_map/mul | solution.py:59
  6.6 0.5 broadcast.17
  7.0 0.0 copy-done
  7.1 0.0 copy-done.1
  7.1 5.1 %multiply_reduce_fusion.1 = (f32[4,4096]{1,0:T(4,128)S(1)}, f32[32,4,4096]{2,1,0:T(4,128)S(1)}) fusion(f32[32,4,4096]{2,1,0:T(4,128)S(1)} %copy-done, f32[32,1,4096]{2,1,0:T(1,128)S(1)} %get-tuple-element.14, f32[32,1,4096]{2,1,0:T(1,128)S(1)} %get-tuple-element.15, f32[32,1,4096]{2,1,0:T(1,128)S(1)} %get-tuple-element.11, f32[32,1,4096]{2,1,0:T(1,128)S(1)} %broadcast.17, ...), kind=kLoop, calls=%fused_computation.4 | loop fusion | flops 7323648 | bytes 10027040 | tf_op jit(solution)/shard_map/reduce_sum | solution.py:47
  12.2 14.9 %all_to_all.15 = f32[16,4,256]{2,1,0:T(4,128)S(1)} all-to-all(f32[16,4,256]{2,1,0:T(4,128)S(1)} %bitcast.282), channel_id=1, replica_groups=mesh['light'=16,'view'=32] {'light'}, dimensions={0} | all-to-all | bytes 131072 | tf_op jit(solution)/shard_map/all_to_all | solution.py:11
  27.1 10.4 %all_to_all.16 = f32[16,4,256]{2,1,0:T(4,128)S(1)} all-to-all(f32[16,4,256]{2,1,0:T(4,128)S(1)} %concatenate.4), channel_id=1, replica_groups=mesh['light'=16,'view'=32] {'light'}, dimensions={0} | all-to-all | bytes 131072 | tf_op jit(solution)/shard_map/all_to_all | solution.py:14
  37.5 3.6 %fusion.10 = (f32[32,4096]{1,0:T(8,128)S(1)}, f32[32,4096]{1,0:T(8,128)S(1)}) fusion(f32[32,4,4096]{2,1,0:T(4,128)S(1)} %get-tuple-element.10, f32[4,4096]{1,0:T(4,128)S(1)} %bitcast.283, f32[32,4,4096]{2,1,0:T(4,128)S(1)} %copy-done), kind=kOutput, calls=%fused_computation.88 | output fusion | flops 20185088 | bytes 5308416 | tf_op jit(solution)/shard_map/jit(cumsum)/reduce_window_sum | solution.py:51
  41.1 0.1 add_bitcast_fusion
  41.1 0.1 copy.70
  41.2 0.1 maximum_bitcast_fusion
  41.3 0.6 copy.69
  42.0 41.9 %all_to_all.17 = f32[32,2,32,128]{3,2,1,0:T(8,128)S(1)} all-to-all(f32[32,2,32,128]{3,2,1,0:T(8,128)S(1)} %copy.69), channel_id=1, replica_groups=mesh['light'=16,'view'=32] {'view'}, dimensions={0} | all-to-all | bytes 2097152 | tf_op jit(solution)/shard_map/all_to_all | solution.py:70
  83.8 0.7 fusion.6
  84.5 0.6 slice_reduce_fusion
  (4 shorter events, 0.1 us)
Async XLA Ops:
  3.6 3.4 %copy-start = (f32[32,4,4096]{2,1,0:T(4,128)S(1)}, f32[32,4,4096]{2,1,0:T(4,128)}, u32[]{:S(2)}) copy-start(f32[32,4,4096]{2,1,0:T(4,128)} %param.3) | copy-start | bytes 6291460
  3.6 3.4 %copy-start.1 = (f32[32,4,4096]{2,1,0:T(4,128)S(1)}, f32[32,4,4096]{2,1,0:T(4,128)}, u32[]{:S(2)}) copy-start(f32[32,4,4096]{2,1,0:T(4,128)} %param.4) | copy-start | bytes 6291460

commit v3 on v2

v3 whole, which is shorter than its diff:
```python
import jax
import jax.numpy as jnp
from jax import lax
from jax.sharding import Mesh
from jax.sharding import PartitionSpec as P

VIEW = ("vz", "vx")


def light_prefix(value):
    count = lax.axis_size("light")
    cells, columns = value.shape
    chunks = value.reshape(cells, count, columns // count).transpose(1, 0, 2)
    mine = lax.all_to_all(chunks, "light", 0, 0)
    running = jnp.cumsum(mine, axis=0)
    before = jnp.concatenate([jnp.zeros_like(running[:1]), running[:-1]], axis=0)
    back = lax.all_to_all(before, "light", 0, 0)
    return back.transpose(1, 0, 2).reshape(cells, columns)


def composite(colors, transes, reversed_rows):
    count = colors.shape[0]
    forward = colors[count - 1]
    for j in range(count - 2, -1, -1):
        forward = colors[j] + transes[j] * forward
    backward = colors[0]
    for j in range(1, count):
        backward = colors[j] + transes[j] * backward
    return jnp.where(reversed_rows, backward, forward)


def shards(density, emission, facing):
    rows, cells, columns = density.shape
    light_count = lax.axis_size("light")
    z_count = lax.axis_size("vz")
    x_count = lax.axis_size("vx")
    view_count = z_count * x_count
    tau_light = density * (1.0 / (rows * light_count))
    tau_view = density * (1.0 / (cells * view_count))
    slab_depth = jnp.sum(tau_light, axis=0)
    incoming = light_prefix(slab_depth)

    reversed_rows = facing == 1
    local_depth = jnp.cumsum(tau_light, axis=0) - tau_light
    shade = jnp.exp(-local_depth)
    step = jnp.exp(-tau_view)
    forward_w = [jnp.ones_like(step[:, 0])]
    for v in range(1, cells):
        forward_w.append(forward_w[-1] * step[:, v - 1])
    backward_w = [jnp.ones_like(step[:, 0])]
    for v in range(cells - 2, -1, -1):
        backward_w.insert(0, backward_w[0] * step[:, v + 1])
    trans = forward_w[-1] * step[:, cells - 1]
    weight = jnp.where(reversed_rows[:, None, None], jnp.stack(backward_w, 1), jnp.stack(forward_w, 1))
    base = emission * (1.0 - step) * weight
    flat = jnp.sum(base, axis=1)
    lit_part = base * shade

    width = columns // view_count
    light = jnp.exp(-incoming)
    color = 0.2 * flat + jnp.sum(lit_part * light[None], axis=1)
    stacked = jnp.stack([color, trans]).reshape(2, rows, z_count, x_count, width).transpose(3, 0, 1, 2, 4)
    along_x = lax.all_to_all(stacked, "vx", 0, 0)
    color_x = composite(along_x[:, 0], along_x[:, 1], reversed_rows[:, None, None])
    trans_x = jnp.prod(along_x[:, 1], axis=0)
    stacked = jnp.stack([color_x, trans_x]).transpose(2, 0, 1, 3)
    along_z = lax.all_to_all(stacked, "vz", 0, 0)
    radiance = composite(along_z[:, 0], along_z[:, 1], reversed_rows[:, None])
    coverage = jnp.prod(along_z[:, 1], axis=0)
    return (radiance, coverage)


def view_split(mesh):
    row = mesh.devices.reshape(mesh.devices.shape[0], -1)[0]
    coords = [getattr(d, "coords", None) for d in row]
    if any(c is None for c in coords):
        return 1
    first_z = coords[0][2]
    return sum(1 for c in coords if c[2] == first_z)


def solution(mesh):
    x_count = view_split(mesh)
    light_count, view_count = mesh.devices.shape
    split = Mesh(mesh.devices.reshape(light_count, view_count // x_count, x_count), ("light",) + VIEW)
    return jax.shard_map(
        shards,
        mesh=split,
        in_specs=(P("light", VIEW, None), P("light", VIEW, None), P("light")),
        out_specs=(P("light", VIEW), P("light", VIEW)),
        check_vma=False,
    )
```

time: 85.4 us -> 83.8 us (0.981)
  blocking collectives: 67.1 us -> 65.4 us
    all_to_all x1 -> x2, blocking collectives: 41.9 us -> 40.2 us  [the longest x1 21.4 us: shards(): along_z = lax.all_to_all(stacked, 'vz', 0, 0)]
where the time goes in v3:
time: 83.8 us; the launch traced here: 83.5 us
  blocking collectives  65.4 us (78%)
  other arithmetic  16.4 us (20%)
  local copies, waits for them, and re-layouts  0.97 us (1%)
    all_to_all x1, blocking collectives, shards(): along_z = lax.all_to_all(stacked, 'vz', 0, 0)  21.4 us
    all_to_all x1, blocking collectives, shards(): along_x = lax.all_to_all(stacked, 'vx', 0, 0)  18.8 us
    all_to_all x1, blocking collectives, light_prefix(): mine = lax.all_to_all(chunks, 'light', 0, 0)  14.9 us
    all_to_all x1, blocking collectives, light_prefix(): back = lax.all_to_all(before, 'light', 0, 0)  10.4 us
    reduce_sum x1, other arithmetic, shards(): slab_depth = jnp.sum(tau_light, axis=0)  5.08 us
    another operation x1, other arithmetic, shards(): local_depth = jnp.cumsum(tau_light, axis=0) - tau_light  3.57 us
    mul x1, other arithmetic, shards(): backward_w.insert(0, backward_w[0] * step[:, v + 1])  2.93 us
    exp x1, other arithmetic, shards(): step = jnp.exp(-tau_view)  2.31 us

profile of v3, /device:TPU:2, one launch (start us, length us, event | category | flops | bytes accessed | tf_op | source)
XLA Modules:
  0.0 83.5 jit_solution(7200856845308005787)
XLA Ops:
  0.6 0.7 broadcast_compare_fusion
  1.3 2.3 %negate_exponential_fusion = f32[32,4,4096]{2,1,0:T(4,128)S(1)} fusion(f32[32,4,4096]{2,1,0:T(4,128)} %param.3), kind=kLoop, calls=%fused_computation.3 | loop fusion | flops 1048576 | bytes 4194304 | tf_op jit(solution)/shard_map/exp | solution.py:46
  3.6 0.0 copy-start
  3.6 0.0 copy-start.1
  3.6 2.9 %slice_multiply_fusion.1 = (f32[32,1,4096]{2,1,0:T(1,128)S(1)}, f32[32,1,4096]{2,1,0:T(1,128)S(1)}, f32[32,1,4096]{2,1,0:T(1,128)S(1)}, f32[32,1,4096]{2,1,0:T(1...) fusion(f32[32,4,4096]{2,1,0:T(4,128)S(1)} %negate_exponential_fusion), kind=kLoop, calls=%fused_computation.12 | loop fusion | flops 655360 | bytes 5767168 | tf_op jit(solution)/shard_map/mul | solution.py:52
  6.6 0.5 broadcast.24
  7.0 0.0 copy-done
  7.1 0.0 copy-done.1
  7.1 5.1 %multiply_reduce_fusion.1 = (f32[4,4096]{1,0:T(4,128)S(1)}, f32[32,4,4096]{2,1,0:T(4,128)S(1)}) fusion(f32[32,4,4096]{2,1,0:T(4,128)S(1)} %copy-done, f32[32,1,4096]{2,1,0:T(1,128)S(1)} %get-tuple-element.14, f32[32,1,4096]{2,1,0:T(1,128)S(1)} %get-tuple-element.15, f32[32,1,4096]{2,1,0:T(1,128)S(1)} %get-tuple-element.11, f32[32,1,4096]{2,1,0:T(1,128)S(1)} %broadcast.24, ...), kind=kLoop, calls=%fused_computation.4 | loop fusion | flops 7323648 | bytes 10027040 | tf_op jit(solution)/shard_map/reduce_sum | solution.py:40
  12.2 14.9 %all_to_all.20 = f32[16,4,256]{2,1,0:T(4,128)S(1)} all-to-all(f32[16,4,256]{2,1,0:T(4,128)S(1)} %bitcast.129), channel_id=1, replica_groups=mesh['light'=16,'vz'=8,'vx'=4] {'light'}, dimensions={0} | all-to-all | bytes 131072 | tf_op jit(solution)/shard_map/all_to_all | solution.py:14
  27.1 10.4 %all_to_all.21 = f32[16,4,256]{2,1,0:T(4,128)S(1)} all-to-all(f32[16,4,256]{2,1,0:T(4,128)S(1)} %concatenate.4), channel_id=1, replica_groups=mesh['light'=16,'vz'=8,'vx'=4] {'light'}, dimensions={0} | all-to-all | bytes 131072 | tf_op jit(solution)/shard_map/all_to_all | solution.py:17
  37.5 3.6 %fusion.15 = (f32[32,4096]{1,0:T(8,128)S(1)}, f32[32,4096]{1,0:T(8,128)S(1)}) fusion(f32[32,4,4096]{2,1,0:T(4,128)S(1)} %get-tuple-element.10, f32[4,4096]{1,0:T(4,128)S(1)} %bitcast.130, f32[32,4,4096]{2,1,0:T(4,128)S(1)} %copy-done), kind=kOutput, calls=%fused_computation.55 | output fusion | flops 20185088 | bytes 5308416 | tf_op jit(solution)/shard_map/jit(cumsum)/reduce_window_sum | solution.py:44
  41.1 0.1 multiply_add_fusion
  41.1 0.4 add.119
  41.5 0.3 maximum_bitcast_fusion
  41.8 0.1 copy.38
  41.8 18.8 %all_to_all.22 = f32[4,2,32,8,128]{4,3,2,1,0:T(8,128)S(1)} all-to-all(f32[4,2,32,8,128]{4,3,2,1,0:T(8,128)S(1)} %copy.38), channel_id=1, replica_groups=mesh['light'=16,'vz'=8,'vx'=4] {'vx'}, dimensions={0} | all-to-all | bytes 2097152 | tf_op jit(solution)/shard_map/all_to_all | solution.py:63
  60.7 0.1 fusion.6
  60.8 0.1 copy.39
  60.9 21.4 %all_to_all.23 = f32[8,2,32,128]{3,2,1,0:T(8,128)S(1)} all-to-all(f32[8,2,32,128]{3,2,1,0:T(8,128)S(1)} %copy.39), channel_id=1, replica_groups=mesh['light'=16,'vz'=8,'vx'=4] {'vz'}, dimensions={0} | all-to-all | bytes 524288 | tf_op jit(solution)/shard_map/all_to_all | solution.py:67
  82.3 0.7 fusion.11
  82.9 0.6 slice_reduce_fusion.1
  (6 shorter events, 0.1 us)
Async XLA Ops:
  3.6 3.4 %copy-start = (f32[32,4,4096]{2,1,0:T(4,128)S(1)}, f32[32,4,4096]{2,1,0:T(4,128)}, u32[]{:S(2)}) copy-start(f32[32,4,4096]{2,1,0:T(4,128)} %param.3) | copy-start | bytes 6291460
  3.6 3.4 %copy-start.1 = (f32[32,4,4096]{2,1,0:T(4,128)S(1)}, f32[32,4,4096]{2,1,0:T(4,128)}, u32[]{:S(2)}) copy-start(f32[32,4,4096]{2,1,0:T(4,128)} %param.4) | copy-start | bytes 6291460

commit v4 on v3

--- a/solution.py
+++ b/solution.py
@@ -1,6 +1,8 @@
 import jax
 import jax.numpy as jnp
 from jax import lax
+from jax.experimental import pallas as pl
+from jax.experimental.pallas import tpu as pltpu
 from jax.sharding import Mesh
 from jax.sharding import PartitionSpec as P
 
@@ -16,6 +18,57 @@
     before = jnp.concatenate([jnp.zeros_like(running[:1]), running[:-1]], axis=0)
     back = lax.all_to_all(before, "light", 0, 0)
     return back.transpose(1, 0, 2).reshape(cells, columns)
+
+
+def shade_kernel(facing_ref, incoming_ref, dens_ref, emit_ref, color_ref, trans_ref, *, light_scale, view_scale):
+    rows, cells, _ = dens_ref.shape
+
+    def row(l, depth):
+        dens = dens_ref[l]
+        emit = emit_ref[l]
+        tau_light = dens * light_scale
+        step = jnp.exp(-(dens * view_scale))
+        lit = emit * (0.2 + jnp.exp(-depth)) * (1.0 - step)
+        s = [step[v:v + 1] for v in range(cells)]
+        c = [lit[v:v + 1] for v in range(cells)]
+        forward = c[cells - 1]
+        for v in range(cells - 2, -1, -1):
+            forward = c[v] + s[v] * forward
+        backward = c[0]
+        for v in range(1, cells):
+            backward = c[v] + s[v] * backward
+        trans = s[0]
+        for v in range(1, cells):
+            trans = trans * s[v]
+        color_ref[pl.ds(l, 1), :] = jnp.where(facing_ref[l] == 1, backward, forward)
+        trans_ref[pl.ds(l, 1), :] = trans
+        return depth + tau_light
+
+    lax.fori_loop(0, rows, row, incoming_ref[...], unroll=8)
+
+
+def shade(facing, incoming, density, emission, light_scale, view_scale, tile=512):
+    rows, cells, columns = density.shape
+    tile = min(tile, columns)
+    body = lambda *refs: shade_kernel(*refs, light_scale=light_scale, view_scale=view_scale)
+    return pl.pallas_call(
+        body,
+        grid=(columns // tile,),
+        in_specs=[
+            pl.BlockSpec(memory_space=pltpu.SMEM),
+            pl.BlockSpec((cells, tile), lambda j: (0, j)),
+            pl.BlockSpec((rows, cells, tile), lambda j: (0, 0, j)),
+            pl.BlockSpec((rows, cells, tile), lambda j: (0, 0, j)),
+        ],
+        out_specs=[
+            pl.BlockSpec((rows, tile), lambda j: (0, j)),
+            pl.BlockSpec((rows, tile), lambda j: (0, j)),
+        ],
+        out_shape=[jax.ShapeDtypeStruct((rows, columns), jnp.float32)] * 2,
+        cost_estimate=pl.CostEstimate(
+            flops=30 * density.size, transcendentals=2 * density.size, bytes_accessed=2 * 4 * density.size + 8 * rows * columns
+        ),
+    )(facing, incoming, density, emission)
 
 
 def composite(colors, transes, reversed_rows):
@@ -36,29 +89,12 @@
     x_count = lax.axis_size("vx")
     view_count = z_count * x_count
     tau_light = density * (1.0 / (rows * light_count))
-    tau_view = density * (1.0 / (cells * view_count))
     slab_depth = jnp.sum(tau_light, axis=0)
     incoming = light_prefix(slab_depth)
 
     reversed_rows = facing == 1
-    local_depth = jnp.cumsum(tau_light, axis=0) - tau_light
-    shade = jnp.exp(-local_depth)
-    step = jnp.exp(-tau_view)
-    forward_w = [jnp.ones_like(step[:, 0])]
-    for v in range(1, cells):
-        forward_w.append(forward_w[-1] * step[:, v - 1])
-    backward_w = [jnp.ones_like(step[:, 0])]
-    for v in range(cells - 2, -1, -1):
-        backward_w.insert(0, backward_w[0] * step[:, v + 1])
-    trans = forward_w[-1] * step[:, cells - 1]
-    weight = jnp.where(reversed_rows[:, None, None], jnp.stack(backward_w, 1), jnp.stack(forward_w, 1))
-    base = emission * (1.0 - step) * weight
-    flat = jnp.sum(base, axis=1)
-    lit_part = base * shade
-
     width = columns // view_count
-    light = jnp.exp(-incoming)
-    color = 0.2 * flat + jnp.sum(lit_part * light[None], axis=1)
+    color, trans = shade(facing, incoming, density, emission, 1.0 / (rows * light_count), 1.0 / (cells * view_count))
     stacked = jnp.stack([color, trans]).reshape(2, rows, z_count, x_count, width).transpose(3, 0, 1, 2, 4)
     along_x = lax.all_to_all(stacked, "vx", 0, 0)
     color_x = composite(along_x[:, 0], along_x[:, 1], reversed_rows[:, None, None])

time: 83.8 us -> 82 us (0.979)
  blocking collectives: 65.4 us -> 47 us
  waiting for transfers between devices: 0 us -> 14.4 us
  other arithmetic: 16.4 us -> 4.6 us
  Pallas kernels: 0 us -> 7.43 us
  starting transfers between devices: 0 us -> 4.91 us
  local copies, waits for them, and re-layouts: 0.97 us -> 2.45 us
    all_to_all x1 -> x0, blocking collectives: 18.8 us -> none  [shards(): along_x = lax.all_to_all(stacked, 'vx', 0, 0)]
    all_to_all x0 -> x1, waiting for transfers between devices: none -> 14.4 us  [shards(): along_x = lax.all_to_all(stacked, 'vx', 0, 0)]
    pallas_call x0 -> x1, Pallas kernels: none -> 7.43 us  [shade(): pl.pallas_call(body, grid=(columns // tile,), in_specs=[pl.BlockSpec(memo...]
    all_to_all x0 -> x1, starting transfers between devices: none -> 4.91 us  [shards(): along_x = lax.all_to_all(stacked, 'vx', 0, 0)]
    another operation x1 -> x0, other arithmetic: 3.57 us -> none  [shards(): local_depth = jnp.cumsum(tau_light, axis=0) - tau_light]
    reduce_sum x1, other arithmetic: 5.08 us -> 2.04 us  [shards(): slab_depth = jnp.sum(tau_light, axis=0)]
    mul x1 -> x0, other arithmetic: 2.93 us -> none  [shards(): backward_w.insert(0, backward_w[0] * step[:, v + 1])]
    exp x2 -> x0, other arithmetic: 2.33 us -> none  [the longest x1 2.31 us: shards(): step = jnp.exp(-tau_view)]
  transfers between devices with their start and end apart: 0 -> 1, of which waited for: 0 -> 1; matrix products, arithmetic and copies ran while one was open for 0% -> 0% of each run, Pallas kernels for 0% -> 0%
where the time goes in v4:
time: 82 us; the launch traced here: 81.5 us
  blocking collectives  47 us (57%)
  waiting for transfers between devices  14.4 us (18%)
  Pallas kernels  7.43 us (9%)
  starting transfers between devices  4.91 us (6%)
  other arithmetic  4.6 us (6%)
  local copies, waits for them, and re-layouts  2.45 us (3%)
    all_to_all x1, blocking collectives, shards(): along_z = lax.all_to_all(stacked, 'vz', 0, 0)  21 us
    all_to_all x1, blocking collectives, light_prefix(): mine = lax.all_to_all(chunks, 'light', 0, 0)  14.9 us
    all_to_all x1, waiting for transfers between devices, shards(): along_x = lax.all_to_all(stacked, 'vx', 0, 0)  14.4 us
    all_to_all x1, blocking collectives, light_prefix(): back = lax.all_to_all(before, 'light', 0, 0)  11.1 us
    pallas_call x1, Pallas kernels, shade(): pl.pallas_call(body, grid=(columns // tile,), in_specs=[pl.BlockSpec(memo...  7.43 us
    all_to_all x1, starting transfers between devices, shards(): along_x = lax.all_to_all(stacked, 'vx', 0, 0)  4.91 us
    another operation x4, local copies, waits for them, and re-layouts, shards(): jnp.stack([color, trans]).reshape(2, rows, z_count, x_count, width)  2.42 us
    reduce_sum x1, other arithmetic, shards(): slab_depth = jnp.sum(tau_light, axis=0)  2.04 us
  transfers between devices with their start and end apart: 1, of which 1 were waited for; matrix products, arithmetic and copies ran while one was open for 0% of the time, Pallas kernels for 0%

profile of v4, /device:TPU:2, one launch (start us, length us, event | category | flops | bytes accessed | tf_op | source)
XLA Modules:
  0.0 81.5 jit_solution(10819546656132053582)
XLA Ops:
  0.6 2.0 %multiply_reduce_fusion = f32[4,4096]{1,0:T(4,128)S(1)} fusion(f32[32,4,4096]{2,1,0:T(4,128)} %refs_2_.1), kind=kLoop, calls=%fused_computation | loop fusion | flops 1032192 | bytes 2162688 | tf_op jit(solution)/shard_map/reduce_sum | solution.py:92
  2.7 14.9 %all_to_all.20 = f32[16,4,256]{2,1,0:T(4,128)S(1)} all-to-all(f32[16,4,256]{2,1,0:T(4,128)S(1)} %bitcast.138), channel_id=1, replica_groups=mesh['light'=16,'vz'=8,'vx'=4] {'light'}, dimensions={0} | all-to-all | bytes 131072 | tf_op jit(solution)/shard_map/all_to_all | solution.py:16
  17.6 11.1 %all_to_all.21 = f32[16,4,256]{2,1,0:T(4,128)} all-to-all(f32[16,4,256]{2,1,0:T(4,128)S(1)} %concatenate.4), channel_id=1, replica_groups=mesh['light'=16,'vz'=8,'vx'=4] {'light'}, dimensions={0} | all-to-all | bytes 131072 | tf_op jit(solution)/shard_map/all_to_all | solution.py:19
  28.7 7.4 %shard_map.50 = (f32[32,4096]{1,0:T(8,128)}, f32[32,4096]{1,0:T(8,128)}) custom-call(s32[32]{0:T(128)} %refs_0_.1, f32[4,4096]{1,0:T(4,128)} %bitcast.137, f32[32,4,4096]{2,1,0:T(4,128)} %refs_2_.1, f32[32,4,4096]{2,1,0:T(4,128)} %refs_3_.1), custom_call_target="tpu_custom_call" | custom-call | flops 15728640 | bytes 5242880 | tf_op jit(solution)/shard_map/pallas_call | solution.py:54
  36.1 0.0 copy-start
  36.1 1.4 %stack.16 = f32[1,32,8,4,128]{4,3,2,1,0:T(4,128)S(1)} reshape(f32[32,4096]{1,0:T(8,128)} %get-tuple-element.4) | data formatting | bytes 1048576 | tf_op jit(solution)/shard_map/stack | solution.py:98
  37.5 0.3 copy.5
  37.9 0.0 copy-done
  37.9 0.4 stack.17
  38.2 0.3 copy.6
  38.5 0.0 copy-start.1
  38.6 1.1 %maximum_bitcast_fusion = f32[4,2,32,8,128]{4,2,3,1,0:T(8,128)} fusion(f32[1,32,8,4,128]{4,1,2,0,3:T(8,128)S(1)} %copy.6, f32[1,32,8,4,128]{4,1,2,0,3:T(8,128)S(1)} %copy.5), kind=kLoop, calls=%fused_computation.1 | loop fusion | flops 262144 | bytes 2097152 | tf_op jit(solution)/shard_map/transpose | solution.py:98
  39.6 4.9 %all-to-all-start.2 = ((f32[4,2,32,8,128]{4,2,3,1,0:T(8,128)}), f32[4,2,32,8,128]{4,2,3,1,0:T(8,128)S(1)}, u32[]{:S(2)}, u32[]{:S(2)}) async-start(f32[4,2,32,8,128]{4,2,3,1,0:T(8,128)} %maximum_bitcast_fusion), calls=%async_computation.2 | async-start | bytes 2097152 | tf_op jit(solution)/shard_map/all_to_all | solution.py:99
  44.6 0.0 copy-done.1
  44.6 14.4 %all-to-all-done.2 = f32[4,2,32,8,128]{4,2,3,1,0:T(8,128)S(1)} async-done(((f32[4,2,32,8,128]{4,2,3,1,0:T(8,128)}), f32[4,2,32,8,128]{4,2,3,1,0:T(8,128)S(1)}, u32[]{:S(2)}, u32[]{:S(2)}) %all-to-all-start.2) | async-done | bytes 1048608 | tf_op jit(solution)/shard_map/all_to_all | solution.py:99
  59.0 0.1 fusion.2
  59.2 21.0 %all_to_all.22 = f32[8,2,32,128]{3,2,1,0:T(8,128)S(1)} all-to-all(f32[8,2,32,128]{3,2,1,0:T(8,128)S(1)} %maximum_bitcast_fusion.1), channel_id=1, replica_groups=mesh['light'=16,'vz'=8,'vx'=4] {'vz'}, dimensions={0} | all-to-all | bytes 524288 | tf_op jit(solution)/shard_map/all_to_all | solution.py:103
  80.2 0.7 fusion.7
  80.9 0.6 slice_reduce_fusion.1
  (6 shorter events, 0.1 us)
Async XLA Ops:
  36.1 1.8 %copy-start = (f32[32,4096]{1,0:T(8,128)S(1)}, f32[32,4096]{1,0:T(8,128)}, u32[]{:S(2)}) copy-start(f32[32,4096]{1,0:T(8,128)} %get-tuple-element.5) | copy-start | bytes 1572868
  38.5 6.0 %copy-start.1 = (s32[32]{0:T(128)S(1)}, s32[32]{0:T(128)}, u32[]{:S(2)}) copy-start(s32[32]{0:T(128)} %refs_0_.1) | copy-start | bytes 388
  39.6 19.3 %all-to-all-start.2 = ((f32[4,2,32,8,128]{4,2,3,1,0:T(8,128)}), f32[4,2,32,8,128]{4,2,3,1,0:T(8,128)S(1)}, u32[]{:S(2)}, u32[]{:S(2)}) async-start(f32[4,2,32,8,128]{4,2,3,1,0:T(8,128)} %maximum_bitcast_fusion), calls=%async_computation.2 | async-start | bytes 2097152 | tf_op jit(solution)/shard_map/all_to_all | solution.py:99

commit v5 on v4

--- a/solution.py
+++ b/solution.py
@@ -20,8 +20,9 @@
     return back.transpose(1, 0, 2).reshape(cells, columns)
 
 
-def shade_kernel(facing_ref, incoming_ref, dens_ref, emit_ref, color_ref, trans_ref, *, light_scale, view_scale):
+def shade_kernel(facing_ref, incoming_ref, dens_ref, emit_ref, out_ref, *, light_scale, view_scale):
     rows, cells, _ = dens_ref.shape
+    blocks, width = out_ref.shape[0], out_ref.shape[-1]
 
     def row(l, depth):
         dens = dens_ref[l]
@@ -40,31 +41,31 @@
         trans = s[0]
         for v in range(1, cells):
             trans = trans * s[v]
-        color_ref[pl.ds(l, 1), :] = jnp.where(facing_ref[l] == 1, backward, forward)
-        trans_ref[pl.ds(l, 1), :] = trans
+        color = jnp.where(facing_ref[l] == 1, backward, forward)
+        for b in range(blocks):
+            out_ref[b, 0, 0, pl.ds(l, 1), :] = color[:, b * width:(b + 1) * width]
+            out_ref[b, 1, 0, pl.ds(l, 1), :] = trans[:, b * width:(b + 1) * width]
         return depth + tau_light
 
     lax.fori_loop(0, rows, row, incoming_ref[...], unroll=8)
 
 
-def shade(facing, incoming, density, emission, light_scale, view_scale, tile=512):
+def shade(facing, incoming, density, emission, light_scale, view_scale, blocks, width):
     rows, cells, columns = density.shape
-    tile = min(tile, columns)
+    tile = blocks * width
+    tiles = columns // tile
     body = lambda *refs: shade_kernel(*refs, light_scale=light_scale, view_scale=view_scale)
     return pl.pallas_call(
         body,
-        grid=(columns // tile,),
+        grid=(tiles,),
         in_specs=[
             pl.BlockSpec(memory_space=pltpu.SMEM),
             pl.BlockSpec((cells, tile), lambda j: (0, j)),
             pl.BlockSpec((rows, cells, tile), lambda j: (0, 0, j)),
             pl.BlockSpec((rows, cells, tile), lambda j: (0, 0, j)),
         ],
-        out_specs=[
-            pl.BlockSpec((rows, tile), lambda j: (0, j)),
-            pl.BlockSpec((rows, tile), lambda j: (0, j)),
-        ],
-        out_shape=[jax.ShapeDtypeStruct((rows, columns), jnp.float32)] * 2,
+        out_specs=pl.BlockSpec((blocks, 2, 1, rows, width), lambda j: (0, 0, j, 0, 0)),
+        out_shape=jax.ShapeDtypeStruct((blocks, 2, tiles, rows, width), jnp.float32),
         cost_estimate=pl.CostEstimate(
             flops=30 * density.size, transcendentals=2 * density.size, bytes_accessed=2 * 4 * density.size + 8 * rows * columns
         ),
@@ -94,13 +95,13 @@
 
     reversed_rows = facing == 1
     width = columns // view_count
-    color, trans = shade(facing, incoming, density, emission, 1.0 / (rows * light_count), 1.0 / (cells * view_count))
-    stacked = jnp.stack([color, trans]).reshape(2, rows, z_count, x_count, width).transpose(3, 0, 1, 2, 4)
+    stacked = shade(
+        facing, incoming, density, emission, 1.0 / (rows * light_count), 1.0 / (cells * view_count), x_count, width
+    )
     along_x = lax.all_to_all(stacked, "vx", 0, 0)
-    color_x = composite(along_x[:, 0], along_x[:, 1], reversed_rows[:, None, None])
+    color_x = composite(along_x[:, 0], along_x[:, 1], reversed_rows[None, :, None])
     trans_x = jnp.prod(along_x[:, 1], axis=0)
-    stacked = jnp.stack([color_x, trans_x]).transpose(2, 0, 1, 3)
-    along_z = lax.all_to_all(stacked, "vz", 0, 0)
+    along_z = lax.all_to_all(jnp.stack([color_x, trans_x], axis=1), "vz", 0, 0)
     radiance = composite(along_z[:, 0], along_z[:, 1], reversed_rows[:, None])
     coverage = jnp.prod(along_z[:, 1], axis=0)
     return (radiance, coverage)

time: 82 us -> 78.4 us (0.956)
  the two profiles are of different devices: /device:TPU:2 before, /device:TPU:8 now
where the time goes in v5:
time: 78.4 us; the launch traced here: 77.7 us
  blocking collectives  46.8 us (60%)
  waiting for transfers between devices  15.7 us (20%)
  Pallas kernels  7.42 us (9%)
  other arithmetic  3.52 us (4%)
  starting transfers between devices  3.51 us (4%)
    all_to_all x1, blocking collectives, shards(): along_z = lax.all_to_all(jnp.stack([color_x, trans_x], axis=1), 'vz', 0, 0)  20.9 us
    all_to_all x1, waiting for transfers between devices, shards(): along_x = lax.all_to_all(stacked, 'vx', 0, 0)  15.7 us
    all_to_all x1, blocking collectives, light_prefix(): mine = lax.all_to_all(chunks, 'light', 0, 0)  14.8 us
    all_to_all x1, blocking collectives, light_prefix(): back = lax.all_to_all(before, 'light', 0, 0)  11.1 us
    pallas_call x1, Pallas kernels, shade(): pl.pallas_call(body, grid=(tiles,), in_specs=[pl.BlockSpec(memory_space=p...  7.42 us
    all_to_all x1, starting transfers between devices, shards(): along_x = lax.all_to_all(stacked, 'vx', 0, 0)  3.51 us
    reduce_sum x1, other arithmetic, shards(): slab_depth = jnp.sum(tau_light, axis=0)  2.04 us
  transfers between devices with their start and end apart: 1, of which 1 were waited for; matrix products, arithmetic and copies ran while one was open for 0% of the time, Pallas kernels for 0%

profile of v5, /device:TPU:8, one launch (start us, length us, event | category | flops | bytes accessed | tf_op | source)
XLA Modules:
  0.0 77.7 jit_solution(14471367200281564213)
XLA Ops:
  0.6 2.0 %multiply_reduce_fusion = f32[4,4096]{1,0:T(4,128)S(1)} fusion(f32[32,4,4096]{2,1,0:T(4,128)} %refs_2_.1), kind=kLoop, calls=%fused_computation | loop fusion | flops 1032192 | bytes 2162688 | tf_op jit(solution)/shard_map/reduce_sum | solution.py:93
  2.7 14.8 %all_to_all.20 = f32[16,4,256]{2,1,0:T(4,128)S(1)} all-to-all(f32[16,4,256]{2,1,0:T(4,128)S(1)} %bitcast.122), channel_id=1, replica_groups=mesh['light'=16,'vz'=8,'vx'=4] {'light'}, dimensions={0} | all-to-all | bytes 131072 | tf_op jit(solution)/shard_map/all_to_all | solution.py:16
  17.6 11.1 %all_to_all.21 = f32[16,4,256]{2,1,0:T(4,128)} all-to-all(f32[16,4,256]{2,1,0:T(4,128)S(1)} %concatenate.3), channel_id=1, replica_groups=mesh['light'=16,'vz'=8,'vx'=4] {'light'}, dimensions={0} | all-to-all | bytes 131072 | tf_op jit(solution)/shard_map/all_to_all | solution.py:19
  28.6 0.0 copy-start
  28.6 7.4 %shard_map.50 = f32[4,2,8,32,128]{4,3,2,1,0:T(8,128)} custom-call(s32[32]{0:T(128)} %refs_0_.1, f32[4,4096]{1,0:T(4,128)} %bitcast.121, f32[32,4,4096]{2,1,0:T(4,128)} %refs_2_.1, f32[32,4,4096]{2,1,0:T(4,128)} %refs_3_.1), custom_call_target="tpu_custom_call" | custom-call | flops 15728640 | bytes 5242880 | tf_op jit(solution)/shard_map/pallas_call | solution.py:58
  36.0 3.5 %all-to-all-start.2 = ((f32[4,2,8,32,128]{4,3,2,1,0:T(8,128)}), f32[4,2,8,32,128]{4,3,2,1,0:T(8,128)S(1)}, u32[]{:S(2)}, u32[]{:S(2)}) async-start(f32[4,2,8,32,128]{4,3,2,1,0:T(8,128)} %shard_map.50), calls=%async_computation.2 | async-start | bytes 2097152 | tf_op jit(solution)/shard_map/all_to_all | solution.py:101
  39.6 0.0 copy-done
  39.6 15.7 %all-to-all-done.2 = f32[4,2,8,32,128]{4,3,2,1,0:T(8,128)S(1)} async-done(((f32[4,2,8,32,128]{4,3,2,1,0:T(8,128)}), f32[4,2,8,32,128]{4,3,2,1,0:T(8,128)S(1)}, u32[]{:S(2)}, u32[]{:S(2)}) %all-to-all-start.2) | async-done | bytes 1048608 | tf_op jit(solution)/shard_map/all_to_all | solution.py:101
  55.3 0.1 fusion.2
  55.5 20.9 %all_to_all.22 = f32[8,2,32,128]{3,2,1,0:T(8,128)S(1)} all-to-all(f32[8,2,32,128]{3,2,1,0:T(8,128)S(1)} %copy.20), channel_id=1, replica_groups=mesh['light'=16,'vz'=8,'vx'=4] {'vz'}, dimensions={0} | all-to-all | bytes 524288 | tf_op jit(solution)/shard_map/all_to_all | solution.py:104
  76.4 0.7 fusion.7
  77.1 0.6 slice_reduce_fusion.1
  (7 shorter events, 0.1 us)
Async XLA Ops:
  28.6 10.9 %copy-start = (s32[32]{0:T(128)S(1)}, s32[32]{0:T(128)}, u32[]{:S(2)}) copy-start(s32[32]{0:T(128)} %refs_0_.1) | copy-start | bytes 388
  36.0 19.2 %all-to-all-start.2 = ((f32[4,2,8,32,128]{4,3,2,1,0:T(8,128)}), f32[4,2,8,32,128]{4,3,2,1,0:T(8,128)S(1)}, u32[]{:S(2)}, u32[]{:S(2)}) async-start(f32[4,2,8,32,128]{4,3,2,1,0:T(8,128)} %shard_map.50), calls=%async_computation.2 | async-start | bytes 2097152 | tf_op jit(solution)/shard_map/all_to_all | solution.py:101

commit v6 on v5

--- a/solution.py
+++ b/solution.py
@@ -38,13 +38,9 @@
         backward = c[0]
         for v in range(1, cells):
             backward = c[v] + s[v] * backward
-        trans = s[0]
-        for v in range(1, cells):
-            trans = trans * s[v]
         color = jnp.where(facing_ref[l] == 1, backward, forward)
         for b in range(blocks):
-            out_ref[b, 0, 0, pl.ds(l, 1), :] = color[:, b * width:(b + 1) * width]
-            out_ref[b, 1, 0, pl.ds(l, 1), :] = trans[:, b * width:(b + 1) * width]
+            out_ref[b, 0, pl.ds(l, 1), :] = color[:, b * width:(b + 1) * width]
         return depth + tau_light
 
     lax.fori_loop(0, rows, row, incoming_ref[...], unroll=8)
@@ -64,8 +60,8 @@
             pl.BlockSpec((rows, cells, tile), lambda j: (0, 0, j)),
             pl.BlockSpec((rows, cells, tile), lambda j: (0, 0, j)),
         ],
-        out_specs=pl.BlockSpec((blocks, 2, 1, rows, width), lambda j: (0, 0, j, 0, 0)),
-        out_shape=jax.ShapeDtypeStruct((blocks, 2, tiles, rows, width), jnp.float32),
+        out_specs=pl.BlockSpec((blocks, 1, rows, width), lambda j: (0, j, 0, 0)),
+        out_shape=jax.ShapeDtypeStruct((blocks, tiles, rows, width), jnp.float32),
         cost_estimate=pl.CostEstimate(
             flops=30 * density.size, transcendentals=2 * density.size, bytes_accessed=2 * 4 * density.size + 8 * rows * columns
         ),
@@ -91,17 +87,20 @@
     view_count = z_count * x_count
     tau_light = density * (1.0 / (rows * light_count))
     slab_depth = jnp.sum(tau_light, axis=0)
+    width = columns // view_count
+    trans = jnp.exp(-jnp.sum(density * (1.0 / (cells * view_count)), axis=1))
+    trans_blocks = trans.reshape(rows, z_count, x_count, width).transpose(2, 1, 0, 3)
+    trans_x = lax.all_to_all(trans_blocks, "vx", 0, 0)
     incoming = light_prefix(slab_depth)
 
     reversed_rows = facing == 1
-    width = columns // view_count
-    stacked = shade(
+    color = shade(
         facing, incoming, density, emission, 1.0 / (rows * light_count), 1.0 / (cells * view_count), x_count, width
     )
-    along_x = lax.all_to_all(stacked, "vx", 0, 0)
-    color_x = composite(along_x[:, 0], along_x[:, 1], reversed_rows[None, :, None])
-    trans_x = jnp.prod(along_x[:, 1], axis=0)
-    along_z = lax.all_to_all(jnp.stack([color_x, trans_x], axis=1), "vz", 0, 0)
+    color_x = lax.all_to_all(color, "vx", 0, 0)
+    color_xg = composite(color_x, trans_x, reversed_rows[None, :, None])
+    trans_xg = jnp.prod(trans_x, axis=0)
+    along_z = lax.all_to_all(jnp.stack([color_xg, trans_xg], axis=1), "vz", 0, 0)
     radiance = composite(along_z[:, 0], along_z[:, 1], reversed_rows[:, None])
     coverage = jnp.prod(along_z[:, 1], axis=0)
     return (radiance, coverage)

time: 78.4 us -> 79.3 us (1.011)
  the two profiles are of different devices: /device:TPU:8 before, /device:TPU:2 now
where the time goes in v6:
time: 79.3 us; the launch traced here: 78.8 us
  blocking collectives  34.8 us (44%)
  waiting for transfers between devices  16 us (20%)
  starting transfers between devices  13.3 us (17%)
  Pallas kernels  7.03 us (9%)
  other arithmetic  4.91 us (6%)
  local copies, waits for them, and re-layouts  2.11 us (3%)
    all_to_all x1, blocking collectives, shards(): lax.all_to_all(jnp.stack([color_xg, trans_xg], axis=1), 'vz', 0, 0)  20 us
    all_to_all x1, blocking collectives, light_prefix(): mine = lax.all_to_all(chunks, 'light', 0, 0)  14.9 us
    all_to_all x1, waiting for transfers between devices, shards(): color_x = lax.all_to_all(color, 'vx', 0, 0)  7.96 us
    pallas_call x1, Pallas kernels, shade(): pl.pallas_call(body, grid=(tiles,), in_specs=[pl.BlockSpec(memory_space=p...  7.03 us
    all_to_all x1, waiting for transfers between devices, light_prefix(): back = lax.all_to_all(before, 'light', 0, 0)  6.22 us
    all_to_all x1, starting transfers between devices, shards(): color_x = lax.all_to_all(color, 'vx', 0, 0)  4.9 us
    all_to_all x1, starting transfers between devices, shards(): trans_x = lax.all_to_all(trans_blocks, 'vx', 0, 0)  4.87 us
    all_to_all x1, starting transfers between devices, light_prefix(): back = lax.all_to_all(before, 'light', 0, 0)  3.5 us
  transfers between devices with their start and end apart: 3, of which 3 were waited for; matrix products, arithmetic and copies ran while one was open for 2% of the time, Pallas kernels for 9%

profile of v6, /device:TPU:2, one launch (start us, length us, event | category | flops | bytes accessed | tf_op | source)
XLA Modules:
  0.0 78.8 jit_solution(10395196741912628216)
XLA Ops:
  0.6 3.3 %multiply_reduce_fusion.1 = (f32[4,4096]{1,0:T(4,128)S(1)}, f32[32,4096]{1,0:T(8,128)S(1)}) fusion(f32[32,4,4096]{2,1,0:T(4,128)} %refs_2_.1), kind=kLoop, calls=%fused_computation.1 | loop fusion | flops 1949696 | bytes 2686976 | tf_op jit(solution)/shard_map/reduce_sum | solution.py:89
  4.0 14.9 %all_to_all.25 = f32[16,4,256]{2,1,0:T(4,128)S(1)} all-to-all(f32[16,4,256]{2,1,0:T(4,128)S(1)} %bitcast.125), channel_id=1, replica_groups=mesh['light'=16,'vz'=8,'vx'=4] {'light'}, dimensions={0} | all-to-all | bytes 131072 | tf_op jit(solution)/shard_map/all_to_all | solution.py:16
  18.9 0.6 concatenate.3
  19.5 3.5 %all-to-all-start.1 = ((f32[16,4,256]{2,1,0:T(4,128)}), f32[16,4,256]{2,1,0:T(4,128)S(1)}, u32[]{:S(2)}, u32[]{:S(2)}) async-start(f32[16,4,256]{2,1,0:T(4,128)} %concatenate.3), calls=%async_computation.1 | async-start | bytes 131072 | tf_op jit(solution)/shard_map/all_to_all | solution.py:19
  23.0 0.1 negate_exponential_fusion
  23.1 0.4 exp.8
  23.5 1.1 %copy.39 = f32[32,8,4,128]{3,0,1,2:T(8,128)} copy(f32[32,8,4,128]{3,2,1,0:T(4,128)S(1)} %exp.8) | data formatting | bytes 1048576 | tf_op jit(solution)/shard_map/exp | solution.py:91
  24.6 6.2 %all-to-all-done.1 = f32[16,4,256]{2,1,0:T(4,128)S(1)} async-done(((f32[16,4,256]{2,1,0:T(4,128)}), f32[16,4,256]{2,1,0:T(4,128)S(1)}, u32[]{:S(2)}, u32[]{:S(2)}) %all-to-all-start.1) | async-done | bytes 65568 | tf_op jit(solution)/shard_map/all_to_all | solution.py:19
  30.8 0.0 copy-start
  30.8 4.9 %all-to-all-start.3 = ((f32[4,8,32,128]{3,2,1,0:T(8,128)}), f32[4,8,32,128]{3,2,1,0:T(8,128)S(1)}, u32[]{:S(2)}, u32[]{:S(2)}) async-start(f32[4,8,32,128]{3,2,1,0:T(8,128)} %bitcast.122), calls=%async_computation.3 | async-start | bytes 1048576 | tf_op jit(solution)/shard_map/all_to_all | solution.py:93
  35.6 0.0 copy-done
  35.6 0.0 copy-start.1
  35.7 7.0 %shard_map.50 = f32[4,8,32,128]{3,2,1,0:T(8,128)} custom-call(s32[32]{0:T(128)} %refs_0_.1, f32[4,4096]{1,0:T(4,128)} %bitcast.124, f32[32,4,4096]{2,1,0:T(4,128)} %refs_2_.1, f32[32,4,4096]{2,1,0:T(4,128)} %refs_3_.1), custom_call_target="tpu_custom_call" | custom-call | flops 15728640 | bytes 5242880 | tf_op jit(solution)/shard_map/pallas_call | solution.py:54
  42.7 1.8 %all-to-all-done.3 = f32[4,8,32,128]{3,2,1,0:T(8,128)S(1)} async-done(((f32[4,8,32,128]{3,2,1,0:T(8,128)}), f32[4,8,32,128]{3,2,1,0:T(8,128)S(1)}, u32[]{:S(2)}, u32[]{:S(2)}) %all-to-all-start.3) | async-done | bytes 524320 | tf_op jit(solution)/shard_map/all_to_all | solution.py:93
  44.5 4.9 %all-to-all-start.2 = ((f32[4,8,32,128]{3,2,1,0:T(8,128)}), f32[4,8,32,128]{3,2,1,0:T(8,128)S(1)}, u32[]{:S(2)}, u32[]{:S(2)}) async-start(f32[4,8,32,128]{3,2,1,0:T(8,128)} %shard_map.50), calls=%async_computation.2 | async-start | bytes 1048576 | tf_op jit(solution)/shard_map/all_to_all | solution.py:100
  49.4 0.0 copy-done.1
  49.4 8.0 %all-to-all-done.2 = f32[4,8,32,128]{3,2,1,0:T(8,128)S(1)} async-done(((f32[4,8,32,128]{3,2,1,0:T(8,128)}), f32[4,8,32,128]{3,2,1,0:T(8,128)S(1)}, u32[]{:S(2)}, u32[]{:S(2)}) %all-to-all-start.2) | async-done | bytes 524320 | tf_op jit(solution)/shard_map/all_to_all | solution.py:100
  57.4 0.1 fusion.2
  57.5 20.0 %all_to_all.26 = f32[8,2,32,128]{3,2,1,0:T(8,128)S(1)} all-to-all(f32[8,2,32,128]{3,2,1,0:T(8,128)S(1)} %copy.37), channel_id=1, replica_groups=mesh['light'=16,'vz'=8,'vx'=4] {'vz'}, dimensions={0} | all-to-all | bytes 524288 | tf_op jit(solution)/shard_map/all_to_all | solution.py:103
  77.5 0.7 fusion.7
  78.2 0.6 slice_reduce_fusion
  (6 shorter events, 0.1 us)
Async XLA Ops:
  19.5 11.3 %all-to-all-start.1 = ((f32[16,4,256]{2,1,0:T(4,128)}), f32[16,4,256]{2,1,0:T(4,128)S(1)}, u32[]{:S(2)}, u32[]{:S(2)}) async-start(f32[16,4,256]{2,1,0:T(4,128)} %concatenate.3), calls=%async_computation.1 | async-start | bytes 131072 | tf_op jit(solution)/shard_map/all_to_all | solution.py:19
  30.8 4.9 %copy-start = (f32[16,4,256]{2,1,0:T(4,128)}, f32[16,4,256]{2,1,0:T(4,128)S(1)}, u32[]{:S(2)}) copy-start(f32[16,4,256]{2,1,0:T(4,128)S(1)} %all-to-all-done.1) | copy-start | bytes 196612
  30.8 13.7 %all-to-all-start.3 = ((f32[4,8,32,128]{3,2,1,0:T(8,128)}), f32[4,8,32,128]{3,2,1,0:T(8,128)S(1)}, u32[]{:S(2)}, u32[]{:S(2)}) async-start(f32[4,8,32,128]{3,2,1,0:T(8,128)} %bitcast.122), calls=%async_computation.3 | async-start | bytes 1048576 | tf_op jit(solution)/shard_map/all_to_all | solution.py:93
  35.6 13.7 %copy-start.1 = (s32[32]{0:T(128)S(1)}, s32[32]{0:T(128)}, u32[]{:S(2)}) copy-start(s32[32]{0:T(128)} %refs_0_.1) | copy-start | bytes 388
  44.5 12.9 %all-to-all-start.2 = ((f32[4,8,32,128]{3,2,1,0:T(8,128)}), f32[4,8,32,128]{3,2,1,0:T(8,128)S(1)}, u32[]{:S(2)}, u32[]{:S(2)}) async-start(f32[4,8,32,128]{3,2,1,0:T(8,128)} %shard_map.50), calls=%async_computation.2 | async-start | bytes 1048576 | tf_op jit(solution)/shard_map/all_to_all | solution.py:100

commit v7 on v5

--- a/solution.py
+++ b/solution.py
@@ -83,6 +83,25 @@
     return jnp.where(reversed_rows, backward, forward)
 
 
+def halving(stacked, axis, reversed_rows):
+    count = lax.axis_size(axis)
+    mine = lax.axis_index(axis)
+    bit = 0
+    while (1 << bit) < count:
+        _, blocks, rows, width = stacked.shape
+        paired = stacked.reshape(2, blocks // 2, 2, rows, width)
+        my_bit = mine >> bit & 1
+        keep = jnp.where(my_bit == 1, paired[:, :, 1], paired[:, :, 0])
+        send = jnp.where(my_bit == 1, paired[:, :, 0], paired[:, :, 1])
+        got = lax.ppermute(send, axis, [(i, i ^ (1 << bit)) for i in range(count)])
+        in_front = ((my_bit == 0) == jnp.logical_not(reversed_rows))[None, :, None]
+        front = jnp.where(in_front, keep, got)
+        back = jnp.where(in_front, got, keep)
+        stacked = jnp.stack([front[0] + front[1] * back[0], front[1] * back[1]])
+        bit += 1
+    return stacked[0, 0], stacked[1, 0]
+
+
 def shards(density, emission, facing):
     rows, cells, columns = density.shape
     light_count = lax.axis_size("light")
@@ -101,9 +120,7 @@
     along_x = lax.all_to_all(stacked, "vx", 0, 0)
     color_x = composite(along_x[:, 0], along_x[:, 1], reversed_rows[None, :, None])
     trans_x = jnp.prod(along_x[:, 1], axis=0)
-    along_z = lax.all_to_all(jnp.stack([color_x, trans_x], axis=1), "vz", 0, 0)
-    radiance = composite(along_z[:, 0], along_z[:, 1], reversed_rows[:, None])
-    coverage = jnp.prod(along_z[:, 1], axis=0)
+    radiance, coverage = halving(jnp.stack([color_x, trans_x]), "vz", reversed_rows)
     return (radiance, coverage)
 
 

time: 78.4 us -> 83.8 us (1.069)
  the two profiles are of different devices: /device:TPU:8 before, /device:TPU:64 now
where the time goes in v7:
time: 83.8 us; the launch traced here: 83.3 us
  blocking collectives  25.9 us (31%)
  waiting for transfers between devices  24.6 us (29%)
  starting transfers between devices  21.3 us (25%)
  Pallas kernels  7.43 us (9%)
  other arithmetic  3.16 us (4%)
    ppermute x3, starting transfers between devices, halving(): got = lax.ppermute(send, axis, [(i, i ^ 1 << bit) for i in range(count)])  16.8 us
    all_to_all x1, waiting for transfers between devices, shards(): along_x = lax.all_to_all(stacked, 'vx', 0, 0)  15.6 us
    all_to_all x1, blocking collectives, light_prefix(): mine = lax.all_to_all(chunks, 'light', 0, 0)  14.9 us
    all_to_all x1, blocking collectives, light_prefix(): back = lax.all_to_all(before, 'light', 0, 0)  11.1 us
    ppermute x3, waiting for transfers between devices, halving(): got = lax.ppermute(send, axis, [(i, i ^ 1 << bit) for i in range(count)])  9.04 us
    pallas_call x1, Pallas kernels, shade(): pl.pallas_call(body, grid=(tiles,), in_specs=[pl.BlockSpec(memory_space=p...  7.43 us
    all_to_all x1, starting transfers between devices, shards(): along_x = lax.all_to_all(stacked, 'vx', 0, 0)  4.44 us
    reduce_sum x1, other arithmetic, shards(): slab_depth = jnp.sum(tau_light, axis=0)  2.04 us
  transfers between devices with their start and end apart: 4, of which 4 were waited for; matrix products, arithmetic and copies ran while one was open for 0% of the time, Pallas kernels for 0%

profile of v7, /device:TPU:64, one launch (start us, length us, event | category | flops | bytes accessed | tf_op | source)
XLA Modules:
  0.0 83.3 jit_solution(14153944544573363940)
XLA Ops:
  0.6 2.0 %multiply_reduce_fusion = f32[4,4096]{1,0:T(4,128)S(1)} fusion(f32[32,4,4096]{2,1,0:T(4,128)} %refs_2_.1), kind=kLoop, calls=%fused_computation | loop fusion | flops 1032192 | bytes 2162688 | tf_op jit(solution)/shard_map/reduce_sum | solution.py:112
  2.7 14.9 %all_to_all.15 = f32[16,4,256]{2,1,0:T(4,128)S(1)} all-to-all(f32[16,4,256]{2,1,0:T(4,128)S(1)} %bitcast.117), channel_id=1, replica_groups=mesh['light'=16,'vz'=8,'vx'=4] {'light'}, dimensions={0} | all-to-all | bytes 131072 | tf_op jit(solution)/shard_map/all_to_all | solution.py:16
  17.6 11.1 %all_to_all.16 = f32[16,4,256]{2,1,0:T(4,128)} all-to-all(f32[16,4,256]{2,1,0:T(4,128)S(1)} %concatenate.5), channel_id=1, replica_groups=mesh['light'=16,'vz'=8,'vx'=4] {'light'}, dimensions={0} | all-to-all | bytes 131072 | tf_op jit(solution)/shard_map/all_to_all | solution.py:19
  28.7 7.4 %shard_map.50 = f32[4,2,8,32,128]{4,3,2,1,0:T(8,128)} custom-call(s32[32]{0:T(128)} %refs_0_.1, f32[4,4096]{1,0:T(4,128)} %bitcast.116, f32[32,4,4096]{2,1,0:T(4,128)} %refs_2_.1, f32[32,4,4096]{2,1,0:T(4,128)} %refs_3_.1), custom_call_target="tpu_custom_call" | custom-call | flops 15728640 | bytes 5242880 | tf_op jit(solution)/shard_map/pallas_call | solution.py:58
  36.1 0.0 copy-start
  36.1 4.4 %all-to-all-start.2 = ((f32[4,2,8,32,128]{4,3,2,1,0:T(8,128)}), f32[4,2,8,32,128]{4,3,2,1,0:T(8,128)S(1)}, u32[]{:S(2)}, u32[]{:S(2)}) async-start(f32[4,2,8,32,128]{4,3,2,1,0:T(8,128)} %shard_map.50), calls=%async_computation.2 | async-start | bytes 2097152 | tf_op jit(solution)/shard_map/all_to_all | solution.py:120
  40.5 0.0 copy-done
  40.5 15.6 %all-to-all-done.2 = f32[4,2,8,32,128]{4,3,2,1,0:T(8,128)S(1)} async-done(((f32[4,2,8,32,128]{4,3,2,1,0:T(8,128)}), f32[4,2,8,32,128]{4,3,2,1,0:T(8,128)S(1)}, u32[]{:S(2)}, u32[]{:S(2)}) %all-to-all-start.2) | async-done | bytes 1048608 | tf_op jit(solution)/shard_map/all_to_all | solution.py:120
  56.1 0.1 fusion.10
  56.3 0.1 add_select_fusion
  56.5 1.9 %collective-permute-start = (f32[2,4,32,128]{3,2,1,0:T(8,128)S(1)}, f32[2,4,32,128]{3,2,1,0:T(8,128)S(1)}, u32[]{:S(2)}, u32[]{:S(2)}) collective-permute-start(f32[2,4,32,128]{3,2,1,0:T(8,128)S(1)} %select_bitcast_fusion), channel_id=1, source_target_pairs={{0,4},{4,0},{8,12},{12,8},{16,20},{20,16},{24,28},{28,24},{1,5},{5... | collective-permute-start | bytes 393224 | tf_op jit(solution)/shard_map/ppermute | solution.py:96
  58.4 4.9 %collective-permute-done = f32[2,4,32,128]{3,2,1,0:T(8,128)S(1)} collective-permute-done((f32[2,4,32,128]{3,2,1,0:T(8,128)S(1)}, f32[2,4,32,128]{3,2,1,0:T(8,128)S(1)}, u32[]{:S(2)}, u32[]{:S(2)}) %collective-permute-start) | collective-permute-done | bytes 131104 | tf_op jit(solution)/shard_map/ppermute | solution.py:96
  63.3 0.1 broadcast_select_fusion.1
  63.5 6.1 %collective-permute-start.1 = (f32[2,2,32,128]{3,2,1,0:T(8,128)S(1)}, f32[2,2,32,128]{3,2,1,0:T(8,128)S(1)}, u32[]{:S(2)}, u32[]{:S(2)}) collective-permute-start(f32[2,2,32,128]{3,2,1,0:T(8,128)S(1)} %select_bitcast_fusion.1), channel_id=1, source_target_pairs={{0,8},{4,12},{8,0},{12,4},{16,24},{20,28},{24,16},{28,20},{1,9},{5... | collective-permute-start | bytes 196616 | tf_op jit(solution)/shard_map/ppermute | solution.py:96
  69.6 2.2 %collective-permute-done.1 = f32[2,2,32,128]{3,2,1,0:T(8,128)S(1)} collective-permute-done((f32[2,2,32,128]{3,2,1,0:T(8,128)S(1)}, f32[2,2,32,128]{3,2,1,0:T(8,128)S(1)}, u32[]{:S(2)}, u32[]{:S(2)}) %collective-permute-start.1) | collective-permute-done | bytes 65568 | tf_op jit(solution)/shard_map/ppermute | solution.py:96
  71.8 0.1 broadcast_select_fusion.3
  71.9 8.8 %collective-permute-start.2 = (f32[2,1,32,128]{3,2,0,1:T(8,128)S(1)}, f32[2,1,32,128]{3,2,0,1:T(8,128)S(1)}, u32[]{:S(2)}, u32[]{:S(2)}) collective-permute-start(f32[2,1,32,128]{3,2,0,1:T(8,128)S(1)} %select_bitcast_fusion.2), channel_id=1, source_target_pairs={{0,16},{4,20},{8,24},{12,28},{16,0},{20,4},{24,8},{28,12},{1,17},{... | collective-permute-start | bytes 98312 | tf_op jit(solution)/shard_map/ppermute | solution.py:96
  80.8 1.9 %collective-permute-done.2 = f32[2,1,32,128]{3,2,0,1:T(8,128)S(1)} collective-permute-done((f32[2,1,32,128]{3,2,0,1:T(8,128)S(1)}, f32[2,1,32,128]{3,2,0,1:T(8,128)S(1)}, u32[]{:S(2)}, u32[]{:S(2)}) %collective-permute-start.2) | collective-permute-done | bytes 32800 | tf_op jit(solution)/shard_map/ppermute | solution.py:96
  82.6 0.1 broadcast_select_fusion.5
  82.7 0.6 fusion.7
  (11 shorter events, 0.2 us)
Async XLA Ops:
  36.1 4.4 %copy-start = (s32[32]{0:T(128)S(1)}, s32[32]{0:T(128)}, u32[]{:S(2)}) copy-start(s32[32]{0:T(128)} %refs_0_.1) | copy-start | bytes 388
  36.1 20.0 %all-to-all-start.2 = ((f32[4,2,8,32,128]{4,3,2,1,0:T(8,128)}), f32[4,2,8,32,128]{4,3,2,1,0:T(8,128)S(1)}, u32[]{:S(2)}, u32[]{:S(2)}) async-start(f32[4,2,8,32,128]{4,3,2,1,0:T(8,128)} %shard_map.50), calls=%async_computation.2 | async-start | bytes 2097152 | tf_op jit(solution)/shard_map/all_to_all | solution.py:120
  56.5 6.9 %collective-permute-start = (f32[2,4,32,128]{3,2,1,0:T(8,128)S(1)}, f32[2,4,32,128]{3,2,1,0:T(8,128)S(1)}, u32[]{:S(2)}, u32[]{:S(2)}) collective-permute-start(f32[2,4,32,128]{3,2,1,0:T(8,128)S(1)} %select_bitcast_fusion), channel_id=1, source_target_pairs={{0,4},{4,0},{8,12},{12,8},{16,20},{20,16},{24,28},{28,24},{1,5},{5... | collective-permute-start | bytes 393224 | tf_op jit(solution)/shard_map/ppermute | solution.py:96
  63.5 8.3 %collective-permute-start.1 = (f32[2,2,32,128]{3,2,1,0:T(8,128)S(1)}, f32[2,2,32,128]{3,2,1,0:T(8,128)S(1)}, u32[]{:S(2)}, u32[]{:S(2)}) collective-permute-start(f32[2,2,32,128]{3,2,1,0:T(8,128)S(1)} %select_bitcast_fusion.1), channel_id=1, source_target_pairs={{0,8},{4,12},{8,0},{12,4},{16,24},{20,28},{24,16},{28,20},{1,9},{5... | collective-permute-start | bytes 196616 | tf_op jit(solution)/shard_map/ppermute | solution.py:96
  71.9 10.7 %collective-permute-start.2 = (f32[2,1,32,128]{3,2,0,1:T(8,128)S(1)}, f32[2,1,32,128]{3,2,0,1:T(8,128)S(1)}, u32[]{:S(2)}, u32[]{:S(2)}) collective-permute-start(f32[2,1,32,128]{3,2,0,1:T(8,128)S(1)} %select_bitcast_fusion.2), channel_id=1, source_target_pairs={{0,16},{4,20},{8,24},{12,28},{16,0},{20,4},{24,8},{28,12},{1,17},{... | collective-permute-start | bytes 98312 | tf_op jit(solution)/shard_map/ppermute | solution.py:96

commit v8 on v5

--- a/solution.py
+++ b/solution.py
@@ -20,7 +20,7 @@
     return back.transpose(1, 0, 2).reshape(cells, columns)
 
 
-def shade_kernel(facing_ref, incoming_ref, dens_ref, emit_ref, out_ref, *, light_scale, view_scale):
+def shade_kernel(facing_ref, dens_ref, emit_ref, out_ref, part_ref, *, light_scale, view_scale):
     rows, cells, _ = dens_ref.shape
     blocks, width = out_ref.shape[0], out_ref.shape[-1]
 
@@ -29,28 +29,35 @@
         emit = emit_ref[l]
         tau_light = dens * light_scale
         step = jnp.exp(-(dens * view_scale))
-        lit = emit * (0.2 + jnp.exp(-depth)) * (1.0 - step)
+        base = emit * (1.0 - step)
+        shaded = base * jnp.exp(-depth)
         s = [step[v:v + 1] for v in range(cells)]
-        c = [lit[v:v + 1] for v in range(cells)]
-        forward = c[cells - 1]
+        flip = facing_ref[l] == 1
+        ahead = [None] * cells
+        behind = [None] * cells
+        ahead[0] = jnp.ones_like(s[0])
+        for v in range(1, cells):
+            ahead[v] = ahead[v - 1] * s[v - 1]
+        behind[cells - 1] = jnp.ones_like(s[0])
         for v in range(cells - 2, -1, -1):
-            forward = c[v] + s[v] * forward
-        backward = c[0]
+            behind[v] = behind[v + 1] * s[v + 1]
+        weight = [jnp.where(flip, behind[v], ahead[v]) for v in range(cells)]
+        flat = weight[0] * base[0:1]
         for v in range(1, cells):
-            backward = c[v] + s[v] * backward
-        trans = s[0]
-        for v in range(1, cells):
-            trans = trans * s[v]
-        color = jnp.where(facing_ref[l] == 1, backward, forward)
+            flat = flat + weight[v] * base[v:v + 1]
+        trans = ahead[cells - 1] * s[cells - 1]
         for b in range(blocks):
-            out_ref[b, 0, 0, pl.ds(l, 1), :] = color[:, b * width:(b + 1) * width]
-            out_ref[b, 1, 0, pl.ds(l, 1), :] = trans[:, b * width:(b + 1) * width]
+            cut = slice(b * width, (b + 1) * width)
+            out_ref[b, 0, 0, pl.ds(l, 1), :] = 0.2 * flat[:, cut]
+            out_ref[b, 1, 0, pl.ds(l, 1), :] = trans[:, cut]
+            for v in range(cells):
+                part_ref[v, b, 0, pl.ds(l, 1), :] = (weight[v] * shaded[v:v + 1])[:, cut]
         return depth + tau_light
 
-    lax.fori_loop(0, rows, row, incoming_ref[...], unroll=8)
+    lax.fori_loop(0, rows, row, jnp.zeros(dens_ref.shape[1:], jnp.float32), unroll=8)
 
 
-def shade(facing, incoming, density, emission, light_scale, view_scale, blocks, width):
+def shade(facing, density, emission, light_scale, view_scale, blocks, width):
     rows, cells, columns = density.shape
     tile = blocks * width
     tiles = columns // tile
@@ -60,16 +67,21 @@
         grid=(tiles,),
         in_specs=[
             pl.BlockSpec(memory_space=pltpu.SMEM),
-            pl.BlockSpec((cells, tile), lambda j: (0, j)),
             pl.BlockSpec((rows, cells, tile), lambda j: (0, 0, j)),
             pl.BlockSpec((rows, cells, tile), lambda j: (0, 0, j)),
         ],
-        out_specs=pl.BlockSpec((blocks, 2, 1, rows, width), lambda j: (0, 0, j, 0, 0)),
-        out_shape=jax.ShapeDtypeStruct((blocks, 2, tiles, rows, width), jnp.float32),
+        out_specs=[
+            pl.BlockSpec((blocks, 2, 1, rows, width), lambda j: (0, 0, j, 0, 0)),
+            pl.BlockSpec((cells, blocks, 1, rows, width), lambda j: (0, 0, j, 0, 0)),
+        ],
+        out_shape=[
+            jax.ShapeDtypeStruct((blocks, 2, tiles, rows, width), jnp.float32),
+            jax.ShapeDtypeStruct((cells, blocks, tiles, rows, width), jnp.float32),
+        ],
         cost_estimate=pl.CostEstimate(
-            flops=30 * density.size, transcendentals=2 * density.size, bytes_accessed=2 * 4 * density.size + 8 * rows * columns
+            flops=40 * density.size, transcendentals=2 * density.size, bytes_accessed=4 * 4 * density.size + 8 * rows * columns
         ),
-    )(facing, incoming, density, emission)
+    )(facing, density, emission)
 
 
 def composite(colors, transes, reversed_rows):
@@ -91,13 +103,15 @@
     view_count = z_count * x_count
     tau_light = density * (1.0 / (rows * light_count))
     slab_depth = jnp.sum(tau_light, axis=0)
-    incoming = light_prefix(slab_depth)
-
     reversed_rows = facing == 1
     width = columns // view_count
-    stacked = shade(
-        facing, incoming, density, emission, 1.0 / (rows * light_count), 1.0 / (cells * view_count), x_count, width
+    unshaded, parts = shade(
+        facing, density, emission, 1.0 / (rows * light_count), 1.0 / (cells * view_count), x_count, width
     )
+    incoming = light_prefix(slab_depth)
+    light = jnp.exp(-incoming).reshape(cells, z_count, x_count, 1, width).transpose(0, 2, 1, 3, 4)
+    color = unshaded[:, 0] + jnp.sum(light * parts, axis=0)
+    stacked = jnp.stack([color, unshaded[:, 1]], axis=1)
     along_x = lax.all_to_all(stacked, "vx", 0, 0)
     color_x = composite(along_x[:, 0], along_x[:, 1], reversed_rows[None, :, None])
     trans_x = jnp.prod(along_x[:, 1], axis=0)

time: 78.4 us -> 76.8 us (0.980)
  blocking collectives: 46.8 us -> 35.6 us
  starting transfers between devices: 3.51 us -> 8.18 us
  other arithmetic: 3.52 us -> 6.88 us
  Pallas kernels: 7.42 us -> 8.48 us
    all_to_all x1 -> x0, blocking collectives: 11.1 us -> none  [light_prefix(): back = lax.all_to_all(before, 'light', 0, 0)]
    all_to_all x0 -> x1, starting transfers between devices: none -> 4.66 us  [light_prefix(): back = lax.all_to_all(before, 'light', 0, 0)]
    reduce_sum x0 -> x1, other arithmetic: none -> 2.07 us  [shards(): color = unshaded[:, 0] + jnp.sum(light * parts, axis=0)]
    another operation x0 -> x1, other arithmetic: none -> 1.1 us  [shards(): stacked = jnp.stack([color, unshaded[:, 1]], axis=1)]
    pallas_call x1, Pallas kernels: 7.42 us -> 8.48 us  [shade(): pl.pallas_call(body, grid=(tiles,), in_specs=[pl.BlockSpec(memory_space=p...]
  transfers between devices with their start and end apart: 1 -> 2, of which waited for: 1 -> 1; matrix products, arithmetic and copies ran while one was open for 0% -> 0% of each run, Pallas kernels for 0% -> 11%
where the time goes in v8:
time: 76.8 us; the launch traced here: 76.3 us
  blocking collectives  35.6 us (46%)
  waiting for transfers between devices  15.6 us (20%)
  Pallas kernels  8.48 us (11%)
  starting transfers between devices  8.18 us (11%)
  other arithmetic  6.88 us (9%)
    all_to_all x1, blocking collectives, shards(): along_z = lax.all_to_all(jnp.stack([color_x, trans_x], axis=1), 'vz', 0, 0)  20.8 us
    all_to_all x1, waiting for transfers between devices, shards(): along_x = lax.all_to_all(stacked, 'vx', 0, 0)  15.6 us
    all_to_all x1, blocking collectives, light_prefix(): mine = lax.all_to_all(chunks, 'light', 0, 0)  14.8 us
    pallas_call x1, Pallas kernels, shade(): pl.pallas_call(body, grid=(tiles,), in_specs=[pl.BlockSpec(memory_space=p...  8.48 us
    all_to_all x1, starting transfers between devices, light_prefix(): back = lax.all_to_all(before, 'light', 0, 0)  4.66 us
    all_to_all x1, starting transfers between devices, shards(): along_x = lax.all_to_all(stacked, 'vx', 0, 0)  3.51 us
    reduce_sum x1, other arithmetic, shards(): color = unshaded[:, 0] + jnp.sum(light * parts, axis=0)  2.07 us
    reduce_sum x1, other arithmetic, shards(): slab_depth = jnp.sum(tau_light, axis=0)  2.04 us
  transfers between devices with their start and end apart: 2, of which 1 were waited for; matrix products, arithmetic and copies ran while one was open for 0% of the time, Pallas kernels for 11%

profile of v8, /device:TPU:8, one launch (start us, length us, event | category | flops | bytes accessed | tf_op | source)
XLA Modules:
  0.0 76.3 jit_solution(16543765304721497529)
XLA Ops:
  0.6 2.0 %multiply_reduce_fusion.1 = f32[4,4096]{1,0:T(4,128)S(1)} fusion(f32[32,4,4096]{2,1,0:T(4,128)} %refs_1_.1), kind=kLoop, calls=%fused_computation.1 | loop fusion | flops 1032192 | bytes 2162688 | tf_op jit(solution)/shard_map/reduce_sum | solution.py:105
  2.7 14.8 %all_to_all.20 = f32[16,4,256]{2,1,0:T(4,128)S(1)} all-to-all(f32[16,4,256]{2,1,0:T(4,128)S(1)} %bitcast.125), channel_id=1, replica_groups=mesh['light'=16,'vz'=8,'vx'=4] {'light'}, dimensions={0} | all-to-all | bytes 131072 | tf_op jit(solution)/shard_map/all_to_all | solution.py:16
  17.5 0.6 concatenate.3
  18.2 4.7 %all-to-all-start.1 = ((f32[16,4,256]{2,1,0:T(4,128)}), f32[16,4,256]{2,1,0:T(4,128)S(1)}, u32[]{:S(2)}, u32[]{:S(2)}) async-start(f32[16,4,256]{2,1,0:T(4,128)} %concatenate.3), calls=%async_computation.1 | async-start | bytes 131072 | tf_op jit(solution)/shard_map/all_to_all | solution.py:19
  22.8 8.5 %shard_map.50 = (f32[4,2,8,32,128]{4,3,2,1,0:T(8,128)}, f32[4,4,8,32,128]{4,3,2,1,0:T(8,128)}) custom-call(s32[32]{0:T(128)} %refs_0_.1, f32[32,4,4096]{2,1,0:T(4,128)} %refs_1_.1, f32[32,4,4096]{2,1,0:T(4,128)} %refs_2_.1), custom_call_target="tpu_custom_call" | custom-call | flops 20971520 | bytes 9437184 | tf_op jit(solution)/shard_map/pallas_call | solution.py:65
  31.3 0.0 copy-start
  31.3 0.0 all-to-all-done.1
  31.4 2.1 %multiply_reduce_fusion = f32[4,8,32,128]{3,2,1,0:T(8,128)S(1)} fusion(f32[4,4,8,32,128]{4,3,2,1,0:T(8,128)} %get-tuple-element.5, f32[4,4,8,128]{3,2,1,0:T(8,128)S(1)} %copy.38), kind=kLoop, calls=%fused_computation | loop fusion | flops 917504 | bytes 2686976 | tf_op jit(solution)/shard_map/reduce_sum | solution.py:113
  33.5 0.0 copy-done
  33.5 0.2 bitcast_add_fusion
  33.7 0.0 copy-start.1
  33.7 1.1 %pad_maximum_fusion = f32[4,2,8,32,128]{4,3,2,1,0:T(8,128)} fusion(f32[4,1,8,32,128]{4,3,2,1,0:T(8,128)S(1)} %get-tuple-element.7, f32[4,1,8,32,128]{4,3,2,1,0:T(8,128)S(1)} %get-tuple-element.6), kind=kLoop, calls=%fused_computation.2 | loop fusion | flops 262144 | bytes 2097152 | tf_op jit(solution)/shard_map/stack | solution.py:114
  34.8 3.5 %all-to-all-start.2 = ((f32[4,2,8,32,128]{4,3,2,1,0:T(8,128)}), f32[4,2,8,32,128]{4,3,2,1,0:T(8,128)S(1)}, u32[]{:S(2)}, u32[]{:S(2)}) async-start(f32[4,2,8,32,128]{4,3,2,1,0:T(8,128)} %pad_maximum_fusion), calls=%async_computation.2 | async-start | bytes 2097152 | tf_op jit(solution)/shard_map/all_to_all | solution.py:115
  38.3 0.0 copy-done.1
  38.3 15.6 %all-to-all-done.2 = f32[4,2,8,32,128]{4,3,2,1,0:T(8,128)S(1)} async-done(((f32[4,2,8,32,128]{4,3,2,1,0:T(8,128)}), f32[4,2,8,32,128]{4,3,2,1,0:T(8,128)S(1)}, u32[]{:S(2)}, u32[]{:S(2)}) %all-to-all-start.2) | async-done | bytes 1048608 | tf_op jit(solution)/shard_map/all_to_all | solution.py:115
  54.0 0.1 fusion.2
  54.2 20.8 %all_to_all.21 = f32[8,2,32,128]{3,2,1,0:T(8,128)S(1)} all-to-all(f32[8,2,32,128]{3,2,1,0:T(8,128)S(1)} %copy.39), channel_id=1, replica_groups=mesh['light'=16,'vz'=8,'vx'=4] {'vz'}, dimensions={0} | all-to-all | bytes 524288 | tf_op jit(solution)/shard_map/all_to_all | solution.py:118
  75.0 0.7 fusion.7
  75.7 0.6 slice_reduce_fusion.1
  (10 shorter events, 0.2 us)
Async XLA Ops:
  18.2 13.2 %all-to-all-start.1 = ((f32[16,4,256]{2,1,0:T(4,128)}), f32[16,4,256]{2,1,0:T(4,128)S(1)}, u32[]{:S(2)}, u32[]{:S(2)}) async-start(f32[16,4,256]{2,1,0:T(4,128)} %concatenate.3), calls=%async_computation.1 | async-start | bytes 131072 | tf_op jit(solution)/shard_map/all_to_all | solution.py:19
  31.3 2.2 %copy-start = (f32[4,2,8,32,128]{4,3,2,1,0:T(8,128)S(1)}, f32[4,2,8,32,128]{4,3,2,1,0:T(8,128)}, u32[]{:S(2)}) copy-start(f32[4,2,8,32,128]{4,3,2,1,0:T(8,128)} %get-tuple-element.4) | copy-start | bytes 3145732
  33.7 4.6 %copy-start.1 = (s32[32]{0:T(128)S(1)}, s32[32]{0:T(128)}, u32[]{:S(2)}) copy-start(s32[32]{0:T(128)} %refs_0_.1) | copy-start | bytes 388
  34.8 19.2 %all-to-all-start.2 = ((f32[4,2,8,32,128]{4,3,2,1,0:T(8,128)}), f32[4,2,8,32,128]{4,3,2,1,0:T(8,128)S(1)}, u32[]{:S(2)}, u32[]{:S(2)}) async-start(f32[4,2,8,32,128]{4,3,2,1,0:T(8,128)} %pad_maximum_fusion), calls=%async_computation.2 | async-start | bytes 2097152 | tf_op jit(solution)/shard_map/all_to_all | solution.py:115

commit v9 on v8

--- a/solution.py
+++ b/solution.py
@@ -110,8 +110,7 @@
     )
     incoming = light_prefix(slab_depth)
     light = jnp.exp(-incoming).reshape(cells, z_count, x_count, 1, width).transpose(0, 2, 1, 3, 4)
-    color = unshaded[:, 0] + jnp.sum(light * parts, axis=0)
-    stacked = jnp.stack([color, unshaded[:, 1]], axis=1)
+    stacked = unshaded.at[:, 0].add(jnp.sum(light * parts, axis=0))
     along_x = lax.all_to_all(stacked, "vx", 0, 0)
     color_x = composite(along_x[:, 0], along_x[:, 1], reversed_rows[None, :, None])
     trans_x = jnp.prod(along_x[:, 1], axis=0)

time: 76.8 us -> 77.4 us (level)
    scatter-add x0 -> x1, other arithmetic: none -> 1.92 us  [shards(): stacked = unshaded.at[:, 0].add(jnp.sum(light * parts, axis=0))]
    another operation x1 -> x0, other arithmetic: 1.1 us -> none  [shards(): stacked = jnp.stack([color, unshaded[:, 1]], axis=1)]
where the time goes in v9:
time: 77.4 us; the launch traced here: 76.9 us
  blocking collectives  35.6 us (46%)
  waiting for transfers between devices  15.6 us (20%)
  Pallas kernels  8.48 us (11%)
  starting transfers between devices  8.18 us (11%)
  other arithmetic  7.48 us (10%)
    all_to_all x1, blocking collectives, shards(): along_z = lax.all_to_all(jnp.stack([color_x, trans_x], axis=1), 'vz', 0, 0)  20.8 us
    all_to_all x1, waiting for transfers between devices, shards(): along_x = lax.all_to_all(stacked, 'vx', 0, 0)  15.6 us
    all_to_all x1, blocking collectives, light_prefix(): mine = lax.all_to_all(chunks, 'light', 0, 0)  14.8 us
    pallas_call x1, Pallas kernels, shade(): pl.pallas_call(body, grid=(tiles,), in_specs=[pl.BlockSpec(memory_space=p...  8.48 us
    all_to_all x1, starting transfers between devices, light_prefix(): back = lax.all_to_all(before, 'light', 0, 0)  4.66 us
    all_to_all x1, starting transfers between devices, shards(): along_x = lax.all_to_all(stacked, 'vx', 0, 0)  3.51 us
    reduce_sum x1, other arithmetic, shards(): slab_depth = jnp.sum(tau_light, axis=0)  2.04 us
    reduce_sum x1, other arithmetic, shards(): stacked = unshaded.at[:, 0].add(jnp.sum(light * parts, axis=0))  2.01 us
  transfers between devices with their start and end apart: 2, of which 1 were waited for; matrix products, arithmetic and copies ran while one was open for 0% of the time, Pallas kernels for 11%

profile of v9, /device:TPU:8, one launch (start us, length us, event | category | flops | bytes accessed | tf_op | source)
XLA Modules:
  0.0 76.9 jit_solution(2327870717024605285)
XLA Ops:
  0.6 2.0 %multiply_reduce_fusion.1 = f32[4,4096]{1,0:T(4,128)S(1)} fusion(f32[32,4,4096]{2,1,0:T(4,128)} %refs_1_.1), kind=kLoop, calls=%fused_computation.1 | loop fusion | flops 1032192 | bytes 2162688 | tf_op jit(solution)/shard_map/reduce_sum | solution.py:105
  2.7 14.8 %all_to_all.20 = f32[16,4,256]{2,1,0:T(4,128)S(1)} all-to-all(f32[16,4,256]{2,1,0:T(4,128)S(1)} %bitcast.127), channel_id=1, replica_groups=mesh['light'=16,'vz'=8,'vx'=4] {'light'}, dimensions={0} | all-to-all | bytes 131072 | tf_op jit(solution)/shard_map/all_to_all | solution.py:16
  17.5 0.6 concatenate.5
  18.2 4.7 %all-to-all-start.1 = ((f32[16,4,256]{2,1,0:T(4,128)}), f32[16,4,256]{2,1,0:T(4,128)S(1)}, u32[]{:S(2)}, u32[]{:S(2)}) async-start(f32[16,4,256]{2,1,0:T(4,128)} %concatenate.5), calls=%async_computation.1 | async-start | bytes 131072 | tf_op jit(solution)/shard_map/all_to_all | solution.py:19
  22.8 8.5 %shard_map.50 = (f32[4,2,8,32,128]{4,3,2,1,0:T(8,128)}, f32[4,4,8,32,128]{4,3,2,1,0:T(8,128)}) custom-call(s32[32]{0:T(128)} %refs_0_.1, f32[32,4,4096]{2,1,0:T(4,128)} %refs_1_.1, f32[32,4,4096]{2,1,0:T(4,128)} %refs_2_.1), custom_call_target="tpu_custom_call" | custom-call | flops 20971520 | bytes 9437184 | tf_op jit(solution)/shard_map/pallas_call | solution.py:65
  31.3 0.0 all-to-all-done.1
  31.4 2.0 %multiply_reduce_fusion = f32[4,8,32,128]{3,2,1,0:T(8,128)S(1)} fusion(f32[4,4,8,32,128]{4,3,2,1,0:T(8,128)} %get-tuple-element.17, f32[4,4,8,128]{3,2,1,0:T(8,128)S(1)} %copy.38), kind=kLoop, calls=%fused_computation | loop fusion | flops 917504 | bytes 2686976 | tf_op jit(solution)/shard_map/reduce_sum | solution.py:113
  33.4 0.0 copy-start
  33.5 1.9 %fusion = f32[4,2,8,32,128]{4,3,2,1,0:T(8,128)} fusion(f32[4,2,8,32,128]{4,3,2,1,0:T(8,128)} %get-tuple-element.16, f32[4,8,32,128]{3,2,1,0:T(8,128)S(1)} %multiply_reduce_fusion), kind=kLoop, calls=%fused_computation.4 | loop fusion | flops 131072 | bytes 1572864 | tf_op jit(solution)/shard_map/scatter-add | solution.py:113
  35.4 3.5 %all-to-all-start.2 = ((f32[4,2,8,32,128]{4,3,2,1,0:T(8,128)}), f32[4,2,8,32,128]{4,3,2,1,0:T(8,128)S(1)}, u32[]{:S(2)}, u32[]{:S(2)}) async-start(f32[4,2,8,32,128]{4,3,2,1,0:T(8,128)} %fusion), calls=%async_computation.2 | async-start | bytes 2097152 | tf_op jit(solution)/shard_map/all_to_all | solution.py:114
  38.9 0.0 copy-done
  38.9 15.6 %all-to-all-done.2 = f32[4,2,8,32,128]{4,3,2,1,0:T(8,128)S(1)} async-done(((f32[4,2,8,32,128]{4,3,2,1,0:T(8,128)}), f32[4,2,8,32,128]{4,3,2,1,0:T(8,128)S(1)}, u32[]{:S(2)}, u32[]{:S(2)}) %all-to-all-start.2) | async-done | bytes 1048608 | tf_op jit(solution)/shard_map/all_to_all | solution.py:114
  54.6 0.1 fusion.3
  54.8 20.8 %all_to_all.21 = f32[8,2,32,128]{3,2,1,0:T(8,128)S(1)} all-to-all(f32[8,2,32,128]{3,2,1,0:T(8,128)S(1)} %copy.39), channel_id=1, replica_groups=mesh['light'=16,'vz'=8,'vx'=4] {'vz'}, dimensions={0} | all-to-all | bytes 524288 | tf_op jit(solution)/shard_map/all_to_all | solution.py:117
  75.6 0.7 fusion.8
  76.2 0.6 slice_reduce_fusion.1
  (10 shorter events, 0.2 us)
Async XLA Ops:
  18.2 13.1 %all-to-all-start.1 = ((f32[16,4,256]{2,1,0:T(4,128)}), f32[16,4,256]{2,1,0:T(4,128)S(1)}, u32[]{:S(2)}, u32[]{:S(2)}) async-start(f32[16,4,256]{2,1,0:T(4,128)} %concatenate.5), calls=%async_computation.1 | async-start | bytes 131072 | tf_op jit(solution)/shard_map/all_to_all | solution.py:19
  33.4 5.5 %copy-start = (s32[32]{0:T(128)S(1)}, s32[32]{0:T(128)}, u32[]{:S(2)}) copy-start(s32[32]{0:T(128)} %refs_0_.1) | copy-start | bytes 388
  35.4 19.2 %all-to-all-start.2 = ((f32[4,2,8,32,128]{4,3,2,1,0:T(8,128)}), f32[4,2,8,32,128]{4,3,2,1,0:T(8,128)S(1)}, u32[]{:S(2)}, u32[]{:S(2)}) async-start(f32[4,2,8,32,128]{4,3,2,1,0:T(8,128)} %fusion), calls=%async_computation.2 | async-start | bytes 2097152 | tf_op jit(solution)/shard_map/all_to_all | solution.py:114

commit v10 on v9

--- a/solution.py
+++ b/solution.py
@@ -84,6 +84,32 @@
     )(facing, density, emission)
 
 
+def lit_kernel(light_ref, parts_ref, unshaded_ref, out_ref):
+    total = unshaded_ref[:, 0]
+    for v in range(parts_ref.shape[0]):
+        total = total + light_ref[v] * parts_ref[v]
+    out_ref[:, 0] = total
+
+
+def apply_light(light, parts, unshaded):
+    cells, blocks, tiles, rows, width = parts.shape
+    return pl.pallas_call(
+        lit_kernel,
+        grid=(tiles,),
+        in_specs=[
+            pl.BlockSpec((cells, blocks, 1, 1, width), lambda j: (0, 0, j, 0, 0)),
+            pl.BlockSpec((cells, blocks, 1, rows, width), lambda j: (0, 0, j, 0, 0)),
+            pl.BlockSpec((blocks, 1, 1, rows, width), lambda j: (0, 0, j, 0, 0)),
+        ],
+        out_specs=pl.BlockSpec((blocks, 1, 1, rows, width), lambda j: (0, 0, j, 0, 0)),
+        out_shape=jax.ShapeDtypeStruct(unshaded.shape, unshaded.dtype),
+        input_output_aliases={2: 0},
+        cost_estimate=pl.CostEstimate(
+            flops=2 * parts.size, transcendentals=0, bytes_accessed=4 * (parts.size + 2 * blocks * tiles * rows * width)
+        ),
+    )(light, parts, unshaded)
+
+
 def composite(colors, transes, reversed_rows):
     count = colors.shape[0]
     forward = colors[count - 1]
@@ -110,7 +136,7 @@
     )
     incoming = light_prefix(slab_depth)
     light = jnp.exp(-incoming).reshape(cells, z_count, x_count, 1, width).transpose(0, 2, 1, 3, 4)
-    stacked = unshaded.at[:, 0].add(jnp.sum(light * parts, axis=0))
+    stacked = apply_light(light, parts, unshaded)
     along_x = lax.all_to_all(stacked, "vx", 0, 0)
     color_x = composite(along_x[:, 0], along_x[:, 1], reversed_rows[None, :, None])
     trans_x = jnp.prod(along_x[:, 1], axis=0)

time: 77.4 us -> 79.6 us (1.028)
  Pallas kernels: 8.48 us -> 13.9 us
  other arithmetic: 7.48 us -> 3.55 us
    pallas_call x0 -> x1, Pallas kernels: none -> 5.4 us  [apply_light(): pl.pallas_call(lit_kernel, grid=(tiles,), in_specs=[pl.BlockSpec((cells,...]
    reduce_sum x1 -> x0, other arithmetic: 2.01 us -> none  [shards(): stacked = unshaded.at[:, 0].add(jnp.sum(light * parts, axis=0))]
    scatter-add x1 -> x0, other arithmetic: 1.92 us -> none  [shards(): stacked = unshaded.at[:, 0].add(jnp.sum(light * parts, axis=0))]
where the time goes in v10:
time: 79.6 us; the launch traced here: 79 us
  blocking collectives  35.6 us (45%)
  waiting for transfers between devices  15.6 us (20%)
  Pallas kernels  13.9 us (17%)
  starting transfers between devices  8.18 us (10%)
  other arithmetic  3.55 us (4%)
  local copies, waits for them, and re-layouts  1.4 us (2%)
    all_to_all x1, blocking collectives, shards(): along_z = lax.all_to_all(jnp.stack([color_x, trans_x], axis=1), 'vz', 0, 0)  20.8 us
    all_to_all x1, waiting for transfers between devices, shards(): along_x = lax.all_to_all(stacked, 'vx', 0, 0)  15.6 us
    all_to_all x1, blocking collectives, light_prefix(): mine = lax.all_to_all(chunks, 'light', 0, 0)  14.8 us
    pallas_call x1, Pallas kernels, shade(): pl.pallas_call(body, grid=(tiles,), in_specs=[pl.BlockSpec(memory_space=p...  8.48 us
    pallas_call x1, Pallas kernels, apply_light(): pl.pallas_call(lit_kernel, grid=(tiles,), in_specs=[pl.BlockSpec((cells,...  5.4 us
    all_to_all x1, starting transfers between devices, light_prefix(): back = lax.all_to_all(before, 'light', 0, 0)  4.66 us
    all_to_all x1, starting transfers between devices, shards(): along_x = lax.all_to_all(stacked, 'vx', 0, 0)  3.51 us
    reduce_sum x1, other arithmetic, shards(): slab_depth = jnp.sum(tau_light, axis=0)  2.04 us
  transfers between devices with their start and end apart: 2, of which 1 were waited for; matrix products, arithmetic and copies ran while one was open for 0% of the time, Pallas kernels for 11%

profile of v10, /device:TPU:8, one launch (start us, length us, event | category | flops | bytes accessed | tf_op | source)
XLA Modules:
  0.0 79.0 jit_solution(13905613528233618784)
XLA Ops:
  0.6 2.0 %multiply_reduce_fusion = f32[4,4096]{1,0:T(4,128)S(1)} fusion(f32[32,4,4096]{2,1,0:T(4,128)} %refs_1_.1), kind=kLoop, calls=%fused_computation | loop fusion | flops 1032192 | bytes 2162688 | tf_op jit(solution)/shard_map/reduce_sum | solution.py:131
  2.7 14.8 %all_to_all.20 = f32[16,4,256]{2,1,0:T(4,128)S(1)} all-to-all(f32[16,4,256]{2,1,0:T(4,128)S(1)} %bitcast.124), channel_id=1, replica_groups=mesh['light'=16,'vz'=8,'vx'=4] {'light'}, dimensions={0} | all-to-all | bytes 131072 | tf_op jit(solution)/shard_map/all_to_all | solution.py:16
  17.5 0.6 concatenate.3
  18.2 4.7 %all-to-all-start.1 = ((f32[16,4,256]{2,1,0:T(4,128)}), f32[16,4,256]{2,1,0:T(4,128)S(1)}, u32[]{:S(2)}, u32[]{:S(2)}) async-start(f32[16,4,256]{2,1,0:T(4,128)} %concatenate.3), calls=%async_computation.1 | async-start | bytes 131072 | tf_op jit(solution)/shard_map/all_to_all | solution.py:19
  22.8 8.5 %shard_map.50 = (f32[4,2,8,32,128]{4,3,2,1,0:T(8,128)}, f32[4,4,8,32,128]{4,3,2,1,0:T(8,128)}) custom-call(s32[32]{0:T(128)} %refs_0_.1, f32[32,4,4096]{2,1,0:T(4,128)} %refs_1_.1, f32[32,4,4096]{2,1,0:T(4,128)} %refs_2_.1), custom_call_target="tpu_custom_call" | custom-call | flops 20971520 | bytes 9437184 | tf_op jit(solution)/shard_map/pallas_call | solution.py:65
  31.3 0.0 all-to-all-done.1
  31.4 0.7 copy.42
  32.1 0.0 copy-start
  32.1 5.4 %shard_map.51 = f32[4,2,8,32,128]{4,3,2,1,0:T(8,128)} custom-call(f32[4,4,8,1,128]{4,3,2,1,0:T(1,128)} %bitcast.123, f32[4,4,8,32,128]{4,3,2,1,0:T(8,128)} %get-tuple-element.4.parts_ref, f32[4,2,8,32,128]{4,3,2,1,0:T(8,128)} %get-tuple-element.5.unshaded_ref), custom_call_target="tpu_custom_call", output_to_operand_aliasing={{}: (2, {})} | custom-call | flops 1048576 | bytes 3145728 | tf_op jit(solution)/shard_map/pallas_call | solution.py:96
  37.5 3.5 %all-to-all-start.2 = ((f32[4,2,8,32,128]{4,3,2,1,0:T(8,128)}), f32[4,2,8,32,128]{4,3,2,1,0:T(8,128)S(1)}, u32[]{:S(2)}, u32[]{:S(2)}) async-start(f32[4,2,8,32,128]{4,3,2,1,0:T(8,128)} %shard_map.51), calls=%async_computation.2 | async-start | bytes 2097152 | tf_op jit(solution)/shard_map/all_to_all | solution.py:140
  41.0 0.0 copy-done
  41.0 15.6 %all-to-all-done.2 = f32[4,2,8,32,128]{4,3,2,1,0:T(8,128)S(1)} async-done(((f32[4,2,8,32,128]{4,3,2,1,0:T(8,128)}), f32[4,2,8,32,128]{4,3,2,1,0:T(8,128)S(1)}, u32[]{:S(2)}, u32[]{:S(2)}) %all-to-all-start.2) | async-done | bytes 1048608 | tf_op jit(solution)/shard_map/all_to_all | solution.py:140
  56.7 0.1 fusion.2
  56.9 20.8 %all_to_all.21 = f32[8,2,32,128]{3,2,1,0:T(8,128)S(1)} all-to-all(f32[8,2,32,128]{3,2,1,0:T(8,128)S(1)} %copy.40), channel_id=1, replica_groups=mesh['light'=16,'vz'=8,'vx'=4] {'vz'}, dimensions={0} | all-to-all | bytes 524288 | tf_op jit(solution)/shard_map/all_to_all | solution.py:143
  77.7 0.7 fusion.7
  78.4 0.6 slice_reduce_fusion.1
  (9 shorter events, 0.2 us)
Async XLA Ops:
  18.2 13.1 %all-to-all-start.1 = ((f32[16,4,256]{2,1,0:T(4,128)}), f32[16,4,256]{2,1,0:T(4,128)S(1)}, u32[]{:S(2)}, u32[]{:S(2)}) async-start(f32[16,4,256]{2,1,0:T(4,128)} %concatenate.3), calls=%async_computation.1 | async-start | bytes 131072 | tf_op jit(solution)/shard_map/all_to_all | solution.py:19
  32.1 8.9 %copy-start = (s32[32]{0:T(128)S(1)}, s32[32]{0:T(128)}, u32[]{:S(2)}) copy-start(s32[32]{0:T(128)} %refs_0_.1) | copy-start | bytes 388
  37.5 19.2 %all-to-all-start.2 = ((f32[4,2,8,32,128]{4,3,2,1,0:T(8,128)}), f32[4,2,8,32,128]{4,3,2,1,0:T(8,128)S(1)}, u32[]{:S(2)}, u32[]{:S(2)}) async-start(f32[4,2,8,32,128]{4,3,2,1,0:T(8,128)} %shard_map.51), calls=%async_computation.2 | async-start | bytes 2097152 | tf_op jit(solution)/shard_map/all_to_all | solution.py:140

commit v11 on v10

--- a/solution.py
+++ b/solution.py
@@ -85,9 +85,10 @@
 
 
 def lit_kernel(light_ref, parts_ref, unshaded_ref, out_ref):
+    j = pl.program_id(0)
     total = unshaded_ref[:, 0]
     for v in range(parts_ref.shape[0]):
-        total = total + light_ref[v] * parts_ref[v]
+        total = total + light_ref[v, :, pl.ds(j, 1)] * parts_ref[v]
     out_ref[:, 0] = total
 
 
@@ -97,7 +98,7 @@
         lit_kernel,
         grid=(tiles,),
         in_specs=[
-            pl.BlockSpec((cells, blocks, 1, 1, width), lambda j: (0, 0, j, 0, 0)),
+            pl.BlockSpec(light.shape, lambda j: (0, 0, 0, 0, 0)),
             pl.BlockSpec((cells, blocks, 1, rows, width), lambda j: (0, 0, j, 0, 0)),
             pl.BlockSpec((blocks, 1, 1, rows, width), lambda j: (0, 0, j, 0, 0)),
         ],

time: 79.6 us -> 79.6 us (level)
  no operation moved by 1% of the time
where the time goes in v11:
time: 79.6 us; the launch traced here: 78.9 us
  blocking collectives  35.6 us (45%)
  waiting for transfers between devices  15.6 us (20%)
  Pallas kernels  13.8 us (17%)
  starting transfers between devices  8.18 us (10%)
  other arithmetic  3.55 us (4%)
  local copies, waits for them, and re-layouts  1.4 us (2%)
    all_to_all x1, blocking collectives, shards(): along_z = lax.all_to_all(jnp.stack([color_x, trans_x], axis=1), 'vz', 0, 0)  20.8 us
    all_to_all x1, waiting for transfers between devices, shards(): along_x = lax.all_to_all(stacked, 'vx', 0, 0)  15.6 us
    all_to_all x1, blocking collectives, light_prefix(): mine = lax.all_to_all(chunks, 'light', 0, 0)  14.8 us
    pallas_call x1, Pallas kernels, shade(): pl.pallas_call(body, grid=(tiles,), in_specs=[pl.BlockSpec(memory_space=p...  8.48 us
    pallas_call x1, Pallas kernels, apply_light(): pl.pallas_call(lit_kernel, grid=(tiles,), in_specs=[pl.BlockSpec(light.sh...  5.36 us
    all_to_all x1, starting transfers between devices, light_prefix(): back = lax.all_to_all(before, 'light', 0, 0)  4.66 us
    all_to_all x1, starting transfers between devices, shards(): along_x = lax.all_to_all(stacked, 'vx', 0, 0)  3.51 us
    reduce_sum x1, other arithmetic, shards(): slab_depth = jnp.sum(tau_light, axis=0)  2.04 us
  transfers between devices with their start and end apart: 2, of which 1 were waited for; matrix products, arithmetic and copies ran while one was open for 0% of the time, Pallas kernels for 11%

profile of v11, /device:TPU:8, one launch (start us, length us, event | category | flops | bytes accessed | tf_op | source)
XLA Modules:
  0.0 78.9 jit_solution(5606917936803645548)
XLA Ops:
  0.6 2.0 %multiply_reduce_fusion = f32[4,4096]{1,0:T(4,128)S(1)} fusion(f32[32,4,4096]{2,1,0:T(4,128)} %refs_1_.1), kind=kLoop, calls=%fused_computation | loop fusion | flops 1032192 | bytes 2162688 | tf_op jit(solution)/shard_map/reduce_sum | solution.py:132
  2.7 14.8 %all_to_all.20 = f32[16,4,256]{2,1,0:T(4,128)S(1)} all-to-all(f32[16,4,256]{2,1,0:T(4,128)S(1)} %bitcast.124), channel_id=1, replica_groups=mesh['light'=16,'vz'=8,'vx'=4] {'light'}, dimensions={0} | all-to-all | bytes 131072 | tf_op jit(solution)/shard_map/all_to_all | solution.py:16
  17.5 0.6 concatenate.3
  18.2 4.7 %all-to-all-start.1 = ((f32[16,4,256]{2,1,0:T(4,128)}), f32[16,4,256]{2,1,0:T(4,128)S(1)}, u32[]{:S(2)}, u32[]{:S(2)}) async-start(f32[16,4,256]{2,1,0:T(4,128)} %concatenate.3), calls=%async_computation.1 | async-start | bytes 131072 | tf_op jit(solution)/shard_map/all_to_all | solution.py:19
  22.8 8.5 %shard_map.50 = (f32[4,2,8,32,128]{4,3,2,1,0:T(8,128)}, f32[4,4,8,32,128]{4,3,2,1,0:T(8,128)}) custom-call(s32[32]{0:T(128)} %refs_0_.1, f32[32,4,4096]{2,1,0:T(4,128)} %refs_1_.1, f32[32,4,4096]{2,1,0:T(4,128)} %refs_2_.1), custom_call_target="tpu_custom_call" | custom-call | flops 20971520 | bytes 9437184 | tf_op jit(solution)/shard_map/pallas_call | solution.py:65
  31.3 0.0 all-to-all-done.1
  31.4 0.7 copy.42
  32.1 0.0 copy-start
  32.1 5.4 %shard_map.51 = f32[4,2,8,32,128]{4,3,2,1,0:T(8,128)} custom-call(f32[4,4,8,1,128]{4,3,2,1,0:T(1,128)} %bitcast.123, f32[4,4,8,32,128]{4,3,2,1,0:T(8,128)} %get-tuple-element.4.parts_ref, f32[4,2,8,32,128]{4,3,2,1,0:T(8,128)} %get-tuple-element.5.unshaded_ref), custom_call_target="tpu_custom_call", output_to_operand_aliasing={{}: (2, {})} | custom-call | flops 1048576 | bytes 3145728 | tf_op jit(solution)/shard_map/pallas_call | solution.py:97
  37.5 3.5 %all-to-all-start.2 = ((f32[4,2,8,32,128]{4,3,2,1,0:T(8,128)}), f32[4,2,8,32,128]{4,3,2,1,0:T(8,128)S(1)}, u32[]{:S(2)}, u32[]{:S(2)}) async-start(f32[4,2,8,32,128]{4,3,2,1,0:T(8,128)} %shard_map.51), calls=%async_computation.2 | async-start | bytes 2097152 | tf_op jit(solution)/shard_map/all_to_all | solution.py:141
  41.0 0.0 copy-done
  41.0 15.6 %all-to-all-done.2 = f32[4,2,8,32,128]{4,3,2,1,0:T(8,128)S(1)} async-done(((f32[4,2,8,32,128]{4,3,2,1,0:T(8,128)}), f32[4,2,8,32,128]{4,3,2,1,0:T(8,128)S(1)}, u32[]{:S(2)}, u32[]{:S(2)}) %all-to-all-start.2) | async-done | bytes 1048608 | tf_op jit(solution)/shard_map/all_to_all | solution.py:141
  56.7 0.1 fusion.2
  56.9 20.8 %all_to_all.21 = f32[8,2,32,128]{3,2,1,0:T(8,128)S(1)} all-to-all(f32[8,2,32,128]{3,2,1,0:T(8,128)S(1)} %copy.40), channel_id=1, replica_groups=mesh['light'=16,'vz'=8,'vx'=4] {'vz'}, dimensions={0} | all-to-all | bytes 524288 | tf_op jit(solution)/shard_map/all_to_all | solution.py:144
  77.7 0.7 fusion.7
  78.3 0.6 slice_reduce_fusion.1
  (9 shorter events, 0.2 us)
Async XLA Ops:
  18.2 13.1 %all-to-all-start.1 = ((f32[16,4,256]{2,1,0:T(4,128)}), f32[16,4,256]{2,1,0:T(4,128)S(1)}, u32[]{:S(2)}, u32[]{:S(2)}) async-start(f32[16,4,256]{2,1,0:T(4,128)} %concatenate.3), calls=%async_computation.1 | async-start | bytes 131072 | tf_op jit(solution)/shard_map/all_to_all | solution.py:19
  32.1 8.9 %copy-start = (s32[32]{0:T(128)S(1)}, s32[32]{0:T(128)}, u32[]{:S(2)}) copy-start(s32[32]{0:T(128)} %refs_0_.1) | copy-start | bytes 388
  37.5 19.2 %all-to-all-start.2 = ((f32[4,2,8,32,128]{4,3,2,1,0:T(8,128)}), f32[4,2,8,32,128]{4,3,2,1,0:T(8,128)S(1)}, u32[]{:S(2)}, u32[]{:S(2)}) async-start(f32[4,2,8,32,128]{4,3,2,1,0:T(8,128)} %shard_map.51), calls=%async_computation.2 | async-start | bytes 2097152 | tf_op jit(solution)/shard_map/all_to_all | solution.py:141

commit v12 on v8

--- a/solution.py
+++ b/solution.py
@@ -46,15 +46,27 @@
         for v in range(1, cells):
             flat = flat + weight[v] * base[v:v + 1]
         trans = ahead[cells - 1] * s[cells - 1]
+        parts = [weight[v] * shaded[v:v + 1] for v in range(cells)]
+        return depth + tau_light, [0.2 * flat, trans] + parts
+
+    group = 8
+
+    def rows_of(g, depth):
+        first = pl.multiple_of(g * group, group)
+        outs = []
+        for k in range(group):
+            depth, got = row(first + k, depth)
+            outs.append(got)
+        lines = [jnp.concatenate([o[i] for o in outs], axis=0) for i in range(2 + cells)]
         for b in range(blocks):
             cut = slice(b * width, (b + 1) * width)
-            out_ref[b, 0, 0, pl.ds(l, 1), :] = 0.2 * flat[:, cut]
-            out_ref[b, 1, 0, pl.ds(l, 1), :] = trans[:, cut]
+            out_ref[b, 0, 0, pl.ds(first, group), :] = lines[0][:, cut]
+            out_ref[b, 1, 0, pl.ds(first, group), :] = lines[1][:, cut]
             for v in range(cells):
-                part_ref[v, b, 0, pl.ds(l, 1), :] = (weight[v] * shaded[v:v + 1])[:, cut]
-        return depth + tau_light
+                part_ref[v, b, 0, pl.ds(first, group), :] = lines[2 + v][:, cut]
+        return depth
 
-    lax.fori_loop(0, rows, row, jnp.zeros(dens_ref.shape[1:], jnp.float32), unroll=8)
+    lax.fori_loop(0, rows // group, rows_of, jnp.zeros(dens_ref.shape[1:], jnp.float32))
 
 
 def shade(facing, density, emission, light_scale, view_scale, blocks, width):

time: 76.8 us -> 77.1 us (level)
  transfers between devices with their start and end apart: 2 -> 2, of which waited for: 1 -> 1; matrix products, arithmetic and copies ran while one was open for 0% -> 0% of each run, Pallas kernels for 11% -> 12%
where the time goes in v12:
time: 77.1 us; the launch traced here: 76.6 us
  blocking collectives  35.6 us (46%)
  waiting for transfers between devices  15.6 us (20%)
  Pallas kernels  8.82 us (11%)
  starting transfers between devices  8.18 us (11%)
  other arithmetic  6.88 us (9%)
    all_to_all x1, blocking collectives, shards(): along_z = lax.all_to_all(jnp.stack([color_x, trans_x], axis=1), 'vz', 0, 0)  20.8 us
    all_to_all x1, waiting for transfers between devices, shards(): along_x = lax.all_to_all(stacked, 'vx', 0, 0)  15.6 us
    all_to_all x1, blocking collectives, light_prefix(): mine = lax.all_to_all(chunks, 'light', 0, 0)  14.8 us
    pallas_call x1, Pallas kernels, shade(): pl.pallas_call(body, grid=(tiles,), in_specs=[pl.BlockSpec(memory_space=p...  8.82 us
    all_to_all x1, starting transfers between devices, light_prefix(): back = lax.all_to_all(before, 'light', 0, 0)  4.66 us
    all_to_all x1, starting transfers between devices, shards(): along_x = lax.all_to_all(stacked, 'vx', 0, 0)  3.51 us
    reduce_sum x1, other arithmetic, shards(): color = unshaded[:, 0] + jnp.sum(light * parts, axis=0)  2.07 us
    reduce_sum x1, other arithmetic, shards(): slab_depth = jnp.sum(tau_light, axis=0)  2.04 us
  transfers between devices with their start and end apart: 2, of which 1 were waited for; matrix products, arithmetic and copies ran while one was open for 0% of the time, Pallas kernels for 12%

profile of v12, /device:TPU:8, one launch (start us, length us, event | category | flops | bytes accessed | tf_op | source)
XLA Modules:
  0.0 76.6 jit_solution(7984071426912252563)
XLA Ops:
  0.6 2.0 %multiply_reduce_fusion.1 = f32[4,4096]{1,0:T(4,128)S(1)} fusion(f32[32,4,4096]{2,1,0:T(4,128)} %refs_1_.1), kind=kLoop, calls=%fused_computation.1 | loop fusion | flops 1032192 | bytes 2162688 | tf_op jit(solution)/shard_map/reduce_sum | solution.py:117
  2.7 14.8 %all_to_all.20 = f32[16,4,256]{2,1,0:T(4,128)S(1)} all-to-all(f32[16,4,256]{2,1,0:T(4,128)S(1)} %bitcast.125), channel_id=1, replica_groups=mesh['light'=16,'vz'=8,'vx'=4] {'light'}, dimensions={0} | all-to-all | bytes 131072 | tf_op jit(solution)/shard_map/all_to_all | solution.py:16
  17.5 0.6 concatenate.3
  18.2 4.7 %all-to-all-start.1 = ((f32[16,4,256]{2,1,0:T(4,128)}), f32[16,4,256]{2,1,0:T(4,128)S(1)}, u32[]{:S(2)}, u32[]{:S(2)}) async-start(f32[16,4,256]{2,1,0:T(4,128)} %concatenate.3), calls=%async_computation.1 | async-start | bytes 131072 | tf_op jit(solution)/shard_map/all_to_all | solution.py:19
  22.8 8.8 %shard_map.50 = (f32[4,2,8,32,128]{4,3,2,1,0:T(8,128)}, f32[4,4,8,32,128]{4,3,2,1,0:T(8,128)}) custom-call(s32[32]{0:T(128)} %refs_0_.1, f32[32,4,4096]{2,1,0:T(4,128)} %refs_1_.1, f32[32,4,4096]{2,1,0:T(4,128)} %refs_2_.1), custom_call_target="tpu_custom_call" | custom-call | flops 20971520 | bytes 9437184 | tf_op jit(solution)/shard_map/pallas_call | solution.py:77
  31.7 0.0 copy-start
  31.7 0.0 all-to-all-done.1
  31.8 2.1 %multiply_reduce_fusion = f32[4,8,32,128]{3,2,1,0:T(8,128)S(1)} fusion(f32[4,4,8,32,128]{4,3,2,1,0:T(8,128)} %get-tuple-element.5, f32[4,4,8,128]{3,2,1,0:T(8,128)S(1)} %copy.38), kind=kLoop, calls=%fused_computation | loop fusion | flops 917504 | bytes 2686976 | tf_op jit(solution)/shard_map/reduce_sum | solution.py:125
  33.8 0.0 copy-done
  33.8 0.2 bitcast_add_fusion
  34.0 0.0 copy-start.1
  34.0 1.1 %pad_maximum_fusion = f32[4,2,8,32,128]{4,3,2,1,0:T(8,128)} fusion(f32[4,1,8,32,128]{4,3,2,1,0:T(8,128)S(1)} %get-tuple-element.7, f32[4,1,8,32,128]{4,3,2,1,0:T(8,128)S(1)} %get-tuple-element.6), kind=kLoop, calls=%fused_computation.2 | loop fusion | flops 262144 | bytes 2097152 | tf_op jit(solution)/shard_map/stack | solution.py:126
  35.1 3.5 %all-to-all-start.2 = ((f32[4,2,8,32,128]{4,3,2,1,0:T(8,128)}), f32[4,2,8,32,128]{4,3,2,1,0:T(8,128)S(1)}, u32[]{:S(2)}, u32[]{:S(2)}) async-start(f32[4,2,8,32,128]{4,3,2,1,0:T(8,128)} %pad_maximum_fusion), calls=%async_computation.2 | async-start | bytes 2097152 | tf_op jit(solution)/shard_map/all_to_all | solution.py:127
  38.6 0.0 copy-done.1
  38.7 15.6 %all-to-all-done.2 = f32[4,2,8,32,128]{4,3,2,1,0:T(8,128)S(1)} async-done(((f32[4,2,8,32,128]{4,3,2,1,0:T(8,128)}), f32[4,2,8,32,128]{4,3,2,1,0:T(8,128)S(1)}, u32[]{:S(2)}, u32[]{:S(2)}) %all-to-all-start.2) | async-done | bytes 1048608 | tf_op jit(solution)/shard_map/all_to_all | solution.py:127
  54.3 0.1 fusion.2
  54.5 20.8 %all_to_all.21 = f32[8,2,32,128]{3,2,1,0:T(8,128)S(1)} all-to-all(f32[8,2,32,128]{3,2,1,0:T(8,128)S(1)} %copy.39), channel_id=1, replica_groups=mesh['light'=16,'vz'=8,'vx'=4] {'vz'}, dimensions={0} | all-to-all | bytes 524288 | tf_op jit(solution)/shard_map/all_to_all | solution.py:130
  75.3 0.7 fusion.7
  76.0 0.6 slice_reduce_fusion.1
  (10 shorter events, 0.2 us)
Async XLA Ops:
  18.2 13.5 %all-to-all-start.1 = ((f32[16,4,256]{2,1,0:T(4,128)}), f32[16,4,256]{2,1,0:T(4,128)S(1)}, u32[]{:S(2)}, u32[]{:S(2)}) async-start(f32[16,4,256]{2,1,0:T(4,128)} %concatenate.3), calls=%async_computation.1 | async-start | bytes 131072 | tf_op jit(solution)/shard_map/all_to_all | solution.py:19
  31.7 2.2 %copy-start = (f32[4,2,8,32,128]{4,3,2,1,0:T(8,128)S(1)}, f32[4,2,8,32,128]{4,3,2,1,0:T(8,128)}, u32[]{:S(2)}) copy-start(f32[4,2,8,32,128]{4,3,2,1,0:T(8,128)} %get-tuple-element.4) | copy-start | bytes 3145732
  34.0 4.6 %copy-start.1 = (s32[32]{0:T(128)S(1)}, s32[32]{0:T(128)}, u32[]{:S(2)}) copy-start(s32[32]{0:T(128)} %refs_0_.1) | copy-start | bytes 388
  35.1 19.2 %all-to-all-start.2 = ((f32[4,2,8,32,128]{4,3,2,1,0:T(8,128)}), f32[4,2,8,32,128]{4,3,2,1,0:T(8,128)S(1)}, u32[]{:S(2)}, u32[]{:S(2)}) async-start(f32[4,2,8,32,128]{4,3,2,1,0:T(8,128)} %pad_maximum_fusion), calls=%async_computation.2 | async-start | bytes 2097152 | tf_op jit(solution)/shard_map/all_to_all | solution.py:127

commit v13 on v8

--- a/solution.py
+++ b/solution.py
@@ -14,8 +14,7 @@
     cells, columns = value.shape
     chunks = value.reshape(cells, count, columns // count).transpose(1, 0, 2)
     mine = lax.all_to_all(chunks, "light", 0, 0)
-    running = jnp.cumsum(mine, axis=0)
-    before = jnp.concatenate([jnp.zeros_like(running[:1]), running[:-1]], axis=0)
+    before = jnp.cumsum(mine, axis=0) - mine
     back = lax.all_to_all(before, "light", 0, 0)
     return back.transpose(1, 0, 2).reshape(cells, columns)
 

time: 76.8 us -> 76.8 us (level)
  no operation moved by 1% of the time
where the time goes in v13:
time: 76.8 us; the launch traced here: 76.3 us
  blocking collectives  35.6 us (46%)
  waiting for transfers between devices  15.6 us (20%)
  Pallas kernels  8.48 us (11%)
  starting transfers between devices  8.18 us (11%)
  other arithmetic  7.5 us (10%)
    all_to_all x1, blocking collectives, shards(): along_z = lax.all_to_all(jnp.stack([color_x, trans_x], axis=1), 'vz', 0, 0)  20.8 us
    all_to_all x1, waiting for transfers between devices, shards(): along_x = lax.all_to_all(stacked, 'vx', 0, 0)  15.6 us
    all_to_all x1, blocking collectives, light_prefix(): mine = lax.all_to_all(chunks, 'light', 0, 0)  14.8 us
    pallas_call x1, Pallas kernels, shade(): pl.pallas_call(body, grid=(tiles,), in_specs=[pl.BlockSpec(memory_space=p...  8.48 us
    all_to_all x1, starting transfers between devices, light_prefix(): back = lax.all_to_all(before, 'light', 0, 0)  4.66 us
    all_to_all x1, starting transfers between devices, shards(): along_x = lax.all_to_all(stacked, 'vx', 0, 0)  3.51 us
    reduce_sum x1, other arithmetic, shards(): color = unshaded[:, 0] + jnp.sum(light * parts, axis=0)  2.07 us
    reduce_sum x1, other arithmetic, shards(): slab_depth = jnp.sum(tau_light, axis=0)  2.04 us
  transfers between devices with their start and end apart: 2, of which 1 were waited for; matrix products, arithmetic and copies ran while one was open for 0% of the time, Pallas kernels for 11%

profile of v13, /device:TPU:8, one launch (start us, length us, event | category | flops | bytes accessed | tf_op | source)
XLA Modules:
  0.0 76.3 jit_solution(18180760250862362194)
XLA Ops:
  0.6 2.0 %multiply_reduce_fusion.1 = f32[4,4096]{1,0:T(4,128)S(1)} fusion(f32[32,4,4096]{2,1,0:T(4,128)} %refs_1_.1), kind=kLoop, calls=%fused_computation.1 | loop fusion | flops 1032192 | bytes 2162688 | tf_op jit(solution)/shard_map/reduce_sum | solution.py:104
  2.7 14.8 %all_to_all.20 = f32[16,4,256]{2,1,0:T(4,128)S(1)} all-to-all(f32[16,4,256]{2,1,0:T(4,128)S(1)} %bitcast.125), channel_id=1, replica_groups=mesh['light'=16,'vz'=8,'vx'=4] {'light'}, dimensions={0} | all-to-all | bytes 131072 | tf_op jit(solution)/shard_map/all_to_all | solution.py:16
  17.5 0.6 reduce-window_subtract_fusion
  18.1 4.7 %all-to-all-start.1 = ((f32[16,4,256]{2,1,0:T(4,128)}), f32[16,4,256]{2,1,0:T(4,128)S(1)}, u32[]{:S(2)}, u32[]{:S(2)}) async-start(f32[16,4,256]{2,1,0:T(4,128)} %reduce-window_subtract_fusion), calls=%async_computation.1 | async-start | bytes 131072 | tf_op jit(solution)/shard_map/all_to_all | solution.py:18
  22.8 8.5 %shard_map.50 = (f32[4,2,8,32,128]{4,3,2,1,0:T(8,128)}, f32[4,4,8,32,128]{4,3,2,1,0:T(8,128)}) custom-call(s32[32]{0:T(128)} %refs_0_.1, f32[32,4,4096]{2,1,0:T(4,128)} %refs_1_.1, f32[32,4,4096]{2,1,0:T(4,128)} %refs_2_.1), custom_call_target="tpu_custom_call" | custom-call | flops 20971520 | bytes 9437184 | tf_op jit(solution)/shard_map/pallas_call | solution.py:64
  31.3 0.0 copy-start
  31.3 0.0 all-to-all-done.1
  31.4 2.1 %multiply_reduce_fusion = f32[4,8,32,128]{3,2,1,0:T(8,128)S(1)} fusion(f32[4,4,8,32,128]{4,3,2,1,0:T(8,128)} %get-tuple-element.5, f32[4,4,8,128]{3,2,1,0:T(8,128)S(1)} %copy.38), kind=kLoop, calls=%fused_computation | loop fusion | flops 917504 | bytes 2686976 | tf_op jit(solution)/shard_map/reduce_sum | solution.py:112
  33.5 0.0 copy-done
  33.5 0.2 bitcast_add_fusion
  33.6 0.0 copy-start.1
  33.7 1.1 %pad_maximum_fusion = f32[4,2,8,32,128]{4,3,2,1,0:T(8,128)} fusion(f32[4,1,8,32,128]{4,3,2,1,0:T(8,128)S(1)} %get-tuple-element.7, f32[4,1,8,32,128]{4,3,2,1,0:T(8,128)S(1)} %get-tuple-element.6), kind=kLoop, calls=%fused_computation.3 | loop fusion | flops 262144 | bytes 2097152 | tf_op jit(solution)/shard_map/stack | solution.py:113
  34.8 3.5 %all-to-all-start.2 = ((f32[4,2,8,32,128]{4,3,2,1,0:T(8,128)}), f32[4,2,8,32,128]{4,3,2,1,0:T(8,128)S(1)}, u32[]{:S(2)}, u32[]{:S(2)}) async-start(f32[4,2,8,32,128]{4,3,2,1,0:T(8,128)} %pad_maximum_fusion), calls=%async_computation.2 | async-start | bytes 2097152 | tf_op jit(solution)/shard_map/all_to_all | solution.py:114
  38.3 0.0 copy-done.1
  38.3 15.6 %all-to-all-done.2 = f32[4,2,8,32,128]{4,3,2,1,0:T(8,128)S(1)} async-done(((f32[4,2,8,32,128]{4,3,2,1,0:T(8,128)}), f32[4,2,8,32,128]{4,3,2,1,0:T(8,128)S(1)}, u32[]{:S(2)}, u32[]{:S(2)}) %all-to-all-start.2) | async-done | bytes 1048608 | tf_op jit(solution)/shard_map/all_to_all | solution.py:114
  54.0 0.1 fusion.2
  54.2 20.8 %all_to_all.21 = f32[8,2,32,128]{3,2,1,0:T(8,128)S(1)} all-to-all(f32[8,2,32,128]{3,2,1,0:T(8,128)S(1)} %copy.39), channel_id=1, replica_groups=mesh['light'=16,'vz'=8,'vx'=4] {'vz'}, dimensions={0} | all-to-all | bytes 524288 | tf_op jit(solution)/shard_map/all_to_all | solution.py:117
  75.0 0.7 fusion.7
  75.6 0.6 slice_reduce_fusion.1
  (8 shorter events, 0.2 us)
Async XLA Ops:
  18.1 13.2 %all-to-all-start.1 = ((f32[16,4,256]{2,1,0:T(4,128)}), f32[16,4,256]{2,1,0:T(4,128)S(1)}, u32[]{:S(2)}, u32[]{:S(2)}) async-start(f32[16,4,256]{2,1,0:T(4,128)} %reduce-window_subtract_fusion), calls=%async_computation.1 | async-start | bytes 131072 | tf_op jit(solution)/shard_map/all_to_all | solution.py:18
  31.3 2.2 %copy-start = (f32[4,2,8,32,128]{4,3,2,1,0:T(8,128)S(1)}, f32[4,2,8,32,128]{4,3,2,1,0:T(8,128)}, u32[]{:S(2)}) copy-start(f32[4,2,8,32,128]{4,3,2,1,0:T(8,128)} %get-tuple-element.4) | copy-start | bytes 3145732
  33.6 4.6 %copy-start.1 = (s32[32]{0:T(128)S(1)}, s32[32]{0:T(128)}, u32[]{:S(2)}) copy-start(s32[32]{0:T(128)} %refs_0_.1) | copy-start | bytes 388
  34.8 19.2 %all-to-all-start.2 = ((f32[4,2,8,32,128]{4,3,2,1,0:T(8,128)}), f32[4,2,8,32,128]{4,3,2,1,0:T(8,128)S(1)}, u32[]{:S(2)}, u32[]{:S(2)}) async-start(f32[4,2,8,32,128]{4,3,2,1,0:T(8,128)} %pad_maximum_fusion), calls=%async_computation.2 | async-start | bytes 2097152 | tf_op jit(solution)/shard_map/all_to_all | solution.py:114

commit v14 on v13

--- a/solution.py
+++ b/solution.py
@@ -83,6 +83,26 @@
     )(facing, density, emission)
 
 
+def slab_kernel(dens_ref, out_ref, *, light_scale):
+    total = dens_ref[0] * light_scale
+    for l in range(1, dens_ref.shape[0]):
+        total = total + dens_ref[l] * light_scale
+    out_ref[...] = total
+
+
+def slab_depth_of(density, light_scale, tile=1024):
+    rows, cells, columns = density.shape
+    tile = min(tile, columns)
+    return pl.pallas_call(
+        lambda d, o: slab_kernel(d, o, light_scale=light_scale),
+        grid=(columns // tile,),
+        in_specs=[pl.BlockSpec((rows, cells, tile), lambda j: (0, 0, j))],
+        out_specs=pl.BlockSpec((cells, tile), lambda j: (0, j)),
+        out_shape=jax.ShapeDtypeStruct((cells, columns), jnp.float32),
+        cost_estimate=pl.CostEstimate(flops=2 * density.size, transcendentals=0, bytes_accessed=4 * density.size),
+    )(density)
+
+
 def composite(colors, transes, reversed_rows):
     count = colors.shape[0]
     forward = colors[count - 1]
@@ -100,8 +120,7 @@
     z_count = lax.axis_size("vz")
     x_count = lax.axis_size("vx")
     view_count = z_count * x_count
-    tau_light = density * (1.0 / (rows * light_count))
-    slab_depth = jnp.sum(tau_light, axis=0)
+    slab_depth = slab_depth_of(density, 1.0 / (rows * light_count))
     reversed_rows = facing == 1
     width = columns // view_count
     unshaded, parts = shade(

time: 76.8 us -> 78.4 us (1.021)
  Pallas kernels: 8.48 us -> 11.9 us
  other arithmetic: 7.5 us -> 5.46 us
    pallas_call x0 -> x1, Pallas kernels: none -> 3.42 us  [slab_depth_of(): pl.pallas_call(lambda d, o: slab_kernel(d, o, light_scale=light_scale), g...]
    reduce_sum x1 -> x0, other arithmetic: 2.04 us -> none  [shards(): slab_depth = jnp.sum(tau_light, axis=0)]
    all_to_all x1, blocking collectives: 14.8 us -> 15.7 us  [light_prefix(): mine = lax.all_to_all(chunks, 'light', 0, 0)]
where the time goes in v14:
time: 78.4 us; the launch traced here: 77.8 us
  blocking collectives  35.8 us (46%)
  waiting for transfers between devices  15.6 us (20%)
  Pallas kernels  11.9 us (15%)
  starting transfers between devices  8.18 us (10%)
  other arithmetic  5.46 us (7%)
    all_to_all x1, blocking collectives, shards(): along_z = lax.all_to_all(jnp.stack([color_x, trans_x], axis=1), 'vz', 0, 0)  20.1 us
    all_to_all x1, blocking collectives, light_prefix(): mine = lax.all_to_all(chunks, 'light', 0, 0)  15.7 us
    all_to_all x1, waiting for transfers between devices, shards(): along_x = lax.all_to_all(stacked, 'vx', 0, 0)  15.6 us
    pallas_call x1, Pallas kernels, shade(): pl.pallas_call(body, grid=(tiles,), in_specs=[pl.BlockSpec(memory_space=p...  8.48 us
    all_to_all x1, starting transfers between devices, light_prefix(): back = lax.all_to_all(before, 'light', 0, 0)  4.66 us
    all_to_all x1, starting transfers between devices, shards(): along_x = lax.all_to_all(stacked, 'vx', 0, 0)  3.51 us
    pallas_call x1, Pallas kernels, slab_depth_of(): pl.pallas_call(lambda d, o: slab_kernel(d, o, light_scale=light_scale), g...  3.42 us
    reduce_sum x1, other arithmetic, shards(): color = unshaded[:, 0] + jnp.sum(light * parts, axis=0)  2.07 us
  transfers between devices with their start and end apart: 2, of which 1 were waited for; matrix products, arithmetic and copies ran while one was open for 0% of the time, Pallas kernels for 11%

profile of v14, /device:TPU:8, one launch (start us, length us, event | category | flops | bytes accessed | tf_op | source)
XLA Modules:
  0.0 77.8 jit_solution(8609517618980044918)
XLA Ops:
  0.6 3.4 %shard_map.51 = f32[4,4096]{1,0:T(4,128)} custom-call(f32[32,4,4096]{2,1,0:T(4,128)} %d.1), custom_call_target="tpu_custom_call" | custom-call | flops 1048576 | bytes 2097152 | tf_op jit(solution)/shard_map/pallas_call | solution.py:96
  4.1 15.7 %all_to_all.20 = f32[16,4,256]{2,1,0:T(4,128)S(1)} all-to-all(f32[16,4,256]{2,1,0:T(4,128)} %bitcast.125), channel_id=1, replica_groups=mesh['light'=16,'vz'=8,'vx'=4] {'light'}, dimensions={0} | all-to-all | bytes 131072 | tf_op jit(solution)/shard_map/all_to_all | solution.py:16
  19.8 0.6 reduce-window_subtract_fusion
  20.4 4.7 %all-to-all-start.1 = ((f32[16,4,256]{2,1,0:T(4,128)}), f32[16,4,256]{2,1,0:T(4,128)S(1)}, u32[]{:S(2)}, u32[]{:S(2)}) async-start(f32[16,4,256]{2,1,0:T(4,128)} %reduce-window_subtract_fusion), calls=%async_computation.1 | async-start | bytes 131072 | tf_op jit(solution)/shard_map/all_to_all | solution.py:18
  25.1 8.5 %shard_map.50 = (f32[4,2,8,32,128]{4,3,2,1,0:T(8,128)}, f32[4,4,8,32,128]{4,3,2,1,0:T(8,128)}) custom-call(s32[32]{0:T(128)} %refs_0_.1, f32[32,4,4096]{2,1,0:T(4,128)} %d.1, f32[32,4,4096]{2,1,0:T(4,128)} %refs_2_.1), custom_call_target="tpu_custom_call" | custom-call | flops 20971520 | bytes 9437184 | tf_op jit(solution)/shard_map/pallas_call | solution.py:64
  33.5 0.0 copy-start
  33.5 0.0 all-to-all-done.1
  33.7 2.1 %multiply_reduce_fusion = f32[4,8,32,128]{3,2,1,0:T(8,128)S(1)} fusion(f32[4,4,8,32,128]{4,3,2,1,0:T(8,128)} %get-tuple-element.5, f32[4,4,8,128]{3,2,1,0:T(8,128)S(1)} %copy.41), kind=kLoop, calls=%fused_computation | loop fusion | flops 917504 | bytes 2686976 | tf_op jit(solution)/shard_map/reduce_sum | solution.py:131
  35.7 0.0 copy-done
  35.7 0.2 bitcast_add_fusion
  35.9 0.0 copy-start.1
  35.9 1.1 %pad_maximum_fusion = f32[4,2,8,32,128]{4,3,2,1,0:T(8,128)} fusion(f32[4,1,8,32,128]{4,3,2,1,0:T(8,128)S(1)} %get-tuple-element.7, f32[4,1,8,32,128]{4,3,2,1,0:T(8,128)S(1)} %get-tuple-element.6), kind=kLoop, calls=%fused_computation.2 | loop fusion | flops 262144 | bytes 2097152 | tf_op jit(solution)/shard_map/stack | solution.py:132
  37.0 3.5 %all-to-all-start.2 = ((f32[4,2,8,32,128]{4,3,2,1,0:T(8,128)}), f32[4,2,8,32,128]{4,3,2,1,0:T(8,128)S(1)}, u32[]{:S(2)}, u32[]{:S(2)}) async-start(f32[4,2,8,32,128]{4,3,2,1,0:T(8,128)} %pad_maximum_fusion), calls=%async_computation.2 | async-start | bytes 2097152 | tf_op jit(solution)/shard_map/all_to_all | solution.py:133
  40.5 0.0 copy-done.1
  40.6 15.6 %all-to-all-done.2 = f32[4,2,8,32,128]{4,3,2,1,0:T(8,128)S(1)} async-done(((f32[4,2,8,32,128]{4,3,2,1,0:T(8,128)}), f32[4,2,8,32,128]{4,3,2,1,0:T(8,128)S(1)}, u32[]{:S(2)}, u32[]{:S(2)}) %all-to-all-start.2) | async-done | bytes 1048608 | tf_op jit(solution)/shard_map/all_to_all | solution.py:133
  56.2 0.1 fusion.2
  56.4 20.1 %all_to_all.21 = f32[8,2,32,128]{3,2,1,0:T(8,128)S(1)} all-to-all(f32[8,2,32,128]{3,2,1,0:T(8,128)S(1)} %copy.42), channel_id=1, replica_groups=mesh['light'=16,'vz'=8,'vx'=4] {'vz'}, dimensions={0} | all-to-all | bytes 524288 | tf_op jit(solution)/shard_map/all_to_all | solution.py:136
  76.5 0.7 fusion.7
  77.2 0.6 slice_reduce_fusion.1
  (8 shorter events, 0.2 us)
Async XLA Ops:
  20.4 13.2 %all-to-all-start.1 = ((f32[16,4,256]{2,1,0:T(4,128)}), f32[16,4,256]{2,1,0:T(4,128)S(1)}, u32[]{:S(2)}, u32[]{:S(2)}) async-start(f32[16,4,256]{2,1,0:T(4,128)} %reduce-window_subtract_fusion), calls=%async_computation.1 | async-start | bytes 131072 | tf_op jit(solution)/shard_map/all_to_all | solution.py:18
  33.5 2.2 %copy-start = (f32[4,2,8,32,128]{4,3,2,1,0:T(8,128)S(1)}, f32[4,2,8,32,128]{4,3,2,1,0:T(8,128)}, u32[]{:S(2)}) copy-start(f32[4,2,8,32,128]{4,3,2,1,0:T(8,128)} %get-tuple-element.4) | copy-start | bytes 3145732
  35.9 4.6 %copy-start.1 = (s32[32]{0:T(128)S(1)}, s32[32]{0:T(128)}, u32[]{:S(2)}) copy-start(s32[32]{0:T(128)} %refs_0_.1) | copy-start | bytes 388
  37.0 19.2 %all-to-all-start.2 = ((f32[4,2,8,32,128]{4,3,2,1,0:T(8,128)}), f32[4,2,8,32,128]{4,3,2,1,0:T(8,128)S(1)}, u32[]{:S(2)}, u32[]{:S(2)}) async-start(f32[4,2,8,32,128]{4,3,2,1,0:T(8,128)} %pad_maximum_fusion), calls=%async_computation.2 | async-start | bytes 2097152 | tf_op jit(solution)/shard_map/all_to_all | solution.py:133

commit v15 on v13

--- a/solution.py
+++ b/solution.py
@@ -53,7 +53,7 @@
                 part_ref[v, b, 0, pl.ds(l, 1), :] = (weight[v] * shaded[v:v + 1])[:, cut]
         return depth + tau_light
 
-    lax.fori_loop(0, rows, row, jnp.zeros(dens_ref.shape[1:], jnp.float32), unroll=8)
+    lax.fori_loop(0, rows, row, jnp.zeros(dens_ref.shape[1:], jnp.float32), unroll=True)
 
 
 def shade(facing, density, emission, light_scale, view_scale, blocks, width):

time: 76.8 us -> 76.7 us (level)
  no operation moved by 1% of the time
where the time goes in v15:
time: 76.7 us; the launch traced here: 76.2 us
  blocking collectives  35.6 us (46%)
  waiting for transfers between devices  15.6 us (20%)
  Pallas kernels  8.4 us (11%)
  starting transfers between devices  8.18 us (11%)
  other arithmetic  7.5 us (10%)
    all_to_all x1, blocking collectives, shards(): along_z = lax.all_to_all(jnp.stack([color_x, trans_x], axis=1), 'vz', 0, 0)  20.8 us
    all_to_all x1, waiting for transfers between devices, shards(): along_x = lax.all_to_all(stacked, 'vx', 0, 0)  15.6 us
    all_to_all x1, blocking collectives, light_prefix(): mine = lax.all_to_all(chunks, 'light', 0, 0)  14.8 us
    pallas_call x1, Pallas kernels, shade(): pl.pallas_call(body, grid=(tiles,), in_specs=[pl.BlockSpec(memory_space=p...  8.4 us
    all_to_all x1, starting transfers between devices, light_prefix(): back = lax.all_to_all(before, 'light', 0, 0)  4.66 us
    all_to_all x1, starting transfers between devices, shards(): along_x = lax.all_to_all(stacked, 'vx', 0, 0)  3.51 us
    reduce_sum x1, other arithmetic, shards(): color = unshaded[:, 0] + jnp.sum(light * parts, axis=0)  2.07 us
    reduce_sum x1, other arithmetic, shards(): slab_depth = jnp.sum(tau_light, axis=0)  2.04 us
  transfers between devices with their start and end apart: 2, of which 1 were waited for; matrix products, arithmetic and copies ran while one was open for 0% of the time, Pallas kernels for 11%

profile of v15, /device:TPU:8, one launch (start us, length us, event | category | flops | bytes accessed | tf_op | source)
XLA Modules:
  0.0 76.2 jit_solution(15666968010488463162)
XLA Ops:
  0.6 2.0 %multiply_reduce_fusion.1 = f32[4,4096]{1,0:T(4,128)S(1)} fusion(f32[32,4,4096]{2,1,0:T(4,128)} %refs_1_.1), kind=kLoop, calls=%fused_computation.1 | loop fusion | flops 1032192 | bytes 2162688 | tf_op jit(solution)/shard_map/reduce_sum | solution.py:104
  2.7 14.8 %all_to_all.20 = f32[16,4,256]{2,1,0:T(4,128)S(1)} all-to-all(f32[16,4,256]{2,1,0:T(4,128)S(1)} %bitcast.125), channel_id=1, replica_groups=mesh['light'=16,'vz'=8,'vx'=4] {'light'}, dimensions={0} | all-to-all | bytes 131072 | tf_op jit(solution)/shard_map/all_to_all | solution.py:16
  17.5 0.6 reduce-window_subtract_fusion
  18.1 4.7 %all-to-all-start.1 = ((f32[16,4,256]{2,1,0:T(4,128)}), f32[16,4,256]{2,1,0:T(4,128)S(1)}, u32[]{:S(2)}, u32[]{:S(2)}) async-start(f32[16,4,256]{2,1,0:T(4,128)} %reduce-window_subtract_fusion), calls=%async_computation.1 | async-start | bytes 131072 | tf_op jit(solution)/shard_map/all_to_all | solution.py:18
  22.8 8.4 %shard_map.50 = (f32[4,2,8,32,128]{4,3,2,1,0:T(8,128)}, f32[4,4,8,32,128]{4,3,2,1,0:T(8,128)}) custom-call(s32[32]{0:T(128)} %refs_0_.1, f32[32,4,4096]{2,1,0:T(4,128)} %refs_1_.1, f32[32,4,4096]{2,1,0:T(4,128)} %refs_2_.1), custom_call_target="tpu_custom_call" | custom-call | flops 20971520 | bytes 9437184 | tf_op jit(solution)/shard_map/pallas_call | solution.py:64
  31.2 0.0 copy-start
  31.2 0.0 all-to-all-done.1
  31.3 2.1 %multiply_reduce_fusion = f32[4,8,32,128]{3,2,1,0:T(8,128)S(1)} fusion(f32[4,4,8,32,128]{4,3,2,1,0:T(8,128)} %get-tuple-element.5, f32[4,4,8,128]{3,2,1,0:T(8,128)S(1)} %copy.38), kind=kLoop, calls=%fused_computation | loop fusion | flops 917504 | bytes 2686976 | tf_op jit(solution)/shard_map/reduce_sum | solution.py:112
  33.4 0.0 copy-done
  33.4 0.2 bitcast_add_fusion
  33.6 0.0 copy-start.1
  33.6 1.1 %pad_maximum_fusion = f32[4,2,8,32,128]{4,3,2,1,0:T(8,128)} fusion(f32[4,1,8,32,128]{4,3,2,1,0:T(8,128)S(1)} %get-tuple-element.7, f32[4,1,8,32,128]{4,3,2,1,0:T(8,128)S(1)} %get-tuple-element.6), kind=kLoop, calls=%fused_computation.3 | loop fusion | flops 262144 | bytes 2097152 | tf_op jit(solution)/shard_map/stack | solution.py:113
  34.7 3.5 %all-to-all-start.2 = ((f32[4,2,8,32,128]{4,3,2,1,0:T(8,128)}), f32[4,2,8,32,128]{4,3,2,1,0:T(8,128)S(1)}, u32[]{:S(2)}, u32[]{:S(2)}) async-start(f32[4,2,8,32,128]{4,3,2,1,0:T(8,128)} %pad_maximum_fusion), calls=%async_computation.2 | async-start | bytes 2097152 | tf_op jit(solution)/shard_map/all_to_all | solution.py:114
  38.2 0.0 copy-done.1
  38.2 15.6 %all-to-all-done.2 = f32[4,2,8,32,128]{4,3,2,1,0:T(8,128)S(1)} async-done(((f32[4,2,8,32,128]{4,3,2,1,0:T(8,128)}), f32[4,2,8,32,128]{4,3,2,1,0:T(8,128)S(1)}, u32[]{:S(2)}, u32[]{:S(2)}) %all-to-all-start.2) | async-done | bytes 1048608 | tf_op jit(solution)/shard_map/all_to_all | solution.py:114
  53.9 0.1 fusion.2
  54.1 20.8 %all_to_all.21 = f32[8,2,32,128]{3,2,1,0:T(8,128)S(1)} all-to-all(f32[8,2,32,128]{3,2,1,0:T(8,128)S(1)} %copy.39), channel_id=1, replica_groups=mesh['light'=16,'vz'=8,'vx'=4] {'vz'}, dimensions={0} | all-to-all | bytes 524288 | tf_op jit(solution)/shard_map/all_to_all | solution.py:117
  74.9 0.7 fusion.7
  75.6 0.6 slice_reduce_fusion.1
  (8 shorter events, 0.2 us)
Async XLA Ops:
  18.1 13.1 %all-to-all-start.1 = ((f32[16,4,256]{2,1,0:T(4,128)}), f32[16,4,256]{2,1,0:T(4,128)S(1)}, u32[]{:S(2)}, u32[]{:S(2)}) async-start(f32[16,4,256]{2,1,0:T(4,128)} %reduce-window_subtract_fusion), calls=%async_computation.1 | async-start | bytes 131072 | tf_op jit(solution)/shard_map/all_to_all | solution.py:18
  31.2 2.2 %copy-start = (f32[4,2,8,32,128]{4,3,2,1,0:T(8,128)S(1)}, f32[4,2,8,32,128]{4,3,2,1,0:T(8,128)}, u32[]{:S(2)}) copy-start(f32[4,2,8,32,128]{4,3,2,1,0:T(8,128)} %get-tuple-element.4) | copy-start | bytes 3145732
  33.6 4.6 %copy-start.1 = (s32[32]{0:T(128)S(1)}, s32[32]{0:T(128)}, u32[]{:S(2)}) copy-start(s32[32]{0:T(128)} %refs_0_.1) | copy-start | bytes 388
  34.7 19.2 %all-to-all-start.2 = ((f32[4,2,8,32,128]{4,3,2,1,0:T(8,128)}), f32[4,2,8,32,128]{4,3,2,1,0:T(8,128)S(1)}, u32[]{:S(2)}, u32[]{:S(2)}) async-start(f32[4,2,8,32,128]{4,3,2,1,0:T(8,128)} %pad_maximum_fusion), calls=%async_computation.2 | async-start | bytes 2097152 | tf_op jit(solution)/shard_map/all_to_all | solution.py:114

commit v16 on v10

--- a/solution.py
+++ b/solution.py
@@ -14,8 +14,7 @@
     cells, columns = value.shape
     chunks = value.reshape(cells, count, columns // count).transpose(1, 0, 2)
     mine = lax.all_to_all(chunks, "light", 0, 0)
-    running = jnp.cumsum(mine, axis=0)
-    before = jnp.concatenate([jnp.zeros_like(running[:1]), running[:-1]], axis=0)
+    before = jnp.cumsum(mine, axis=0) - mine
     back = lax.all_to_all(before, "light", 0, 0)
     return back.transpose(1, 0, 2).reshape(cells, columns)
 
@@ -85,23 +84,24 @@
 
 
 def lit_kernel(light_ref, parts_ref, unshaded_ref, out_ref):
-    total = unshaded_ref[:, 0]
+    b = pl.program_id(0)
+    total = unshaded_ref[0, 0]
     for v in range(parts_ref.shape[0]):
-        total = total + light_ref[v] * parts_ref[v]
-    out_ref[:, 0] = total
+        total = total + light_ref[v, b] * parts_ref[v, 0]
+    out_ref[0, 0] = total
 
 
 def apply_light(light, parts, unshaded):
     cells, blocks, tiles, rows, width = parts.shape
     return pl.pallas_call(
         lit_kernel,
-        grid=(tiles,),
+        grid=(blocks,),
         in_specs=[
-            pl.BlockSpec((cells, blocks, 1, 1, width), lambda j: (0, 0, j, 0, 0)),
-            pl.BlockSpec((cells, blocks, 1, rows, width), lambda j: (0, 0, j, 0, 0)),
-            pl.BlockSpec((blocks, 1, 1, rows, width), lambda j: (0, 0, j, 0, 0)),
+            pl.BlockSpec(light.shape, lambda b: (0, 0, 0, 0, 0)),
+            pl.BlockSpec((cells, 1, tiles, rows, width), lambda b: (0, b, 0, 0, 0)),
+            pl.BlockSpec((1, 1, tiles, rows, width), lambda b: (b, 0, 0, 0, 0)),
         ],
-        out_specs=pl.BlockSpec((blocks, 1, 1, rows, width), lambda j: (0, 0, j, 0, 0)),
+        out_specs=pl.BlockSpec((1, 1, tiles, rows, width), lambda b: (b, 0, 0, 0, 0)),
         out_shape=jax.ShapeDtypeStruct(unshaded.shape, unshaded.dtype),
         input_output_aliases={2: 0},
         cost_estimate=pl.CostEstimate(

time: 79.6 us -> 77.7 us (0.976)
  Pallas kernels: 13.9 us -> 12.1 us
    pallas_call x1, Pallas kernels: 5.4 us -> 3.57 us  [apply_light(): pl.pallas_call(lit_kernel, grid=(blocks,), in_specs=[pl.BlockSpec(light.s...]
where the time goes in v16:
time: 77.7 us; the launch traced here: 77.1 us
  blocking collectives  35.6 us (46%)
  waiting for transfers between devices  15.6 us (20%)
  Pallas kernels  12.1 us (16%)
  starting transfers between devices  8.18 us (11%)
  other arithmetic  4.17 us (5%)
    all_to_all x1, blocking collectives, shards(): along_z = lax.all_to_all(jnp.stack([color_x, trans_x], axis=1), 'vz', 0, 0)  20.8 us
    all_to_all x1, waiting for transfers between devices, shards(): along_x = lax.all_to_all(stacked, 'vx', 0, 0)  15.6 us
    all_to_all x1, blocking collectives, light_prefix(): mine = lax.all_to_all(chunks, 'light', 0, 0)  14.8 us
    pallas_call x1, Pallas kernels, shade(): pl.pallas_call(body, grid=(tiles,), in_specs=[pl.BlockSpec(memory_space=p...  8.48 us
    all_to_all x1, starting transfers between devices, light_prefix(): back = lax.all_to_all(before, 'light', 0, 0)  4.66 us
    pallas_call x1, Pallas kernels, apply_light(): pl.pallas_call(lit_kernel, grid=(blocks,), in_specs=[pl.BlockSpec(light.s...  3.57 us
    all_to_all x1, starting transfers between devices, shards(): along_x = lax.all_to_all(stacked, 'vx', 0, 0)  3.51 us
    reduce_sum x1, other arithmetic, shards(): slab_depth = jnp.sum(tau_light, axis=0)  2.04 us
  transfers between devices with their start and end apart: 2, of which 1 were waited for; matrix products, arithmetic and copies ran while one was open for 0% of the time, Pallas kernels for 11%

profile of v16, /device:TPU:8, one launch (start us, length us, event | category | flops | bytes accessed | tf_op | source)
XLA Modules:
  0.0 77.1 jit_solution(3537953520177258455)
XLA Ops:
  0.6 2.0 %multiply_reduce_fusion = f32[4,4096]{1,0:T(4,128)S(1)} fusion(f32[32,4,4096]{2,1,0:T(4,128)} %refs_1_.1), kind=kLoop, calls=%fused_computation | loop fusion | flops 1032192 | bytes 2162688 | tf_op jit(solution)/shard_map/reduce_sum | solution.py:131
  2.7 14.8 %all_to_all.20 = f32[16,4,256]{2,1,0:T(4,128)S(1)} all-to-all(f32[16,4,256]{2,1,0:T(4,128)S(1)} %bitcast.124), channel_id=1, replica_groups=mesh['light'=16,'vz'=8,'vx'=4] {'light'}, dimensions={0} | all-to-all | bytes 131072 | tf_op jit(solution)/shard_map/all_to_all | solution.py:16
  17.5 0.6 reduce-window_subtract_fusion
  18.1 4.7 %all-to-all-start.1 = ((f32[16,4,256]{2,1,0:T(4,128)}), f32[16,4,256]{2,1,0:T(4,128)S(1)}, u32[]{:S(2)}, u32[]{:S(2)}) async-start(f32[16,4,256]{2,1,0:T(4,128)} %reduce-window_subtract_fusion), calls=%async_computation.1 | async-start | bytes 131072 | tf_op jit(solution)/shard_map/all_to_all | solution.py:18
  22.8 8.5 %shard_map.50 = (f32[4,2,8,32,128]{4,3,2,1,0:T(8,128)}, f32[4,4,8,32,128]{4,3,2,1,0:T(8,128)}) custom-call(s32[32]{0:T(128)} %refs_0_.1, f32[32,4,4096]{2,1,0:T(4,128)} %refs_1_.1, f32[32,4,4096]{2,1,0:T(4,128)} %refs_2_.1), custom_call_target="tpu_custom_call" | custom-call | flops 20971520 | bytes 9437184 | tf_op jit(solution)/shard_map/pallas_call | solution.py:64
  31.3 0.0 all-to-all-done.1
  31.4 0.7 copy.42
  32.1 0.0 copy-start
  32.1 3.6 %shard_map.51 = f32[4,2,8,32,128]{4,3,2,1,0:T(8,128)} custom-call(f32[4,4,8,1,128]{4,3,2,1,0:T(1,128)} %bitcast.123, f32[4,4,8,32,128]{4,3,2,1,0:T(8,128)} %get-tuple-element.4.parts_ref, f32[4,2,8,32,128]{4,3,2,1,0:T(8,128)} %get-tuple-element.5.unshaded_ref), custom_call_target="tpu_custom_call", output_to_operand_aliasing={{}: (2, {})} | custom-call | flops 1048576 | bytes 3145728 | tf_op jit(solution)/shard_map/pallas_call | solution.py:96
  35.6 3.5 %all-to-all-start.2 = ((f32[4,2,8,32,128]{4,3,2,1,0:T(8,128)}), f32[4,2,8,32,128]{4,3,2,1,0:T(8,128)S(1)}, u32[]{:S(2)}, u32[]{:S(2)}) async-start(f32[4,2,8,32,128]{4,3,2,1,0:T(8,128)} %shard_map.51), calls=%async_computation.2 | async-start | bytes 2097152 | tf_op jit(solution)/shard_map/all_to_all | solution.py:140
  39.2 0.0 copy-done
  39.2 15.6 %all-to-all-done.2 = f32[4,2,8,32,128]{4,3,2,1,0:T(8,128)S(1)} async-done(((f32[4,2,8,32,128]{4,3,2,1,0:T(8,128)}), f32[4,2,8,32,128]{4,3,2,1,0:T(8,128)S(1)}, u32[]{:S(2)}, u32[]{:S(2)}) %all-to-all-start.2) | async-done | bytes 1048608 | tf_op jit(solution)/shard_map/all_to_all | solution.py:140
  54.9 0.1 fusion.2
  55.0 20.8 %all_to_all.21 = f32[8,2,32,128]{3,2,1,0:T(8,128)S(1)} all-to-all(f32[8,2,32,128]{3,2,1,0:T(8,128)S(1)} %copy.40), channel_id=1, replica_groups=mesh['light'=16,'vz'=8,'vx'=4] {'vz'}, dimensions={0} | all-to-all | bytes 524288 | tf_op jit(solution)/shard_map/all_to_all | solution.py:143
  75.8 0.7 fusion.7
  76.5 0.6 slice_reduce_fusion.1
  (7 shorter events, 0.2 us)
Async XLA Ops:
  18.1 13.1 %all-to-all-start.1 = ((f32[16,4,256]{2,1,0:T(4,128)}), f32[16,4,256]{2,1,0:T(4,128)S(1)}, u32[]{:S(2)}, u32[]{:S(2)}) async-start(f32[16,4,256]{2,1,0:T(4,128)} %reduce-window_subtract_fusion), calls=%async_computation.1 | async-start | bytes 131072 | tf_op jit(solution)/shard_map/all_to_all | solution.py:18
  32.1 7.1 %copy-start = (s32[32]{0:T(128)S(1)}, s32[32]{0:T(128)}, u32[]{:S(2)}) copy-start(s32[32]{0:T(128)} %refs_0_.1) | copy-start | bytes 388
  35.6 19.2 %all-to-all-start.2 = ((f32[4,2,8,32,128]{4,3,2,1,0:T(8,128)}), f32[4,2,8,32,128]{4,3,2,1,0:T(8,128)S(1)}, u32[]{:S(2)}, u32[]{:S(2)}) async-start(f32[4,2,8,32,128]{4,3,2,1,0:T(8,128)} %shard_map.51), calls=%async_computation.2 | async-start | bytes 2097152 | tf_op jit(solution)/shard_map/all_to_all | solution.py:140

commit v17 on v13

--- a/solution.py
+++ b/solution.py
@@ -126,7 +126,8 @@
     if any(c is None for c in coords):
         return 1
     first_z = coords[0][2]
-    return sum(1 for c in coords if c[2] == first_z)
+    x_extent = sum(1 for c in coords if c[2] == first_z)
+    return 2 * x_extent if len(row) % (2 * x_extent) == 0 else x_extent
 
 
 def solution(mesh):

time: 76.8 us -> 74 us (0.964)
  blocking collectives: 35.6 us -> 33.2 us
  starting transfers between devices: 8.18 us -> 9.89 us
  Pallas kernels: 8.48 us -> 7.12 us
    all_to_all x1, blocking collectives: 20.8 us -> 18.3 us  [shards(): along_z = lax.all_to_all(jnp.stack([color_x, trans_x], axis=1), 'vz', 0, 0)]
    all_to_all x1, starting transfers between devices: 3.51 us -> 5.23 us  [shards(): along_x = lax.all_to_all(stacked, 'vx', 0, 0)]
    pallas_call x1, Pallas kernels: 8.48 us -> 7.12 us  [shade(): pl.pallas_call(body, grid=(tiles,), in_specs=[pl.BlockSpec(memory_space=p...]
  transfers between devices with their start and end apart: 2 -> 2, of which waited for: 1 -> 1; matrix products, arithmetic and copies ran while one was open for 0% -> 0% of each run, Pallas kernels for 11% -> 10%
where the time goes in v17:
time: 74 us; the launch traced here: 73.5 us
  blocking collectives  33.2 us (45%)
  waiting for transfers between devices  15.1 us (20%)
  starting transfers between devices  9.89 us (13%)
  other arithmetic  7.45 us (10%)
  Pallas kernels  7.12 us (10%)
    all_to_all x1, blocking collectives, shards(): along_z = lax.all_to_all(jnp.stack([color_x, trans_x], axis=1), 'vz', 0, 0)  18.3 us
    all_to_all x1, waiting for transfers between devices, shards(): along_x = lax.all_to_all(stacked, 'vx', 0, 0)  15.1 us
    all_to_all x1, blocking collectives, light_prefix(): mine = lax.all_to_all(chunks, 'light', 0, 0)  14.8 us
    pallas_call x1, Pallas kernels, shade(): pl.pallas_call(body, grid=(tiles,), in_specs=[pl.BlockSpec(memory_space=p...  7.12 us
    all_to_all x1, starting transfers between devices, shards(): along_x = lax.all_to_all(stacked, 'vx', 0, 0)  5.23 us
    all_to_all x1, starting transfers between devices, light_prefix(): back = lax.all_to_all(before, 'light', 0, 0)  4.66 us
    reduce_sum x1, other arithmetic, shards(): color = unshaded[:, 0] + jnp.sum(light * parts, axis=0)  2.05 us
    reduce_sum x1, other arithmetic, shards(): slab_depth = jnp.sum(tau_light, axis=0)  2.04 us
  transfers between devices with their start and end apart: 2, of which 1 were waited for; matrix products, arithmetic and copies ran while one was open for 0% of the time, Pallas kernels for 10%

profile of v17, /device:TPU:8, one launch (start us, length us, event | category | flops | bytes accessed | tf_op | source)
XLA Modules:
  0.0 73.5 jit_solution(6155518198172359113)
XLA Ops:
  0.6 2.0 %multiply_reduce_fusion.1 = f32[4,4096]{1,0:T(4,128)S(1)} fusion(f32[32,4,4096]{2,1,0:T(4,128)} %refs_1_.1), kind=kLoop, calls=%fused_computation.1 | loop fusion | flops 1032192 | bytes 2162688 | tf_op jit(solution)/shard_map/reduce_sum | solution.py:104
  2.7 14.8 %all_to_all.20 = f32[16,4,256]{2,1,0:T(4,128)S(1)} all-to-all(f32[16,4,256]{2,1,0:T(4,128)S(1)} %bitcast.124), channel_id=1, replica_groups=mesh['light'=16,'vz'=4,'vx'=8] {'light'}, dimensions={0} | all-to-all | bytes 131072 | tf_op jit(solution)/shard_map/all_to_all | solution.py:16
  17.5 0.6 reduce-window_subtract_fusion
  18.1 4.7 %all-to-all-start.1 = ((f32[16,4,256]{2,1,0:T(4,128)}), f32[16,4,256]{2,1,0:T(4,128)S(1)}, u32[]{:S(2)}, u32[]{:S(2)}) async-start(f32[16,4,256]{2,1,0:T(4,128)} %reduce-window_subtract_fusion), calls=%async_computation.1 | async-start | bytes 131072 | tf_op jit(solution)/shard_map/all_to_all | solution.py:18
  22.8 7.1 %shard_map.50 = (f32[8,2,4,32,128]{4,3,2,1,0:T(8,128)}, f32[4,8,4,32,128]{4,3,2,1,0:T(8,128)}) custom-call(s32[32]{0:T(128)} %refs_0_.1, f32[32,4,4096]{2,1,0:T(4,128)} %refs_1_.1, f32[32,4,4096]{2,1,0:T(4,128)} %refs_2_.1), custom_call_target="tpu_custom_call" | custom-call | flops 20971520 | bytes 9437184 | tf_op jit(solution)/shard_map/pallas_call | solution.py:64
  29.9 0.0 copy-start
  29.9 0.0 all-to-all-done.1
  30.0 2.1 %multiply_reduce_fusion = f32[8,4,32,128]{3,2,1,0:T(8,128)S(1)} fusion(f32[4,8,4,32,128]{4,3,2,1,0:T(8,128)} %get-tuple-element.5, f32[4,8,4,128]{3,2,1,0:T(4,128)S(1)} %copy.22), kind=kLoop, calls=%fused_computation | loop fusion | flops 917504 | bytes 2686976 | tf_op jit(solution)/shard_map/reduce_sum | solution.py:112
  32.1 0.0 copy-done
  32.1 0.2 bitcast_add_fusion
  32.3 0.0 copy-start.1
  32.3 1.1 %pad_maximum_fusion = f32[8,2,4,32,128]{4,3,2,1,0:T(8,128)} fusion(f32[8,1,4,32,128]{4,3,2,1,0:T(8,128)S(1)} %get-tuple-element.7, f32[8,1,4,32,128]{4,3,2,1,0:T(8,128)S(1)} %get-tuple-element.6), kind=kLoop, calls=%fused_computation.3 | loop fusion | flops 262144 | bytes 2097152 | tf_op jit(solution)/shard_map/stack | solution.py:113
  33.4 5.2 %all-to-all-start.2 = ((f32[8,2,4,32,128]{4,3,2,1,0:T(8,128)}), f32[8,2,4,32,128]{4,3,2,1,0:T(8,128)S(1)}, u32[]{:S(2)}, u32[]{:S(2)}) async-start(f32[8,2,4,32,128]{4,3,2,1,0:T(8,128)} %pad_maximum_fusion), calls=%async_computation.2 | async-start | bytes 2097152 | tf_op jit(solution)/shard_map/all_to_all | solution.py:114
  38.6 0.0 copy-done.1
  38.6 15.1 %all-to-all-done.2 = f32[8,2,4,32,128]{4,3,2,1,0:T(8,128)S(1)} async-done(((f32[8,2,4,32,128]{4,3,2,1,0:T(8,128)}), f32[8,2,4,32,128]{4,3,2,1,0:T(8,128)S(1)}, u32[]{:S(2)}, u32[]{:S(2)}) %all-to-all-start.2) | async-done | bytes 1048608 | tf_op jit(solution)/shard_map/all_to_all | solution.py:114
  53.7 0.1 fusion.2
  53.9 18.3 %all_to_all.21 = f32[4,2,32,128]{3,2,1,0:T(8,128)S(1)} all-to-all(f32[4,2,32,128]{3,2,1,0:T(8,128)S(1)} %copy.23), channel_id=1, replica_groups=mesh['light'=16,'vz'=4,'vx'=8] {'vz'}, dimensions={0} | all-to-all | bytes 262144 | tf_op jit(solution)/shard_map/all_to_all | solution.py:117
  72.2 0.7 fusion.7
  72.9 0.6 slice_reduce_fusion.1
  (8 shorter events, 0.1 us)
Async XLA Ops:
  18.1 11.8 %all-to-all-start.1 = ((f32[16,4,256]{2,1,0:T(4,128)}), f32[16,4,256]{2,1,0:T(4,128)S(1)}, u32[]{:S(2)}, u32[]{:S(2)}) async-start(f32[16,4,256]{2,1,0:T(4,128)} %reduce-window_subtract_fusion), calls=%async_computation.1 | async-start | bytes 131072 | tf_op jit(solution)/shard_map/all_to_all | solution.py:18
  29.9 2.2 %copy-start = (f32[8,2,4,32,128]{4,3,2,1,0:T(8,128)S(1)}, f32[8,2,4,32,128]{4,3,2,1,0:T(8,128)}, u32[]{:S(2)}) copy-start(f32[8,2,4,32,128]{4,3,2,1,0:T(8,128)} %get-tuple-element.4) | copy-start | bytes 3145732
  32.3 6.3 %copy-start.1 = (s32[32]{0:T(128)S(1)}, s32[32]{0:T(128)}, u32[]{:S(2)}) copy-start(s32[32]{0:T(128)} %refs_0_.1) | copy-start | bytes 388
  33.4 20.3 %all-to-all-start.2 = ((f32[8,2,4,32,128]{4,3,2,1,0:T(8,128)}), f32[8,2,4,32,128]{4,3,2,1,0:T(8,128)S(1)}, u32[]{:S(2)}, u32[]{:S(2)}) async-start(f32[8,2,4,32,128]{4,3,2,1,0:T(8,128)} %pad_maximum_fusion), calls=%async_computation.2 | async-start | bytes 2097152 | tf_op jit(solution)/shard_map/all_to_all | solution.py:114

commit v18 on v17

--- a/solution.py
+++ b/solution.py
@@ -127,7 +127,7 @@
         return 1
     first_z = coords[0][2]
     x_extent = sum(1 for c in coords if c[2] == first_z)
-    return 2 * x_extent if len(row) % (2 * x_extent) == 0 else x_extent
+    return 4 * x_extent if len(row) % (4 * x_extent) == 0 else x_extent
 
 
 def solution(mesh):

time: 74 us -> 85.9 us (1.16)
  the two profiles are of different devices: /device:TPU:8 before, /device:TPU:64 now
where the time goes in v18:
time: 85.9 us; the launch traced here: 85.5 us
  blocking collectives  30.5 us (36%)
  waiting for transfers between devices  26.7 us (31%)
  starting transfers between devices  12.9 us (15%)
  other arithmetic  7.35 us (9%)
  Pallas kernels  7.25 us (8%)
    all_to_all x1, waiting for transfers between devices, shards(): along_x = lax.all_to_all(stacked, 'vx', 0, 0)  26.2 us
    all_to_all x1, blocking collectives, shards(): along_z = lax.all_to_all(jnp.stack([color_x, trans_x], axis=1), 'vz', 0, 0)  15.6 us
    all_to_all x1, blocking collectives, light_prefix(): mine = lax.all_to_all(chunks, 'light', 0, 0)  14.9 us
    all_to_all x1, starting transfers between devices, shards(): along_x = lax.all_to_all(stacked, 'vx', 0, 0)  9.41 us
    pallas_call x1, Pallas kernels, shade(): pl.pallas_call(body, grid=(tiles,), in_specs=[pl.BlockSpec(memory_space=p...  7.25 us
    all_to_all x1, starting transfers between devices, light_prefix(): back = lax.all_to_all(before, 'light', 0, 0)  3.5 us
    reduce_sum x1, other arithmetic, shards(): slab_depth = jnp.sum(tau_light, axis=0)  2.04 us
    reduce_sum x1, other arithmetic, shards(): color = unshaded[:, 0] + jnp.sum(light * parts, axis=0)  1.98 us
  transfers between devices with their start and end apart: 2, of which 2 were waited for; matrix products, arithmetic and copies ran while one was open for 0% of the time, Pallas kernels for 8%

profile of v18, /device:TPU:64, one launch (start us, length us, event | category | flops | bytes accessed | tf_op | source)
XLA Modules:
  0.0 85.5 jit_solution(14272483963595076992)
XLA Ops:
  0.6 2.0 %multiply_reduce_fusion.1 = f32[4,4096]{1,0:T(4,128)S(1)} fusion(f32[32,4,4096]{2,1,0:T(4,128)} %refs_1_.1), kind=kLoop, calls=%fused_computation.1 | loop fusion | flops 1032192 | bytes 2162688 | tf_op jit(solution)/shard_map/reduce_sum | solution.py:104
  2.7 14.9 %all_to_all.20 = f32[16,4,256]{2,1,0:T(4,128)S(1)} all-to-all(f32[16,4,256]{2,1,0:T(4,128)S(1)} %bitcast.172), channel_id=1, replica_groups=mesh['light'=16,'vz'=2,'vx'=16] {'light'}, dimensions={0} | all-to-all | bytes 131072 | tf_op jit(solution)/shard_map/all_to_all | solution.py:16
  17.5 0.6 reduce-window_subtract_fusion
  18.2 3.5 %all-to-all-start.1 = ((f32[16,4,256]{2,1,0:T(4,128)}), f32[16,4,256]{2,1,0:T(4,128)S(1)}, u32[]{:S(2)}, u32[]{:S(2)}) async-start(f32[16,4,256]{2,1,0:T(4,128)} %reduce-window_subtract_fusion), calls=%async_computation.1 | async-start | bytes 131072 | tf_op jit(solution)/shard_map/all_to_all | solution.py:18
  21.7 7.2 %shard_map.50 = (f32[16,2,2,32,128]{4,3,2,1,0:T(8,128)}, f32[4,16,2,32,128]{4,3,2,1,0:T(8,128)}) custom-call(s32[32]{0:T(128)} %refs_0_.1, f32[32,4,4096]{2,1,0:T(4,128)} %refs_1_.1, f32[32,4,4096]{2,1,0:T(4,128)} %refs_2_.1), custom_call_target="tpu_custom_call" | custom-call | flops 20971520 | bytes 9437184 | tf_op jit(solution)/shard_map/pallas_call | solution.py:64
  28.9 0.0 copy-start
  28.9 0.5 all-to-all-done.1
  29.6 2.0 %multiply_reduce_fusion = f32[16,2,32,128]{3,2,1,0:T(8,128)S(1)} fusion(f32[4,16,2,32,128]{4,3,2,1,0:T(8,128)} %get-tuple-element.5, f32[4,16,2,128]{3,2,1,0:T(2,128)S(1)} %copy.14), kind=kLoop, calls=%fused_computation | loop fusion | flops 917504 | bytes 2686976 | tf_op jit(solution)/shard_map/reduce_sum | solution.py:112
  31.5 0.0 copy-done
  31.6 0.2 bitcast_add_fusion
  31.7 0.0 copy-start.1
  31.7 1.1 %pad_maximum_fusion = f32[16,2,2,32,128]{4,3,2,1,0:T(8,128)} fusion(f32[16,1,2,32,128]{4,3,2,1,0:T(8,128)S(1)} %get-tuple-element.7, f32[16,1,2,32,128]{4,3,2,1,0:T(8,128)S(1)} %get-tuple-element.6), kind=kLoop, calls=%fused_computation.3 | loop fusion | flops 262144 | bytes 2097152 | tf_op jit(solution)/shard_map/stack | solution.py:113
  32.8 9.4 %all-to-all-start.2 = ((f32[16,2,2,32,128]{4,3,2,1,0:T(8,128)}), f32[16,2,2,32,128]{4,3,2,1,0:T(8,128)S(1)}, u32[]{:S(2)}, u32[]{:S(2)}) async-start(f32[16,2,2,32,128]{4,3,2,1,0:T(8,128)} %pad_maximum_fusion), calls=%async_computation.2 | async-start | bytes 2097152 | tf_op jit(solution)/shard_map/all_to_all | solution.py:114
  42.2 0.0 copy-done.1
  42.2 26.2 %all-to-all-done.2 = f32[16,2,2,32,128]{4,3,2,1,0:T(8,128)S(1)} async-done(((f32[16,2,2,32,128]{4,3,2,1,0:T(8,128)}), f32[16,2,2,32,128]{4,3,2,1,0:T(8,128)S(1)}, u32[]{:S(2)}, u32[]{:S(2)}) %all-to-all-start.2) | async-done | bytes 1048608 | tf_op jit(solution)/shard_map/all_to_all | solution.py:114
  68.5 0.1 fusion.2
  68.6 15.6 %all_to_all.21 = f32[2,2,32,128]{3,2,1,0:T(8,128)S(1)} all-to-all(f32[2,2,32,128]{3,2,1,0:T(8,128)S(1)} %copy.15), channel_id=1, replica_groups=mesh['light'=16,'vz'=2,'vx'=16] {'vz'}, dimensions={0} | all-to-all | bytes 131072 | tf_op jit(solution)/shard_map/all_to_all | solution.py:117
  84.2 0.7 fusion.7
  84.9 0.6 slice_reduce_fusion.1
  (8 shorter events, 0.1 us)
Async XLA Ops:
  18.2 11.3 %all-to-all-start.1 = ((f32[16,4,256]{2,1,0:T(4,128)}), f32[16,4,256]{2,1,0:T(4,128)S(1)}, u32[]{:S(2)}, u32[]{:S(2)}) async-start(f32[16,4,256]{2,1,0:T(4,128)} %reduce-window_subtract_fusion), calls=%async_computation.1 | async-start | bytes 131072 | tf_op jit(solution)/shard_map/all_to_all | solution.py:18
  28.9 2.6 %copy-start = (f32[16,2,2,32,128]{4,3,2,1,0:T(8,128)S(1)}, f32[16,2,2,32,128]{4,3,2,1,0:T(8,128)}, u32[]{:S(2)}) copy-start(f32[16,2,2,32,128]{4,3,2,1,0:T(8,128)} %get-tuple-element.4) | copy-start | bytes 3145732
  31.7 10.5 %copy-start.1 = (s32[32]{0:T(128)S(1)}, s32[32]{0:T(128)}, u32[]{:S(2)}) copy-start(s32[32]{0:T(128)} %refs_0_.1) | copy-start | bytes 388
  32.8 35.6 %all-to-all-start.2 = ((f32[16,2,2,32,128]{4,3,2,1,0:T(8,128)}), f32[16,2,2,32,128]{4,3,2,1,0:T(8,128)S(1)}, u32[]{:S(2)}, u32[]{:S(2)}) async-start(f32[16,2,2,32,128]{4,3,2,1,0:T(8,128)} %pad_maximum_fusion), calls=%async_computation.2 | async-start | bytes 2097152 | tf_op jit(solution)/shard_map/all_to_all | solution.py:114
